TPU v7x, 128 devices: a whole 4x4x4 slice. The times are simulated.
128 devices in a mesh: flow: 8 (over y, core), link: 16 (over x, z).
Axes of the slice: x: 4, y: 4, z: 4, core: 2. Of those that a mesh axis runs over, the one named last changes fastest.
Arguments:
- route_tiles: bfloat16 [1024, 2048, 128], P('flow', 'link'), may hold values from 0 to 1, as said below
- tile_count: int32 [8, 16], P('flow', 'link'), may hold values from 16 to 128, as said below
- tile_flow: int32 [8, 2048], P('flow', 'link'), may hold values from 0 to 1023
- tile_link: int32 [8, 2048], P('flow', 'link'), may hold values from 0 to 511, as said below
- flow_class: int32 [1048576], P('flow'), may hold values from 0 to 255
- class_weight: float32 [256], replicated, may hold values from 0.25 to 4
- access_price: float32 [1048576], P('flow'), may hold values from 0.5 to 4
- capacity: float32 [1048576], P('link'), may hold values from 1 to 8
- init_price: float32 [1048576], P('link'), may hold values from 0.5 to 2
Outputs:
- flow_rate: float32 [1048576], P('flow')
- link_price: float32 [1048576], P('link')
Inputs may be any that keep to these rules, and one draw needn't show every extreme that they name: `route_tiles`: entries are 0 or 1. `tile_count`: counts follow 128 divided by 1, 2, 4 or 8; some device uses all 128 slots in every draw. `tile_link`: within one device's slots no link block repeats.
All inputs are finite; a program needn't handle non-finite values.
Results may differ from a plain program's by a relative error of at most 0.0014.
Values may be sent and summed in bfloat16 or wider, within the bound.
No kernel may reach another device: no remote copies, remote signals or barrier semaphores. Data moves between devices by JAX's collectives and lax.ppermute only.
A program may use at most 64 MiB of HBM per device.

v0:
```python
import jax
import jax.numpy as jnp
from jax import lax
from jax.experimental import pallas as pl
from jax.experimental.pallas import tpu as pltpu
from jax.sharding import PartitionSpec as P


step_size = 0.5


f32 = jnp.float32
bf16 = jnp.bfloat16

T = 128
S = 128
HALF = S // 2
PAYLOAD = HALF + 8
INDEX = HALF
EXPONENT = HALF + 1
GROUP = 16
CHUNKS = S // GROUP

SM = pl.BlockSpec(memory_space=pltpu.SMEM)
HB = pl.BlockSpec(memory_space=pltpu.HBM)
VM = pl.BlockSpec(memory_space=pltpu.VMEM)
PARAMS = pltpu.CompilerParams(vmem_limit_bytes=16 << 20)


def in_vmem(x):
    return pltpu.with_memory_space_constraint(x, pltpu.VMEM)


def in_hbm(x):
    return pltpu.with_memory_space_constraint(x, pltpu.HBM)


def dot(a, b):
    return lax.dot_general(a, b, (((1,), (0,)), ((), ())), preferred_element_type=f32)


def dot_t(a, b):
    return lax.dot_general(a, b, (((1,), (1,)), ((), ())), preferred_element_type=f32)


def used_index(index_row, count, unused=-1):
    slot = lax.broadcasted_iota(jnp.int32, index_row.shape, 1)
    return jnp.where(slot < count, index_row, unused)


def own_column(index_row, count):
    row = used_index(index_row, count, -2).astype(f32)
    return jnp.broadcast_to(row, (S, S)).T.astype(jnp.int32)


def put_payload(out, terms, index_row):
    largest = jnp.max(terms, axis=1, keepdims=True)
    exponent = jnp.floor(jnp.log(jnp.maximum(largest, 1e-30)) * 1.4426950408889634) + 1.0
    scale = jnp.exp2(16.0 - exponent)
    coded = jnp.minimum(jnp.round(terms * scale), 65535.0).astype(jnp.int32)
    out[:HALF, :] = coded[:HALF, :] | (coded[HALF:, :] << 16)
    out[INDEX:EXPONENT, :] = index_row
    exponent_row = jnp.broadcast_to(exponent, (S, S)).T[:1, :].astype(jnp.int32)
    out[EXPONENT : EXPONENT + 1, :] = exponent_row


def decoded(words):
    top = lax.shift_right_logical(words, 16)
    high = jnp.concatenate([words & 0xFF00, top & 0xFF00], axis=0)
    low = jnp.concatenate([words & 0xFF, top & 0xFF], axis=0)
    return jnp.concatenate([high.astype(f32).astype(bf16), low.astype(f32).astype(bf16)], axis=1)


def matched_sum(column, blocks, codes):
    hits = []
    for ref in blocks:
        for k in range(ref.shape[0]):
            scale = jnp.exp2((ref[k, EXPONENT : EXPONENT + 1, :] - 16).astype(f32))
            hits.append(jnp.where(column == ref[k, INDEX:EXPONENT, :], scale, 0.0).astype(bf16))
    both = dot(jnp.concatenate(hits, axis=1), codes)
    return both[:, :T] + both[:, T:]


def decode(blocks):
    return jnp.concatenate([decoded(ref[k, :HALF, :]) for ref in blocks for k in range(ref.shape[0])], axis=0)


def own_slots():
    lane_slot = lax.broadcasted_iota(jnp.int32, (GROUP, GROUP * T), 1) // T
    return lane_slot == lax.broadcasted_iota(jnp.int32, (GROUP, GROUP * T), 0)


def spread(rows, own):
    return jnp.where(own, jnp.concatenate([rows] * GROUP, axis=1).astype(f32), 0.0).astype(bf16)


def route_terms(tiles, ready, picked, out):
    own = own_slots()

    def body(g, carry):
        ready(g)
        rows = pl.ds(g * GROUP, GROUP)
        out[rows, :] = dot(spread(picked[rows, :], own), tiles[rows].reshape(GROUP * T, T))
        return carry

    lax.fori_loop(0, CHUNKS, body, 0)


def load_terms(tiles, sent, out):
    own = own_slots()

    def body(g, carry):
        rows = pl.ds(g * GROUP, GROUP)
        wide = jnp.concatenate([tiles[g * GROUP + i] for i in range(GROUP)], axis=1)
        out[rows, :] = dot_t(spread(sent[rows, :], own), wide)
        return carry

    lax.fori_loop(0, CHUNKS, body, 0)


def first_route_kernel(
    count, flow_in, link_in, price_in, tiles, out, kept, index, sems, more, flow_row, link_row, price, picked, terms
):
    small = [
        pltpu.make_async_copy(a, b, more.at[i])
        for i, (a, b) in enumerate(((flow_in, flow_row), (link_in, link_row), (price_in, price)))
    ]

    def copy(g):
        rows = pl.ds(g * GROUP, GROUP)
        return pltpu.make_async_copy(tiles.at[rows], kept.at[rows], sems.at[g])

    for c in small:
        c.start()
    for g in range(CHUNKS):
        copy(g).start()
    for c in small:
        c.wait()
    used = count[0, 0]
    flow_used = used_index(flow_row[...], used)
    index[:S, :] = own_column(flow_row[...], used)
    column = own_column(link_row[...], used)
    index[S : 2 * S, :] = column
    index[2 * S : 2 * S + 1, :] = flow_used
    index[2 * S + 1 : 2 * S + 2, :] = used_index(link_row[...], used)
    at = lax.broadcasted_iota(jnp.int32, (S, T), 1)
    hits = [jnp.where(column == at + c * T, 1.0, 0.0).astype(bf16) for c in range(price.shape[0] // T)]
    picked[...] = dot(jnp.concatenate(hits, axis=1), price[...].astype(bf16)).astype(bf16)
    route_terms(kept, lambda g: copy(g).wait(), picked, terms)
    put_payload(out, terms[...], flow_used)


def load_kernel(index, own, tiles, *rest):
    blocks, (out, sent, terms) = rest[:-3], rest[-3:]
    route_sum = matched_sum(index[:S, :], blocks, decode(blocks))
    sent[...] = (own[0] / (own[1] + route_sum)).astype(bf16)
    load_terms(tiles, sent, terms)
    put_payload(out, terms[...], index[2 * S + 1 : 2 * S + 2, :])


def route_kernel(index, own, tiles, *rest):
    blocks, (out, picked, terms) = rest[:-3], rest[-3:]
    load = matched_sum(index[S : 2 * S, :], blocks, decode(blocks))
    picked[...] = (own[2] * jnp.exp(step_size * (load / own[3] - 1.0))).astype(bf16)
    route_terms(tiles, lambda g: None, picked, terms)
    put_payload(out, terms[...], index[2 * S : 2 * S + 1, :])


def rate_kernel(weight, access, *rest):
    blocks, (out, code) = rest[:-2], rest[-2:]
    code[...] = decode(blocks)

    def body(c, carry):
        column = lax.broadcasted_iota(jnp.int32, (S, T), 0) + c * T
        total = matched_sum(column, blocks, code[...])
        rows = pl.ds(pl.multiple_of(c * T, T), T)
        out[rows, :] = weight[rows, :] / (access[rows, :] + total)
        return carry

    lax.fori_loop(0, out.shape[0] // T, body, 0)


def price_kernel(price, capacity, *rest):
    blocks, (out, code) = rest[:-2], rest[-2:]
    code[...] = decode(blocks)

    def body(c, carry):
        column = lax.broadcasted_iota(jnp.int32, (S, T), 0) + c * T
        total = matched_sum(column, blocks, code[...])
        rows = pl.ds(pl.multiple_of(c * T, T), T)
        out[rows, :] = price[rows, :] * jnp.exp(step_size * (total / capacity[rows, :] - 1.0))
        return carry

    lax.fori_loop(0, out.shape[0] // T, body, 0)


def prepare_kernel(flow_in, link_in, flow_class, table, access, price, capacity, weight, own, sems, flow_at, link_at):
    small = [pltpu.make_async_copy(flow_in, flow_at, sems.at[0]), pltpu.make_async_copy(link_in, link_at, sems.at[1])]
    for c in small:
        c.start()
    low = jnp.broadcast_to(table[0:1, :], (8, T))
    high = jnp.broadcast_to(table[1:2, :], (8, T))

    def look(r, carry):
        rows = pl.ds(pl.multiple_of(r * 8, 8), 8)
        which = flow_class[rows, :]
        lane = which & (T - 1)
        from_low = jnp.take_along_axis(low, lane, axis=1)
        from_high = jnp.take_along_axis(high, lane, axis=1)
        weight[rows, :] = jnp.where(which < T, from_low, from_high)
        return carry

    lax.fori_loop(0, flow_class.shape[0] // 8, look, 0, unroll=8)

    for c in small:
        c.wait()

    def pick(s, carry):
        f = flow_at[0, s]
        l = link_at[0, s]
        own[0, pl.ds(s, 1), :] = weight[pl.ds(f, 1), :]
        own[1, pl.ds(s, 1), :] = access[pl.ds(f, 1), :]
        own[2, pl.ds(s, 1), :] = price[pl.ds(l, 1), :]
        own[3, pl.ds(s, 1), :] = capacity[pl.ds(l, 1), :]
        return carry

    lax.fori_loop(0, S, pick, 0, unroll=8)


def shifts():
    def device(y, core, x, z):
        return ((y % 4) * 2 + core) * 16 + (x % 4) * 4 + z % 4

    every = [(y, c, x, z) for y in range(4) for c in range(2) for x in range(4) for z in range(4)]

    def moved(f):
        return [(device(*p), device(*f(*p))) for p in every]

    order = (1, 3, 2)
    first = [moved(lambda y, c, x, z, d=d: (y, c, x + d, z) if c == 0 else (y, c, x, z + d)) for d in order]
    second = [moved(lambda y, c, x, z, d=d: (y, c, x, z + d) if c == 0 else (y, c, x + d, z)) for d in order]
    along_y = [moved(lambda y, c, x, z, d=d: (y + d, c, x, z)) for d in order]
    partner = moved(lambda y, c, x, z: (y, 1 - c, x, z))
    return first, second, along_y, partner


FIRST, SECOND, ALONG_Y, PARTNER = shifts()


def send(x, perm):
    return lax.ppermute(x, ("flow", "link"), perm)


def gather_link(x):
    near = jnp.stack([x] + [send(x, p) for p in FIRST])
    far = []
    for p in SECOND:
        far.append(send(near, p))
    return [near] + far


def gather_flow(x):
    near = [x]
    for p in ALONG_Y:
        near.append(send(x, p))
    near = jnp.stack(near)
    return [near, send(near, PARTNER)]


def on_device(
    route_tiles,
    tile_count,
    tile_flow,
    tile_link,
    flow_class,
    class_weight,
    access_price,
    capacity,
    init_price,
):
    flow_blocks = access_price.shape[0] // T
    link_blocks = capacity.shape[0] // T
    cap = capacity.reshape(link_blocks, T)
    price = init_price.reshape(link_blocks, T)
    access = access_price.reshape(flow_blocks, T)
    payload = pltpu.VMEM((PAYLOAD, T), jnp.int32)

    def tile_call(body, own, tiles, blocks):
        return pl.pallas_call(
            body,
            out_shape=payload,
            in_specs=[VM] * (3 + len(blocks)),
            out_specs=VM,
            scratch_shapes=[pltpu.VMEM((S, T), bf16), pltpu.VMEM((S, T), f32)],
            compiler_params=PARAMS,
        )(in_vmem(index), in_vmem(own), in_vmem(tiles), *[in_vmem(x) for x in blocks])

    def full_call(body, a, b, blocks):
        pieces = sum(x.shape[0] for x in blocks)
        return pl.pallas_call(
            body,
            out_shape=jax.ShapeDtypeStruct(a.shape, f32),
            in_specs=[VM] * (2 + len(blocks)),
            out_specs=VM,
            scratch_shapes=[pltpu.VMEM((pieces * S, 2 * T), bf16)],
            compiler_params=PARAMS,
        )(a, b, *[in_vmem(x) for x in blocks])

    route_one, tiles, index = pl.pallas_call(
        first_route_kernel,
        out_shape=(payload, pltpu.VMEM((S, T, T), bf16), pltpu.VMEM((2 * S + 8, T), jnp.int32)),
        in_specs=[SM] + [HB] * 4,
        out_specs=(VM, VM, VM),
        scratch_shapes=[
            pltpu.SemaphoreType.DMA((CHUNKS,)),
            pltpu.SemaphoreType.DMA((3,)),
            pltpu.VMEM((1, S), jnp.int32),
            pltpu.VMEM((1, S), jnp.int32),
            pltpu.VMEM(price.shape, f32),
            pltpu.VMEM((S, T), bf16),
            pltpu.VMEM((S, T), f32),
        ],
        compiler_params=PARAMS,
        name="first_route",
    )(tile_count, *[in_hbm(x) for x in (tile_flow, tile_link, price, route_tiles)])
    weight, own = pl.pallas_call(
        prepare_kernel,
        out_shape=(pltpu.VMEM((flow_blocks, T), f32), pltpu.VMEM((4, S, T), f32)),
        in_specs=[HB, HB] + [VM] * 5,
        out_specs=(VM, VM),
        scratch_shapes=[pltpu.SemaphoreType.DMA((2,)), pltpu.SMEM((1, S), jnp.int32), pltpu.SMEM((1, S), jnp.int32)],
        compiler_params=PARAMS,
        name="prepare",
    )(in_hbm(tile_flow), in_hbm(tile_link), flow_class.reshape(flow_blocks, T), class_weight.reshape(2, T), access, price, cap)

    routes = gather_link(route_one)
    loads = gather_flow(tile_call(load_kernel, own, tiles, routes))
    price_one = full_call(price_kernel, price, cap, loads)
    routes = gather_link(tile_call(route_kernel, own, tiles, loads))
    rate = full_call(rate_kernel, weight, access, routes)
    loads = gather_flow(tile_call(load_kernel, own, tiles, routes))
    price_two = full_call(price_kernel, price_one, cap, loads)
    return (rate.reshape(-1), price_two.reshape(-1))


def solution(mesh):
    return jax.shard_map(
        on_device,
        mesh=mesh,
        in_specs=(
            P("flow", "link", None),
            P("flow", "link"),
            P("flow", "link"),
            P("flow", "link"),
            P("flow"),
            P(),
            P("flow"),
            P("link"),
            P("link"),
        ),
        out_specs=(P("flow"), P("link")),
        check_vma=False,
    )
```

profile of v0, /device:TPU:0, one launch (start us, length us, event | category | flops | bytes accessed | tf_op | source)
XLA Modules:
  0.0 75.3 jit_solution(13368665430589207193)
XLA Ops:
  1.4 4.1 %first_route.1 = (s32[72,128]{1,0:T(8,128)S(1)}, bf16[128,128,128]{2,1,0:T(8,128)(2,1)S(1)}, s32[264,128]{1,0:T(8,128)S(1)}) custom-call(s32[1,1]{1,0:T(1,128)S(6)} %copy.11.count, s32[1,128]{1,0:T(1,128)} %flow_in.3, s32[1,128]{1,0:T(1,128)} %link_in.3, f32[512,128]{1,0:T(8,128)} %bitcast.26, bf16[128,128,128]{2,1,0:T(8,128)(2,1)} %tiles.1), custom_call_target="tpu_custom_call" | custom-call | tf_op jit(solution)/shard_map/first_route/pallas_call | solution.py:309
  5.5 3.2 %collective-permute-start.2 = (s32[72,128]{1,0:T(8,128)S(1)}, s32[72,128]{1,0:T(8,128)S(1)}, u32[]{:S(2)}, u32[]{:S(2)}) collective-permute-start(s32[72,128]{1,0:T(8,128)S(1)} %get-tuple-element.11), channel_id=1, source_target_pairs={{0,8},{1,9},{2,10},{3,11},{4,12},{5,13},{6,14},{7,15},{8,0},{9,1},... | collective-permute-start | bytes 110600 | tf_op jit(solution)/shard_map/ppermute | solution.py:251
  11.1 1.6 %collective-permute-done.1 = s32[72,128]{1,0:T(8,128)S(1)} collective-permute-done((s32[72,128]{1,0:T(8,128)S(1)}, s32[72,128]{1,0:T(8,128)S(1)}, u32[]{:S(2)}, u32[]{:S(2)}) %collective-permute-start.1) | collective-permute-done | bytes 36896 | tf_op jit(solution)/shard_map/ppermute | solution.py:251
  12.7 2.4 %collective-permute-done = s32[72,128]{1,0:T(8,128)S(1)} collective-permute-done((s32[72,128]{1,0:T(8,128)S(1)}, s32[72,128]{1,0:T(8,128)S(1)}, u32[]{:S(2)}, u32[]{:S(2)}) %collective-permute-start) | collective-permute-done | bytes 36896 | tf_op jit(solution)/shard_map/ppermute | solution.py:251
  15.1 4.0 %collective-permute-start.5 = (s32[4,72,128]{2,1,0:T(8,128)S(1)}, s32[4,72,128]{2,1,0:T(8,128)S(1)}, u32[]{:S(2)}, u32[]{:S(2)}) collective-permute-start(s32[4,72,128]{2,1,0:T(8,128)S(1)} %pad_add_fusion.rest_0_), channel_id=1, source_target_pairs={{0,2},{1,3},{2,0},{3,1},{4,6},{5,7},{6,4},{7,5},{8,10},{9,11},{10,... | collective-permute-start | bytes 442376 | tf_op jit(solution)/shard_map/ppermute | solution.py:251
  19.0 1.6 %collective-permute-start.4 = (s32[4,72,128]{2,1,0:T(8,128)S(1)}, s32[4,72,128]{2,1,0:T(8,128)S(1)}, u32[]{:S(2)}, u32[]{:S(2)}) collective-permute-start(s32[4,72,128]{2,1,0:T(8,128)S(1)} %pad_add_fusion.rest_0_), channel_id=1, source_target_pairs={{0,3},{1,0},{2,1},{3,2},{4,7},{5,4},{6,5},{7,6},{8,11},{9,8},{10,9... | collective-permute-start | bytes 442376 | tf_op jit(solution)/shard_map/ppermute | solution.py:251
  21.4 2.1 %prepare.1 = (f32[1024,128]{1,0:T(8,128)S(1)}, f32[4,128,128]{2,1,0:T(8,128)S(1)}) custom-call(s32[1,128]{1,0:T(1,128)} %flow_in.3, s32[1,128]{1,0:T(1,128)} %link_in.3, s32[1024,128]{1,0:T(8,128)S(1)} %bitcast.31, f32[2,128]{1,0:T(2,128)S(1)} %bitcast.36, f32[1024,128]{1,0:T(8,128)S(1)} %bitcast.29, f32[512,128]{1,0:T(8,128)S(1)} %bitcast.27, ...), custom_call_target="tpu_custom_call" | custom-call | tf_op jit(solution)/shard_map/prepare/pallas_call | solution.py:326
  23.5 2.6 %collective-permute-done.4.rest_2_ = s32[4,72,128]{2,1,0:T(8,128)S(1)} collective-permute-done((s32[4,72,128]{2,1,0:T(8,128)S(1)}, s32[4,72,128]{2,1,0:T(8,128)S(1)}, u32[]{:S(2)}, u32[]{:S(2)}) %collective-permute-start.4) | collective-permute-done | bytes 147488 | tf_op jit(solution)/shard_map/ppermute | solution.py:251
  27.0 2.6 %shard_map.104 = s32[72,128]{1,0:T(8,128)S(1)} custom-call(s32[264,128]{1,0:T(8,128)S(1)} %get-tuple-element.8.index, f32[4,128,128]{2,1,0:T(8,128)S(1)} %get-tuple-element.9.own, bf16[128,128,128]{2,1,0:T(8,128)(2,1)S(1)} %get-tuple-element.10.tiles, s32[4,72,128]{2,1,0:T(8,128)S(1)} %pad_add_fusion.rest_0_, ...), custom_call_target="tpu_custom_call" | custom-call | tf_op jit(solution)/shard_map/pallas_call | solution.py:289
  29.6 3.2 %collective-permute-start.8 = (s32[72,128]{1,0:T(8,128)S(1)}, s32[72,128]{1,0:T(8,128)S(1)}, u32[]{:S(2)}, u32[]{:S(2)}) collective-permute-start(s32[72,128]{1,0:T(8,128)S(1)} %shard_map.104), channel_id=1, source_target_pairs={{0,64},{1,65},{2,66},{3,67},{4,68},{5,69},{6,70},{7,71},{8,72},{9,... | collective-permute-start | bytes 110600 | tf_op jit(solution)/shard_map/ppermute | solution.py:251
  35.1 1.7 %collective-permute-done.7 = s32[72,128]{1,0:T(8,128)S(1)} collective-permute-done((s32[72,128]{1,0:T(8,128)S(1)}, s32[72,128]{1,0:T(8,128)S(1)}, u32[]{:S(2)}, u32[]{:S(2)}) %collective-permute-start.7) | collective-permute-done | bytes 36896 | tf_op jit(solution)/shard_map/ppermute | solution.py:251
  36.8 2.3 %collective-permute-done.6 = s32[72,128]{1,0:T(8,128)S(1)} collective-permute-done((s32[72,128]{1,0:T(8,128)S(1)}, s32[72,128]{1,0:T(8,128)S(1)}, u32[]{:S(2)}, u32[]{:S(2)}) %collective-permute-start.6) | collective-permute-done | bytes 36896 | tf_op jit(solution)/shard_map/ppermute | solution.py:251
  40.6 2.0 %shard_map.105 = s32[72,128]{1,0:T(8,128)S(1)} custom-call(s32[264,128]{1,0:T(8,128)S(1)} %get-tuple-element.8.index, f32[4,128,128]{2,1,0:T(8,128)S(1)} %get-tuple-element.9.own, bf16[128,128,128]{2,1,0:T(8,128)(2,1)S(1)} %get-tuple-element.10.tiles, s32[4,72,128]{2,1,0:T(8,128)S(1)} %pad_add_fusion.1.rest_0_, s32[4,72,128]{2,1,0:T(8,128)S(1)} %collective-permute-done.9.rest_1_), custom_call_target="tpu_custom_call" | custom-call | tf_op jit(solution)/shard_map/pallas_call | solution.py:289
  42.6 1.4 %collective-permute-start.11 = (s32[72,128]{1,0:T(8,128)S(1)}, s32[72,128]{1,0:T(8,128)S(1)}, u32[]{:S(2)}, u32[]{:S(2)}) collective-permute-start(s32[72,128]{1,0:T(8,128)S(1)} %shard_map.105), channel_id=1, source_target_pairs={{0,12},{1,13},{2,14},{3,15},{4,0},{5,1},{6,2},{7,3},{8,4},{9,5},{1... | collective-permute-start | bytes 110600 | tf_op jit(solution)/shard_map/ppermute | solution.py:251
  44.7 3.4 %collective-permute-done.12 = s32[72,128]{1,0:T(8,128)S(1)} collective-permute-done((s32[72,128]{1,0:T(8,128)S(1)}, s32[72,128]{1,0:T(8,128)S(1)}, u32[]{:S(2)}, u32[]{:S(2)}) %collective-permute-start.12) | collective-permute-done | bytes 36896 | tf_op jit(solution)/shard_map/ppermute | solution.py:251
  50.5 1.6 %collective-permute-start.14 = (s32[4,72,128]{2,1,0:T(8,128)S(1)}, s32[4,72,128]{2,1,0:T(8,128)S(1)}, u32[]{:S(2)}, u32[]{:S(2)}) collective-permute-start(s32[4,72,128]{2,1,0:T(8,128)S(1)} %pad_add_fusion.2.rest_0_), channel_id=1, source_target_pairs={{0,3},{1,0},{2,1},{3,2},{4,7},{5,4},{6,5},{7,6},{8,11},{9,8},{10,9... | collective-permute-start | bytes 442376 | tf_op jit(solution)/shard_map/ppermute | solution.py:251
  52.5 3.5 %collective-permute-done.15.rest_3_ = s32[4,72,128]{2,1,0:T(8,128)S(1)} collective-permute-done((s32[4,72,128]{2,1,0:T(8,128)S(1)}, s32[4,72,128]{2,1,0:T(8,128)S(1)}, u32[]{:S(2)}, u32[]{:S(2)}) %collective-permute-start.15) | collective-permute-done | bytes 147488 | tf_op jit(solution)/shard_map/ppermute | solution.py:251
  56.2 2.2 %collective-permute-done.13.rest_1_ = s32[4,72,128]{2,1,0:T(8,128)S(1)} collective-permute-done((s32[4,72,128]{2,1,0:T(8,128)S(1)}, s32[4,72,128]{2,1,0:T(8,128)S(1)}, u32[]{:S(2)}, u32[]{:S(2)}) %collective-permute-start.13) | collective-permute-done | bytes 147488 | tf_op jit(solution)/shard_map/ppermute | solution.py:251
  58.4 2.6 %shard_map.108 = s32[72,128]{1,0:T(8,128)S(1)} custom-call(s32[264,128]{1,0:T(8,128)S(1)} %get-tuple-element.8.index, f32[4,128,128]{2,1,0:T(8,128)S(1)} %get-tuple-element.9.own, bf16[128,128,128]{2,1,0:T(8,128)(2,1)S(1)} %get-tuple-element.10.tiles, s32[4,72,128]{2,1,0:T(8,128)S(1)} %pad_add_fusion.2.rest_0_, ...), custom_call_target="tpu_custom_call" | custom-call | tf_op jit(solution)/shard_map/pallas_call | solution.py:289
  61.6 2.0 %collective-permute-start.17 = (s32[72,128]{1,0:T(8,128)S(1)}, s32[72,128]{1,0:T(8,128)S(1)}, u32[]{:S(2)}, u32[]{:S(2)}) collective-permute-start(s32[72,128]{1,0:T(8,128)S(1)} %shard_map.108), channel_id=1, source_target_pairs={{0,96},{1,97},{2,98},{3,99},{4,100},{5,101},{6,102},{7,103},{8,104... | collective-permute-start | bytes 110600 | tf_op jit(solution)/shard_map/ppermute | solution.py:251
  63.6 3.0 %collective-permute-done.18 = s32[72,128]{1,0:T(8,128)S(1)} collective-permute-done((s32[72,128]{1,0:T(8,128)S(1)}, s32[72,128]{1,0:T(8,128)S(1)}, u32[]{:S(2)}, u32[]{:S(2)}) %collective-permute-start.18) | collective-permute-done | bytes 36896 | tf_op jit(solution)/shard_map/ppermute | solution.py:251
  66.6 2.1 %collective-permute-done.16 = s32[72,128]{1,0:T(8,128)S(1)} collective-permute-done((s32[72,128]{1,0:T(8,128)S(1)}, s32[72,128]{1,0:T(8,128)S(1)}, u32[]{:S(2)}, u32[]{:S(2)}) %collective-permute-start.16) | collective-permute-done | bytes 36896 | tf_op jit(solution)/shard_map/ppermute | solution.py:251
  69.9 3.6 %shard_map.106 = f32[1024,128]{1,0:T(8,128)} custom-call(f32[1024,128]{1,0:T(8,128)S(1)} %get-tuple-element.7.weight, f32[1024,128]{1,0:T(8,128)S(1)} %bitcast.30, s32[4,72,128]{2,1,0:T(8,128)S(1)} %pad_add_fusion.2.rest_0_, s32[4,72,128]{2,1,0:T(8,128)S(1)} %collective-permute-done.13.rest_1_, s32[4,72,128]{2,1,0:T(8,128)S(1)} %collective-permute-done.14.rest_2_, ...), custom_call_target="tpu_custom_call" | custom-call | tf_op jit(solution)/shard_map/pallas_call | solution.py:300
  73.5 1.8 %shard_map.109 = f32[512,128]{1,0:T(8,128)} custom-call(f32[512,128]{1,0:T(8,128)S(1)} %shard_map.107.price, f32[512,128]{1,0:T(8,128)S(1)} %bitcast.25, s32[4,72,128]{2,1,0:T(8,128)S(1)} %pad_add_fusion.3.rest_0_, s32[4,72,128]{2,1,0:T(8,128)S(1)} %collective-permute-done.19.rest_1_), custom_call_target="tpu_custom_call" | custom-call | tf_op jit(solution)/shard_map/pallas_call | solution.py:300
  (38 shorter events, 13.3 us)
Async XLA Ops:
  0.6 20.8 %copy-start.1 = (f32[65536]{0:T(1024)S(1)}, f32[65536]{0:T(1024)}, u32[]{:S(2)}) copy-start(f32[65536]{0:T(1024)} %param.17) | copy-start | bytes 786436
  0.6 20.8 %copy-start = (f32[65536]{0:T(1024)S(1)}, f32[65536]{0:T(1024)}, u32[]{:S(2)}) copy-start(f32[65536]{0:T(1024)} %param.16) | copy-start | bytes 786436
  0.7 20.8 %copy-start.2 = (f32[131072]{0:T(1024)S(1)}, f32[131072]{0:T(1024)}, u32[]{:S(2)}) copy-start(f32[131072]{0:T(1024)} %param.15) | copy-start | bytes 1572868
  0.7 20.8 %copy-start.4 = (f32[256]{0:T(256)S(1)}, f32[256]{0:T(256)}, u32[]{:S(2)}) copy-start(f32[256]{0:T(256)} %param.14) | copy-start | bytes 3076
  5.5 5.5 %collective-permute-start.2 = (s32[72,128]{1,0:T(8,128)S(1)}, s32[72,128]{1,0:T(8,128)S(1)}, u32[]{:S(2)}, u32[]{:S(2)}) collective-permute-start(s32[72,128]{1,0:T(8,128)S(1)} %get-tuple-element.11), channel_id=1, source_target_pairs={{0,8},{1,9},{2,10},{3,11},{4,12},{5,13},{6,14},{7,15},{8,0},{9,1},... | collective-permute-start | bytes 110600 | tf_op jit(solution)/shard_map/ppermute | solution.py:251
  8.7 4.0 %collective-permute-start.1 = (s32[72,128]{1,0:T(8,128)S(1)}, s32[72,128]{1,0:T(8,128)S(1)}, u32[]{:S(2)}, u32[]{:S(2)}) collective-permute-start(s32[72,128]{1,0:T(8,128)S(1)} %get-tuple-element.11), channel_id=1, source_target_pairs={{0,12},{1,13},{2,14},{3,15},{4,0},{5,1},{6,2},{7,3},{8,4},{9,5},{1... | collective-permute-start | bytes 110600 | tf_op jit(solution)/shard_map/ppermute | solution.py:251
  9.9 5.2 %collective-permute-start = (s32[72,128]{1,0:T(8,128)S(1)}, s32[72,128]{1,0:T(8,128)S(1)}, u32[]{:S(2)}, u32[]{:S(2)}) collective-permute-start(s32[72,128]{1,0:T(8,128)S(1)} %get-tuple-element.11), channel_id=1, source_target_pairs={{0,4},{1,5},{2,6},{3,7},{4,8},{5,9},{6,10},{7,11},{8,12},{9,13},{1... | collective-permute-start | bytes 110600 | tf_op jit(solution)/shard_map/ppermute | solution.py:251
  15.1 8.4 %collective-permute-start.5 = (s32[4,72,128]{2,1,0:T(8,128)S(1)}, s32[4,72,128]{2,1,0:T(8,128)S(1)}, u32[]{:S(2)}, u32[]{:S(2)}) collective-permute-start(s32[4,72,128]{2,1,0:T(8,128)S(1)} %pad_add_fusion.rest_0_), channel_id=1, source_target_pairs={{0,2},{1,3},{2,0},{3,1},{4,6},{5,7},{6,4},{7,5},{8,10},{9,11},{10,... | collective-permute-start | bytes 442376 | tf_op jit(solution)/shard_map/ppermute | solution.py:251
  19.0 7.1 %collective-permute-start.4 = (s32[4,72,128]{2,1,0:T(8,128)S(1)}, s32[4,72,128]{2,1,0:T(8,128)S(1)}, u32[]{:S(2)}, u32[]{:S(2)}) collective-permute-start(s32[4,72,128]{2,1,0:T(8,128)S(1)} %pad_add_fusion.rest_0_), channel_id=1, source_target_pairs={{0,3},{1,0},{2,1},{3,2},{4,7},{5,4},{6,5},{7,6},{8,11},{9,8},{10,9... | collective-permute-start | bytes 442376 | tf_op jit(solution)/shard_map/ppermute | solution.py:251
  20.6 6.4 %collective-permute-start.3 = (s32[4,72,128]{2,1,0:T(8,128)S(1)}, s32[4,72,128]{2,1,0:T(8,128)S(1)}, u32[]{:S(2)}, u32[]{:S(2)}) collective-permute-start(s32[4,72,128]{2,1,0:T(8,128)S(1)} %pad_add_fusion.rest_0_), channel_id=1, source_target_pairs={{0,1},{1,2},{2,3},{3,0},{4,5},{5,6},{6,7},{7,4},{8,9},{9,10},{10,1... | collective-permute-start | bytes 442376 | tf_op jit(solution)/shard_map/ppermute | solution.py:251
  29.6 5.5 %collective-permute-start.8 = (s32[72,128]{1,0:T(8,128)S(1)}, s32[72,128]{1,0:T(8,128)S(1)}, u32[]{:S(2)}, u32[]{:S(2)}) collective-permute-start(s32[72,128]{1,0:T(8,128)S(1)} %shard_map.104), channel_id=1, source_target_pairs={{0,64},{1,65},{2,66},{3,67},{4,68},{5,69},{6,70},{7,71},{8,72},{9,... | collective-permute-start | bytes 110600 | tf_op jit(solution)/shard_map/ppermute | solution.py:251
  32.9 4.0 %collective-permute-start.7 = (s32[72,128]{1,0:T(8,128)S(1)}, s32[72,128]{1,0:T(8,128)S(1)}, u32[]{:S(2)}, u32[]{:S(2)}) collective-permute-start(s32[72,128]{1,0:T(8,128)S(1)} %shard_map.104), channel_id=1, source_target_pairs={{0,96},{1,97},{2,98},{3,99},{4,100},{5,101},{6,102},{7,103},{8,104... | collective-permute-start | bytes 110600 | tf_op jit(solution)/shard_map/ppermute | solution.py:251
  33.9 5.2 %collective-permute-start.6 = (s32[72,128]{1,0:T(8,128)S(1)}, s32[72,128]{1,0:T(8,128)S(1)}, u32[]{:S(2)}, u32[]{:S(2)}) collective-permute-start(s32[72,128]{1,0:T(8,128)S(1)} %shard_map.104), channel_id=1, source_target_pairs={{0,32},{1,33},{2,34},{3,35},{4,36},{5,37},{6,38},{7,39},{8,40},{9,... | collective-permute-start | bytes 110600 | tf_op jit(solution)/shard_map/ppermute | solution.py:251
  39.1 1.5 %collective-permute-start.9 = (s32[4,72,128]{2,1,0:T(8,128)S(1)}, s32[4,72,128]{2,1,0:T(8,128)S(1)}, u32[]{:S(2)}, u32[]{:S(2)}) collective-permute-start(s32[4,72,128]{2,1,0:T(8,128)S(1)} %pad_add_fusion.1.rest_0_), channel_id=1, source_target_pairs={{0,16},{1,17},{2,18},{3,19},{4,20},{5,21},{6,22},{7,23},{8,24},{9,... | collective-permute-start | bytes 442376 | tf_op jit(solution)/shard_map/ppermute | solution.py:251
  42.5 5.5 %collective-permute-start.12 = (s32[72,128]{1,0:T(8,128)S(1)}, s32[72,128]{1,0:T(8,128)S(1)}, u32[]{:S(2)}, u32[]{:S(2)}) collective-permute-start(s32[72,128]{1,0:T(8,128)S(1)} %shard_map.105), channel_id=1, source_target_pairs={{0,8},{1,9},{2,10},{3,11},{4,12},{5,13},{6,14},{7,15},{8,0},{9,1},... | collective-permute-start | bytes 110600 | tf_op jit(solution)/shard_map/ppermute | solution.py:251
  42.6 5.5 %collective-permute-start.11 = (s32[72,128]{1,0:T(8,128)S(1)}, s32[72,128]{1,0:T(8,128)S(1)}, u32[]{:S(2)}, u32[]{:S(2)}) collective-permute-start(s32[72,128]{1,0:T(8,128)S(1)} %shard_map.105), channel_id=1, source_target_pairs={{0,12},{1,13},{2,14},{3,15},{4,0},{5,1},{6,2},{7,3},{8,4},{9,5},{1... | collective-permute-start | bytes 110600 | tf_op jit(solution)/shard_map/ppermute | solution.py:251
  44.0 5.2 %collective-permute-start.10 = (s32[72,128]{1,0:T(8,128)S(1)}, s32[72,128]{1,0:T(8,128)S(1)}, u32[]{:S(2)}, u32[]{:S(2)}) collective-permute-start(s32[72,128]{1,0:T(8,128)S(1)} %shard_map.105), channel_id=1, source_target_pairs={{0,4},{1,5},{2,6},{3,7},{4,8},{5,9},{6,10},{7,11},{8,12},{9,13},{1... | collective-permute-start | bytes 110600 | tf_op jit(solution)/shard_map/ppermute | solution.py:251
  49.2 6.7 %collective-permute-start.15 = (s32[4,72,128]{2,1,0:T(8,128)S(1)}, s32[4,72,128]{2,1,0:T(8,128)S(1)}, u32[]{:S(2)}, u32[]{:S(2)}) collective-permute-start(s32[4,72,128]{2,1,0:T(8,128)S(1)} %pad_add_fusion.2.rest_0_), channel_id=1, source_target_pairs={{0,2},{1,3},{2,0},{3,1},{4,6},{5,7},{6,4},{7,5},{8,10},{9,11},{10,... | collective-permute-start | bytes 442376 | tf_op jit(solution)/shard_map/ppermute | solution.py:251
  50.5 5.7 %collective-permute-start.14 = (s32[4,72,128]{2,1,0:T(8,128)S(1)}, s32[4,72,128]{2,1,0:T(8,128)S(1)}, u32[]{:S(2)}, u32[]{:S(2)}) collective-permute-start(s32[4,72,128]{2,1,0:T(8,128)S(1)} %pad_add_fusion.2.rest_0_), channel_id=1, source_target_pairs={{0,3},{1,0},{2,1},{3,2},{4,7},{5,4},{6,5},{7,6},{8,11},{9,8},{10,9... | collective-permute-start | bytes 442376 | tf_op jit(solution)/shard_map/ppermute | solution.py:251
  52.1 6.4 %collective-permute-start.13 = (s32[4,72,128]{2,1,0:T(8,128)S(1)}, s32[4,72,128]{2,1,0:T(8,128)S(1)}, u32[]{:S(2)}, u32[]{:S(2)}) collective-permute-start(s32[4,72,128]{2,1,0:T(8,128)S(1)} %pad_add_fusion.2.rest_0_), channel_id=1, source_target_pairs={{0,1},{1,2},{2,3},{3,0},{4,5},{5,6},{6,7},{7,4},{8,9},{9,10},{10,1... | collective-permute-start | bytes 442376 | tf_op jit(solution)/shard_map/ppermute | solution.py:251
  61.1 5.5 %collective-permute-start.18 = (s32[72,128]{1,0:T(8,128)S(1)}, s32[72,128]{1,0:T(8,128)S(1)}, u32[]{:S(2)}, u32[]{:S(2)}) collective-permute-start(s32[72,128]{1,0:T(8,128)S(1)} %shard_map.108), channel_id=1, source_target_pairs={{0,64},{1,65},{2,66},{3,67},{4,68},{5,69},{6,70},{7,71},{8,72},{9,... | collective-permute-start | bytes 110600 | tf_op jit(solution)/shard_map/ppermute | solution.py:251
  61.6 5.0 %collective-permute-start.17 = (s32[72,128]{1,0:T(8,128)S(1)}, s32[72,128]{1,0:T(8,128)S(1)}, u32[]{:S(2)}, u32[]{:S(2)}) collective-permute-start(s32[72,128]{1,0:T(8,128)S(1)} %shard_map.108), channel_id=1, source_target_pairs={{0,96},{1,97},{2,98},{3,99},{4,100},{5,101},{6,102},{7,103},{8,104... | collective-permute-start | bytes 110600 | tf_op jit(solution)/shard_map/ppermute | solution.py:251
  63.5 5.2 %collective-permute-start.16 = (s32[72,128]{1,0:T(8,128)S(1)}, s32[72,128]{1,0:T(8,128)S(1)}, u32[]{:S(2)}, u32[]{:S(2)}) collective-permute-start(s32[72,128]{1,0:T(8,128)S(1)} %shard_map.108), channel_id=1, source_target_pairs={{0,32},{1,33},{2,34},{3,35},{4,36},{5,37},{6,38},{7,39},{8,40},{9,... | collective-permute-start | bytes 110600 | tf_op jit(solution)/shard_map/ppermute | solution.py:251
  68.7 4.8 %collective-permute-start.19 = (s32[4,72,128]{2,1,0:T(8,128)S(1)}, s32[4,72,128]{2,1,0:T(8,128)S(1)}, u32[]{:S(2)}, u32[]{:S(2)}) collective-permute-start(s32[4,72,128]{2,1,0:T(8,128)S(1)} %pad_add_fusion.3.rest_0_), channel_id=1, source_target_pairs={{0,16},{1,17},{2,18},{3,19},{4,20},{5,21},{6,22},{7,23},{8,24},{9,... | collective-permute-start | bytes 442376 | tf_op jit(solution)/shard_map/ppermute | solution.py:251
  (1 other events, 20.8 us)
where the time goes:
time: 76.8 us; the launch traced here: 75.3 us
  waiting for transfers between devices  28.9 us (38%)
  starting transfers between devices  25 us (33%)
  Pallas kernels  19.8 us (26%)
  between operations  1.53 us (2%)
    ppermute x20, waiting for transfers between devices, send(): return lax.ppermute(x, ('flow', 'link'), perm)  28.9 us
    ppermute x20, starting transfers between devices, send(): return lax.ppermute(x, ('flow', 'link'), perm)  25 us
    pallas_call x3, Pallas kernels, tile_call(): pl.pallas_call(body, out_shape=payload, in_specs=[VM] * (3 + len(blocks))...  7.23 us
    pallas_call x3, Pallas kernels, full_call(): pl.pallas_call(body, out_shape=jax.ShapeDtypeStruct(a.shape, f32), in_spe...  6.46 us
    pallas_call x1, Pallas kernels, on_device(): pl.pallas_call(first_route_kernel, out_shape=(payload, pltpu.VMEM((S, T,...  4.09 us
    pallas_call x1, Pallas kernels, on_device(): pl.pallas_call(prepare_kernel, out_shape=(pltpu.VMEM((flow_blocks, T), f3...  2.06 us
  transfers between devices with their start and end apart: 20, of which 16 were waited for; matrix products, arithmetic and copies ran while one was open for 0% of the time, Pallas kernels for 9%

commit v1 on v0

--- a/solution.py
+++ b/solution.py
@@ -20,6 +20,7 @@
 EXPONENT = HALF + 1
 GROUP = 16
 CHUNKS = S // GROUP
+FETCH = 32
 
 SM = pl.BlockSpec(memory_space=pltpu.SMEM)
 HB = pl.BlockSpec(memory_space=pltpu.HBM)
@@ -37,10 +38,6 @@
 
 def dot(a, b):
     return lax.dot_general(a, b, (((1,), (0,)), ((), ())), preferred_element_type=f32)
-
-
-def dot_t(a, b):
-    return lax.dot_general(a, b, (((1,), (1,)), ((), ())), preferred_element_type=f32)
 
 
 def used_index(index_row, count, unused=-1):
@@ -94,28 +91,17 @@
     return jnp.where(own, jnp.concatenate([rows] * GROUP, axis=1).astype(f32), 0.0).astype(bf16)
 
 
-def route_terms(tiles, ready, picked, out):
+def tile_terms(tiles, ready, picked, out):
     own = own_slots()
-
-    def body(g, carry):
+    for g in range(CHUNKS):
         ready(g)
-        rows = pl.ds(g * GROUP, GROUP)
+        rows = slice(g * GROUP, (g + 1) * GROUP)
         out[rows, :] = dot(spread(picked[rows, :], own), tiles[rows].reshape(GROUP * T, T))
-        return carry
-
-    lax.fori_loop(0, CHUNKS, body, 0)
-
-
-def load_terms(tiles, sent, out):
-    own = own_slots()
-
-    def body(g, carry):
-        rows = pl.ds(g * GROUP, GROUP)
-        wide = jnp.concatenate([tiles[g * GROUP + i] for i in range(GROUP)], axis=1)
-        out[rows, :] = dot_t(spread(sent[rows, :], own), wide)
-        return carry
-
-    lax.fori_loop(0, CHUNKS, body, 0)
+
+
+def turn_kernel(tiles, out):
+    for s in range(S):
+        out[s] = tiles[s].T
 
 
 def first_route_kernel(
@@ -127,12 +113,12 @@
     ]
 
     def copy(g):
-        rows = pl.ds(g * GROUP, GROUP)
+        rows = pl.ds(g * FETCH, FETCH)
         return pltpu.make_async_copy(tiles.at[rows], kept.at[rows], sems.at[g])
 
     for c in small:
         c.start()
-    for g in range(CHUNKS):
+    for g in range(S // FETCH):
         copy(g).start()
     for c in small:
         c.wait()
@@ -146,7 +132,12 @@
     at = lax.broadcasted_iota(jnp.int32, (S, T), 1)
     hits = [jnp.where(column == at + c * T, 1.0, 0.0).astype(bf16) for c in range(price.shape[0] // T)]
     picked[...] = dot(jnp.concatenate(hits, axis=1), price[...].astype(bf16)).astype(bf16)
-    route_terms(kept, lambda g: copy(g).wait(), picked, terms)
+
+    def ready(g):
+        if g * GROUP % FETCH == 0:
+            copy(g * GROUP // FETCH).wait()
+
+    tile_terms(kept, ready, picked, terms)
     put_payload(out, terms[...], flow_used)
 
 
@@ -154,7 +145,7 @@
     blocks, (out, sent, terms) = rest[:-3], rest[-3:]
     route_sum = matched_sum(index[:S, :], blocks, decode(blocks))
     sent[...] = (own[0] / (own[1] + route_sum)).astype(bf16)
-    load_terms(tiles, sent, terms)
+    tile_terms(tiles, lambda g: None, sent, terms)
     put_payload(out, terms[...], index[2 * S + 1 : 2 * S + 2, :])
 
 
@@ -162,42 +153,85 @@
     blocks, (out, picked, terms) = rest[:-3], rest[-3:]
     load = matched_sum(index[S : 2 * S, :], blocks, decode(blocks))
     picked[...] = (own[2] * jnp.exp(step_size * (load / own[3] - 1.0))).astype(bf16)
-    route_terms(tiles, lambda g: None, picked, terms)
+    tile_terms(tiles, lambda g: None, picked, terms)
     put_payload(out, terms[...], index[2 * S : 2 * S + 1, :])
 
 
+def every_sum(blocks, code, hits, n, emit):
+    code[...] = decode(blocks)
+    rows = lax.broadcasted_iota(jnp.int32, (S, T), 0)
+    chunk, scale = [], []
+    for ref in blocks:
+        for k in range(ref.shape[0]):
+            index = ref[k, INDEX:EXPONENT, :]
+            at = slice(len(chunk) * T, (len(chunk) + 1) * T)
+            hits[:, at] = jnp.where(rows == (index & (T - 1)), 1.0, 0.0).astype(bf16)
+            chunk.append(index >> 7)
+            scale.append(jnp.exp2((ref[k, EXPONENT : EXPONENT + 1, :] - 16).astype(f32)))
+    chunk = jnp.concatenate(chunk, axis=1)
+    scale = jnp.concatenate(scale, axis=1)
+    for c in range(n):
+        mine = jnp.where(chunk == c, scale, 0.0)
+        mine = jnp.broadcast_to(mine, (GROUP, mine.shape[1])).astype(bf16)
+        both = dot(hits[...] * jnp.concatenate([mine] * (S // GROUP), axis=0), code[...])
+        emit(slice(c * T, (c + 1) * T), both[:, :T] + both[:, T:])
+
+
 def rate_kernel(weight, access, *rest):
-    blocks, (out, code) = rest[:-2], rest[-2:]
-    code[...] = decode(blocks)
-
-    def body(c, carry):
-        column = lax.broadcasted_iota(jnp.int32, (S, T), 0) + c * T
-        total = matched_sum(column, blocks, code[...])
-        rows = pl.ds(pl.multiple_of(c * T, T), T)
-        out[rows, :] = weight[rows, :] / (access[rows, :] + total)
-        return carry
-
-    lax.fori_loop(0, out.shape[0] // T, body, 0)
-
-
-def price_kernel(price, capacity, *rest):
-    blocks, (out, code) = rest[:-2], rest[-2:]
-    code[...] = decode(blocks)
-
-    def body(c, carry):
-        column = lax.broadcasted_iota(jnp.int32, (S, T), 0) + c * T
-        total = matched_sum(column, blocks, code[...])
-        rows = pl.ds(pl.multiple_of(c * T, T), T)
+    blocks, (out, code, hits, buf, sems) = rest[:-5], rest[-5:]
+    copies = []
+
+    def emit(rows, total):
+        buf[rows, :] = weight[rows, :] / (access[rows, :] + total)
+        copies.append(pltpu.make_async_copy(buf.at[rows], out.at[rows], sems.at[len(copies)]))
+        copies[-1].start()
+
+    every_sum(blocks, code, hits, out.shape[0] // T, emit)
+    for c in copies:
+        c.wait()
+
+
+def first_price_kernel(price, capacity, *rest):
+    blocks, (out, code, hits) = rest[:-3], rest[-3:]
+
+    def emit(rows, total):
         out[rows, :] = price[rows, :] * jnp.exp(step_size * (total / capacity[rows, :] - 1.0))
-        return carry
-
-    lax.fori_loop(0, out.shape[0] // T, body, 0)
-
-
-def prepare_kernel(flow_in, link_in, flow_class, table, access, price, capacity, weight, own, sems, flow_at, link_at):
-    small = [pltpu.make_async_copy(flow_in, flow_at, sems.at[0]), pltpu.make_async_copy(link_in, link_at, sems.at[1])]
-    for c in small:
+
+    every_sum(blocks, code, hits, out.shape[0] // T, emit)
+
+
+def last_price_kernel(price, capacity, *rest):
+    blocks, (out, code, hits, buf, sems) = rest[:-5], rest[-5:]
+    copies = []
+
+    def emit(rows, total):
+        buf[rows, :] = price[rows, :] * jnp.exp(step_size * (total / capacity[rows, :] - 1.0))
+        copies.append(pltpu.make_async_copy(buf.at[rows], out.at[rows], sems.at[len(copies)]))
+        copies[-1].start()
+
+    every_sum(blocks, code, hits, out.shape[0] // T, emit)
+    for c in copies:
+        c.wait()
+
+
+def prepare_kernel(
+    flow_in, link_in, class_in, table_in, access_in, price_in, capacity_in,
+    weight, own, access, price, capacity, sems, flow_at, link_at, flow_class, table,
+):
+    ends = (
+        (class_in, flow_class),
+        (table_in, table),
+        (flow_in, flow_at),
+        (link_in, link_at),
+        (access_in, access),
+        (price_in, price),
+        (capacity_in, capacity),
+    )
+    copies = [pltpu.make_async_copy(a, b, sems.at[i]) for i, (a, b) in enumerate(ends)]
+    for c in copies:
         c.start()
+    for c in copies[:2]:
+        c.wait()
     low = jnp.broadcast_to(table[0:1, :], (8, T))
     high = jnp.broadcast_to(table[1:2, :], (8, T))
 
@@ -210,9 +244,8 @@
         weight[rows, :] = jnp.where(which < T, from_low, from_high)
         return carry
 
-    lax.fori_loop(0, flow_class.shape[0] // 8, look, 0, unroll=8)
-
-    for c in small:
+    lax.fori_loop(0, flow_class.shape[0] // 8, look, 0, unroll=16)
+    for c in copies[2:]:
         c.wait()
 
     def pick(s, carry):
@@ -224,7 +257,7 @@
         own[3, pl.ds(s, 1), :] = capacity[pl.ds(l, 1), :]
         return carry
 
-    lax.fori_loop(0, S, pick, 0, unroll=8)
+    lax.fori_loop(0, S, pick, 0, unroll=16)
 
 
 def shifts():
@@ -237,9 +270,9 @@
         return [(device(*p), device(*f(*p))) for p in every]
 
     order = (1, 3, 2)
-    first = [moved(lambda y, c, x, z, d=d: (y, c, x + d, z) if c == 0 else (y, c, x, z + d)) for d in order]
-    second = [moved(lambda y, c, x, z, d=d: (y, c, x, z + d) if c == 0 else (y, c, x + d, z)) for d in order]
-    along_y = [moved(lambda y, c, x, z, d=d: (y + d, c, x, z)) for d in order]
+    first = [moved(lambda y, c, x, z, d=d: (y, 1, x + d, z) if c == 0 else (y, 0, x, z + d)) for d in order]
+    second = [moved(lambda y, c, x, z, d=d: (y, 1, x + d, z) if c == 0 else (y, 0, x, z + d)) for d in order]
+    along_y = [moved(lambda y, c, x, z, d=d: (y + d, 1 - c, x, z)) for d in order]
     partner = moved(lambda y, c, x, z: (y, 1 - c, x, z))
     return first, second, along_y, partner
 
@@ -252,11 +285,13 @@
 
 
 def gather_link(x):
-    near = jnp.stack([x] + [send(x, p) for p in FIRST])
-    far = []
+    near, far = [send(x, PARTNER)], []
+    for p in FIRST:
+        near.append(send(x, p))
+    near = jnp.stack(near)
     for p in SECOND:
         far.append(send(near, p))
-    return [near] + far
+    return [send(near, PARTNER)] + far
 
 
 def gather_flow(x):
@@ -295,16 +330,19 @@
             compiler_params=PARAMS,
         )(in_vmem(index), in_vmem(own), in_vmem(tiles), *[in_vmem(x) for x in blocks])
 
-    def full_call(body, a, b, blocks):
+    def full_call(body, a, b, blocks, last):
         pieces = sum(x.shape[0] for x in blocks)
+        scratch = [pltpu.VMEM((pieces * S, 2 * T), bf16), pltpu.VMEM((S, pieces * S), bf16)]
+        if last:
+            scratch += [pltpu.VMEM(a.shape, f32), pltpu.SemaphoreType.DMA((a.shape[0] // T,))]
         return pl.pallas_call(
             body,
-            out_shape=jax.ShapeDtypeStruct(a.shape, f32),
+            out_shape=pltpu.HBM(a.shape, f32) if last else pltpu.VMEM(a.shape, f32),
             in_specs=[VM] * (2 + len(blocks)),
-            out_specs=VM,
-            scratch_shapes=[pltpu.VMEM((pieces * S, 2 * T), bf16)],
+            out_specs=HB if last else VM,
+            scratch_shapes=scratch,
             compiler_params=PARAMS,
-        )(a, b, *[in_vmem(x) for x in blocks])
+        )(in_vmem(a), in_vmem(b), *[in_vmem(x) for x in blocks])
 
     route_one, tiles, index = pl.pallas_call(
         first_route_kernel,
@@ -312,7 +350,7 @@
         in_specs=[SM] + [HB] * 4,
         out_specs=(VM, VM, VM),
         scratch_shapes=[
-            pltpu.SemaphoreType.DMA((CHUNKS,)),
+            pltpu.SemaphoreType.DMA((S // FETCH,)),
             pltpu.SemaphoreType.DMA((3,)),
             pltpu.VMEM((1, S), jnp.int32),
             pltpu.VMEM((1, S), jnp.int32),
@@ -323,23 +361,55 @@
         compiler_params=PARAMS,
         name="first_route",
     )(tile_count, *[in_hbm(x) for x in (tile_flow, tile_link, price, route_tiles)])
-    weight, own = pl.pallas_call(
+    turned = pl.pallas_call(
+        turn_kernel,
+        out_shape=pltpu.VMEM((S, T, T), bf16),
+        in_specs=[VM],
+        out_specs=VM,
+        compiler_params=PARAMS,
+        name="turn",
+    )(in_vmem(tiles))
+    full = (access.shape, price.shape, cap.shape)
+    weight, own, access, price, cap = pl.pallas_call(
         prepare_kernel,
-        out_shape=(pltpu.VMEM((flow_blocks, T), f32), pltpu.VMEM((4, S, T), f32)),
-        in_specs=[HB, HB] + [VM] * 5,
-        out_specs=(VM, VM),
-        scratch_shapes=[pltpu.SemaphoreType.DMA((2,)), pltpu.SMEM((1, S), jnp.int32), pltpu.SMEM((1, S), jnp.int32)],
+        out_shape=(
+            pltpu.VMEM((flow_blocks, T), f32),
+            pltpu.VMEM((4, S, T), f32),
+            *[pltpu.VMEM(shape, f32) for shape in full],
+        ),
+        in_specs=[HB] * 7,
+        out_specs=(VM,) * 5,
+        scratch_shapes=[
+            pltpu.SemaphoreType.DMA((7,)),
+            pltpu.SMEM((1, S), jnp.int32),
+            pltpu.SMEM((1, S), jnp.int32),
+            pltpu.VMEM((flow_blocks, T), jnp.int32),
+            pltpu.VMEM((2, T), f32),
+        ],
         compiler_params=PARAMS,
         name="prepare",
-    )(in_hbm(tile_flow), in_hbm(tile_link), flow_class.reshape(flow_blocks, T), class_weight.reshape(2, T), access, price, cap)
+    )(
+        *[
+            in_hbm(x)
+            for x in (
+                tile_flow,
+                tile_link,
+                flow_class.reshape(flow_blocks, T),
+                class_weight.reshape(2, T),
+                access,
+                price,
+                cap,
+            )
+        ]
+    )
 
     routes = gather_link(route_one)
-    loads = gather_flow(tile_call(load_kernel, own, tiles, routes))
-    price_one = full_call(price_kernel, price, cap, loads)
+    loads = gather_flow(tile_call(load_kernel, own, turned, routes))
+    price_one = full_call(first_price_kernel, price, cap, loads, False)
     routes = gather_link(tile_call(route_kernel, own, tiles, loads))
-    rate = full_call(rate_kernel, weight, access, routes)
-    loads = gather_flow(tile_call(load_kernel, own, tiles, routes))
-    price_two = full_call(price_kernel, price_one, cap, loads)
+    rate = full_call(rate_kernel, weight, access, routes, True)
+    loads = gather_flow(tile_call(load_kernel, own, turned, routes))
+    price_two = full_call(last_price_kernel, price_one, cap, loads, True)
     return (rate.reshape(-1), price_two.reshape(-1))
 
 

time: 76.8 us -> 65 us (0.85)
  Pallas kernels: 19.8 us -> 15 us
  waiting for transfers between devices: 28.9 us -> 24.2 us
  starting transfers between devices: 25 us -> 23.2 us
    ppermute x20 -> x24, waiting for transfers between devices: 28.9 us -> 24.2 us  [send(): return lax.ppermute(x, ('flow', 'link'), perm)]
    pallas_call x3, Pallas kernels: 7.23 us -> 3.74 us  [tile_call(): pl.pallas_call(body, out_shape=payload, in_specs=[VM] * (3 + len(blocks))...]
    ppermute x20 -> x24, starting transfers between devices: 25 us -> 23.2 us  [send(): return lax.ppermute(x, ('flow', 'link'), perm)]
    pallas_call x3 -> x4, Pallas kernels: 6.46 us -> 5.27 us  [the longest x3 4.14 us: full_call(): pl.pallas_call(body, out_shape=pltpu.HBM(a.shape, f32) if last else pltpu...]
  transfers between devices with their start and end apart: 20 -> 24, of which waited for: 16 -> 14; matrix products, arithmetic and copies ran while one was open for 0% -> 0% of each run, Pallas kernels for 9% -> 10%
where the time goes in v1:
time: 65 us; the launch traced here: 63.9 us
  waiting for transfers between devices  24.2 us (37%)
  starting transfers between devices  23.2 us (36%)
  Pallas kernels  15 us (23%)
  between operations  1.54 us (2%)
    ppermute x24, waiting for transfers between devices, send(): return lax.ppermute(x, ('flow', 'link'), perm)  24.2 us
    ppermute x24, starting transfers between devices, send(): return lax.ppermute(x, ('flow', 'link'), perm)  23.2 us
    pallas_call x3, Pallas kernels, full_call(): pl.pallas_call(body, out_shape=pltpu.HBM(a.shape, f32) if last else pltpu...  4.14 us
    pallas_call x3, Pallas kernels, tile_call(): pl.pallas_call(body, out_shape=payload, in_specs=[VM] * (3 + len(blocks))...  3.74 us
    pallas_call x1, Pallas kernels, on_device(): pl.pallas_call(first_route_kernel, out_shape=(payload, pltpu.VMEM((S, T,...  3.38 us
    pallas_call x1, Pallas kernels, on_device(): pl.pallas_call(prepare_kernel, out_shape=(pltpu.VMEM((flow_blocks, T), f3...  2.58 us
  transfers between devices with their start and end apart: 24, of which 14 were waited for; matrix products, arithmetic and copies ran while one was open for 0% of the time, Pallas kernels for 10%

profile of v1, /device:TPU:0, one launch (start us, length us, event | category | flops | bytes accessed | tf_op | source)
XLA Modules:
  0.0 63.9 jit_solution(9112631978631227846)
XLA Ops:
  1.3 3.4 %first_route.1 = (s32[72,128]{1,0:T(8,128)S(1)}, bf16[128,128,128]{2,1,0:T(8,128)(2,1)S(1)}, s32[264,128]{1,0:T(8,128)S(1)}) custom-call(s32[1,1]{1,0:T(1,128)S(6)} %copy.11.count, s32[1,128]{1,0:T(1,128)} %flow_in.3, s32[1,128]{1,0:T(1,128)} %link_in.3, f32[512,128]{1,0:T(8,128)} %bitcast.25, bf16[128,128,128]{2,1,0:T(8,128)(2,1)} %tiles.1), custom_call_target="tpu_custom_call" | custom-call | tf_op jit(solution)/shard_map/first_route/pallas_call | solution.py:347
  4.7 2.6 %collective-permute-start.3 = (s32[72,128]{1,0:T(8,128)S(1)}, s32[72,128]{1,0:T(8,128)S(1)}, u32[]{:S(2)}, u32[]{:S(2)}) collective-permute-start(s32[72,128]{1,0:T(8,128)S(1)} %get-tuple-element.15), channel_id=1, source_target_pairs={{0,24},{1,25},{2,26},{3,27},{4,28},{5,29},{6,30},{7,31},{8,16},{9,... | collective-permute-start | bytes 110600 | tf_op jit(solution)/shard_map/ppermute | solution.py:284
  7.3 3.9 %collective-permute-start.2 = (s32[72,128]{1,0:T(8,128)S(1)}, s32[72,128]{1,0:T(8,128)S(1)}, u32[]{:S(2)}, u32[]{:S(2)}) collective-permute-start(s32[72,128]{1,0:T(8,128)S(1)} %get-tuple-element.15), channel_id=1, source_target_pairs={{0,28},{1,29},{2,30},{3,31},{4,16},{5,17},{6,18},{7,19},{8,20},{9,... | collective-permute-start | bytes 110600 | tf_op jit(solution)/shard_map/ppermute | solution.py:284
  12.8 3.0 %collective-permute-done.1 = s32[72,128]{1,0:T(8,128)S(1)} collective-permute-done((s32[72,128]{1,0:T(8,128)S(1)}, s32[72,128]{1,0:T(8,128)S(1)}, u32[]{:S(2)}, u32[]{:S(2)}) %collective-permute-start.1) | collective-permute-done | bytes 36896 | tf_op jit(solution)/shard_map/ppermute | solution.py:284
  16.3 1.2 %collective-permute-start.5 = (s32[4,72,128]{2,1,0:T(8,128)S(1)}, s32[4,72,128]{2,1,0:T(8,128)S(1)}, u32[]{:S(2)}, u32[]{:S(2)}) collective-permute-start(s32[4,72,128]{2,1,0:T(8,128)S(1)} %pad_add_fusion), channel_id=1, source_target_pairs={{0,20},{1,21},{2,22},{3,23},{4,24},{5,25},{6,26},{7,27},{8,28},{9,... | collective-permute-start | bytes 442376 | tf_op jit(solution)/shard_map/ppermute | solution.py:284
  17.9 1.1 %turn.1.tiles = bf16[128,128,128]{2,1,0:T(8,128)(2,1)S(1)} custom-call(bf16[128,128,128]{2,1,0:T(8,128)(2,1)S(1)} %get-tuple-element.14.tiles), custom_call_target="tpu_custom_call" | custom-call | tf_op jit(solution)/shard_map/turn/pallas_call | solution.py:364
  19.0 2.6 %prepare.1 = (f32[1024,128]{1,0:T(8,128)S(1)}, f32[4,128,128]{2,1,0:T(8,128)S(1)}, f32[1024,128]{1,0:T(8,128)S(1)}, f32[512,128]{1,0:T(8,128)S(1)}, f32[512,128]{1,0:T(8,128)S(1)}) custom-call(s32[1,128]{1,0:T(1,128)} %flow_in.3, s32[1,128]{1,0:T(1,128)} %link_in.3, s32[1024,128]{1,0:T(8,128)} %bitcast.27, f32[2,128]{1,0:T(2,128)} %bitcast.46, ...), custom_call_target="tpu_custom_call" | custom-call | tf_op jit(solution)/shard_map/prepare/pallas_call | solution.py:373
  22.1 1.5 %collective-permute-done.5.rest_1_ = s32[4,72,128]{2,1,0:T(8,128)S(1)} collective-permute-done((s32[4,72,128]{2,1,0:T(8,128)S(1)}, s32[4,72,128]{2,1,0:T(8,128)S(1)}, u32[]{:S(2)}, u32[]{:S(2)}) %collective-permute-start.5) | collective-permute-done | bytes 147488 | tf_op jit(solution)/shard_map/ppermute | solution.py:284
  23.5 1.3 %shard_map.104 = s32[72,128]{1,0:T(8,128)S(1)} custom-call(s32[264,128]{1,0:T(8,128)S(1)} %get-tuple-element.12.index, f32[4,128,128]{2,1,0:T(8,128)S(1)} %get-tuple-element.13.own, bf16[128,128,128]{2,1,0:T(8,128)(2,1)S(1)} %turn.1.tiles, s32[4,72,128]{2,1,0:T(8,128)S(1)} %collective-permute-done.4.rest_0_, ...), custom_call_target="tpu_custom_call" | custom-call | tf_op jit(solution)/shard_map/pallas_call | solution.py:324
  24.9 3.1 %collective-permute-start.10 = (s32[72,128]{1,0:T(8,128)S(1)}, s32[72,128]{1,0:T(8,128)S(1)}, u32[]{:S(2)}, u32[]{:S(2)}) collective-permute-start(s32[72,128]{1,0:T(8,128)S(1)} %shard_map.104), channel_id=1, source_target_pairs={{0,80},{1,81},{2,82},{3,83},{4,84},{5,85},{6,86},{7,87},{8,88},{9,... | collective-permute-start | bytes 110600 | tf_op jit(solution)/shard_map/ppermute | solution.py:284
  29.8 1.6 %collective-permute-done.9 = s32[72,128]{1,0:T(8,128)S(1)} collective-permute-done((s32[72,128]{1,0:T(8,128)S(1)}, s32[72,128]{1,0:T(8,128)S(1)}, u32[]{:S(2)}, u32[]{:S(2)}) %collective-permute-start.9) | collective-permute-done | bytes 36896 | tf_op jit(solution)/shard_map/ppermute | solution.py:284
  31.4 2.1 %collective-permute-done.8 = s32[72,128]{1,0:T(8,128)S(1)} collective-permute-done((s32[72,128]{1,0:T(8,128)S(1)}, s32[72,128]{1,0:T(8,128)S(1)}, u32[]{:S(2)}, u32[]{:S(2)}) %collective-permute-start.8) | collective-permute-done | bytes 36896 | tf_op jit(solution)/shard_map/ppermute | solution.py:284
  36.1 1.5 %collective-permute-start.15 = (s32[72,128]{1,0:T(8,128)S(1)}, s32[72,128]{1,0:T(8,128)S(1)}, u32[]{:S(2)}, u32[]{:S(2)}) collective-permute-start(s32[72,128]{1,0:T(8,128)S(1)} %shard_map.105), channel_id=1, source_target_pairs={{0,24},{1,25},{2,26},{3,27},{4,28},{5,29},{6,30},{7,31},{8,16},{9,... | collective-permute-start | bytes 110600 | tf_op jit(solution)/shard_map/ppermute | solution.py:284
  39.1 1.9 %collective-permute-done.15 = s32[72,128]{1,0:T(8,128)S(1)} collective-permute-done((s32[72,128]{1,0:T(8,128)S(1)}, s32[72,128]{1,0:T(8,128)S(1)}, u32[]{:S(2)}, u32[]{:S(2)}) %collective-permute-start.15) | collective-permute-done | bytes 36896 | tf_op jit(solution)/shard_map/ppermute | solution.py:284
  41.0 2.2 %collective-permute-done.13 = s32[72,128]{1,0:T(8,128)S(1)} collective-permute-done((s32[72,128]{1,0:T(8,128)S(1)}, s32[72,128]{1,0:T(8,128)S(1)}, u32[]{:S(2)}, u32[]{:S(2)}) %collective-permute-start.13) | collective-permute-done | bytes 36896 | tf_op jit(solution)/shard_map/ppermute | solution.py:284
  43.3 1.5 %collective-permute-start.18 = (s32[4,72,128]{2,1,0:T(8,128)S(1)}, s32[4,72,128]{2,1,0:T(8,128)S(1)}, u32[]{:S(2)}, u32[]{:S(2)}) collective-permute-start(s32[4,72,128]{2,1,0:T(8,128)S(1)} %pad_add_fusion.2), channel_id=1, source_target_pairs={{0,28},{1,29},{2,30},{3,31},{4,16},{5,17},{6,18},{7,19},{8,20},{9,... | collective-permute-start | bytes 442376 | tf_op jit(solution)/shard_map/ppermute | solution.py:284
  45.6 3.8 %collective-permute-done.19.rest_3_ = s32[4,72,128]{2,1,0:T(8,128)S(1)} collective-permute-done((s32[4,72,128]{2,1,0:T(8,128)S(1)}, s32[4,72,128]{2,1,0:T(8,128)S(1)}, u32[]{:S(2)}, u32[]{:S(2)}) %collective-permute-start.19) | collective-permute-done | bytes 147488 | tf_op jit(solution)/shard_map/ppermute | solution.py:284
  49.4 1.5 %collective-permute-done.17.rest_1_ = s32[4,72,128]{2,1,0:T(8,128)S(1)} collective-permute-done((s32[4,72,128]{2,1,0:T(8,128)S(1)}, s32[4,72,128]{2,1,0:T(8,128)S(1)}, u32[]{:S(2)}, u32[]{:S(2)}) %collective-permute-start.17) | collective-permute-done | bytes 147488 | tf_op jit(solution)/shard_map/ppermute | solution.py:284
  50.9 1.3 %shard_map.108 = s32[72,128]{1,0:T(8,128)S(1)} custom-call(s32[264,128]{1,0:T(8,128)S(1)} %get-tuple-element.12.index, f32[4,128,128]{2,1,0:T(8,128)S(1)} %get-tuple-element.13.own, bf16[128,128,128]{2,1,0:T(8,128)(2,1)S(1)} %turn.1.tiles, s32[4,72,128]{2,1,0:T(8,128)S(1)} %collective-permute-done.16.rest_0_, ...), custom_call_target="tpu_custom_call" | custom-call | tf_op jit(solution)/shard_map/pallas_call | solution.py:324
  52.9 1.6 %collective-permute-start.21 = (s32[72,128]{1,0:T(8,128)S(1)}, s32[72,128]{1,0:T(8,128)S(1)}, u32[]{:S(2)}, u32[]{:S(2)}) collective-permute-start(s32[72,128]{1,0:T(8,128)S(1)} %shard_map.108), channel_id=1, source_target_pairs={{0,112},{1,113},{2,114},{3,115},{4,116},{5,117},{6,118},{7,119},{8... | collective-permute-start | bytes 110600 | tf_op jit(solution)/shard_map/ppermute | solution.py:284
  54.6 2.6 %collective-permute-done.22 = s32[72,128]{1,0:T(8,128)S(1)} collective-permute-done((s32[72,128]{1,0:T(8,128)S(1)}, s32[72,128]{1,0:T(8,128)S(1)}, u32[]{:S(2)}, u32[]{:S(2)}) %collective-permute-start.22) | collective-permute-done | bytes 36896 | tf_op jit(solution)/shard_map/ppermute | solution.py:284
  57.2 1.9 %collective-permute-done.20 = s32[72,128]{1,0:T(8,128)S(1)} collective-permute-done((s32[72,128]{1,0:T(8,128)S(1)}, s32[72,128]{1,0:T(8,128)S(1)}, u32[]{:S(2)}, u32[]{:S(2)}) %collective-permute-start.20) | collective-permute-done | bytes 36896 | tf_op jit(solution)/shard_map/ppermute | solution.py:284
  60.2 2.3 %shard_map.106 = f32[1024,128]{1,0:T(8,128)} custom-call(f32[1024,128]{1,0:T(8,128)S(1)} %get-tuple-element.10.weight, f32[1024,128]{1,0:T(8,128)S(1)} %get-tuple-element.11.access, s32[4,72,128]{2,1,0:T(8,128)S(1)} %collective-permute-done.16.rest_0_, s32[4,72,128]{2,1,0:T(8,128)S(1)} %collective-permute-done.17.rest_1_, ...), custom_call_target="tpu_custom_call" | custom-call | tf_op jit(solution)/shard_map/pallas_call | solution.py:338
  62.5 1.3 %shard_map.109 = f32[512,128]{1,0:T(8,128)} custom-call(f32[512,128]{1,0:T(8,128)S(1)} %shard_map.107.price, f32[512,128]{1,0:T(8,128)S(1)} %get-tuple-element.17.capacity, s32[4,72,128]{2,1,0:T(8,128)S(1)} %pad_add_fusion.3.rest_0_, s32[4,72,128]{2,1,0:T(8,128)S(1)} %collective-permute-done.23.rest_1_), custom_call_target="tpu_custom_call" | custom-call | tf_op jit(solution)/shard_map/pallas_call | solution.py:338
  (37 shorter events, 11.6 us)
Async XLA Ops:
  4.7 7.7 %collective-permute-start.3 = (s32[72,128]{1,0:T(8,128)S(1)}, s32[72,128]{1,0:T(8,128)S(1)}, u32[]{:S(2)}, u32[]{:S(2)}) collective-permute-start(s32[72,128]{1,0:T(8,128)S(1)} %get-tuple-element.15), channel_id=1, source_target_pairs={{0,24},{1,25},{2,26},{3,27},{4,28},{5,29},{6,30},{7,31},{8,16},{9,... | collective-permute-start | bytes 110600 | tf_op jit(solution)/shard_map/ppermute | solution.py:284
  7.3 5.5 %collective-permute-start.2 = (s32[72,128]{1,0:T(8,128)S(1)}, s32[72,128]{1,0:T(8,128)S(1)}, u32[]{:S(2)}, u32[]{:S(2)}) collective-permute-start(s32[72,128]{1,0:T(8,128)S(1)} %get-tuple-element.15), channel_id=1, source_target_pairs={{0,28},{1,29},{2,30},{3,31},{4,16},{5,17},{6,18},{7,19},{8,20},{9,... | collective-permute-start | bytes 110600 | tf_op jit(solution)/shard_map/ppermute | solution.py:284
  11.2 4.6 %collective-permute-start.1 = (s32[72,128]{1,0:T(8,128)S(1)}, s32[72,128]{1,0:T(8,128)S(1)}, u32[]{:S(2)}, u32[]{:S(2)}) collective-permute-start(s32[72,128]{1,0:T(8,128)S(1)} %get-tuple-element.15), channel_id=1, source_target_pairs={{0,20},{1,21},{2,22},{3,23},{4,24},{5,25},{6,26},{7,27},{8,28},{9,... | collective-permute-start | bytes 110600 | tf_op jit(solution)/shard_map/ppermute | solution.py:284
  11.7 4.1 %collective-permute-start = (s32[72,128]{1,0:T(8,128)S(1)}, s32[72,128]{1,0:T(8,128)S(1)}, u32[]{:S(2)}, u32[]{:S(2)}) collective-permute-start(s32[72,128]{1,0:T(8,128)S(1)} %get-tuple-element.15), channel_id=1, source_target_pairs={{0,16},{1,17},{2,18},{3,19},{4,20},{5,21},{6,22},{7,23},{8,24},{9,... | collective-permute-start | bytes 110600 | tf_op jit(solution)/shard_map/ppermute | solution.py:284
  15.8 6.2 %collective-permute-start.7 = (s32[4,72,128]{2,1,0:T(8,128)S(1)}, s32[4,72,128]{2,1,0:T(8,128)S(1)}, u32[]{:S(2)}, u32[]{:S(2)}) collective-permute-start(s32[4,72,128]{2,1,0:T(8,128)S(1)} %pad_add_fusion), channel_id=1, source_target_pairs={{0,24},{1,25},{2,26},{3,27},{4,28},{5,29},{6,30},{7,31},{8,16},{9,... | collective-permute-start | bytes 442376 | tf_op jit(solution)/shard_map/ppermute | solution.py:284
  15.9 6.2 %collective-permute-start.6 = (s32[4,72,128]{2,1,0:T(8,128)S(1)}, s32[4,72,128]{2,1,0:T(8,128)S(1)}, u32[]{:S(2)}, u32[]{:S(2)}) collective-permute-start(s32[4,72,128]{2,1,0:T(8,128)S(1)} %pad_add_fusion), channel_id=1, source_target_pairs={{0,28},{1,29},{2,30},{3,31},{4,16},{5,17},{6,18},{7,19},{8,20},{9,... | collective-permute-start | bytes 442376 | tf_op jit(solution)/shard_map/ppermute | solution.py:284
  16.3 7.3 %collective-permute-start.5 = (s32[4,72,128]{2,1,0:T(8,128)S(1)}, s32[4,72,128]{2,1,0:T(8,128)S(1)}, u32[]{:S(2)}, u32[]{:S(2)}) collective-permute-start(s32[4,72,128]{2,1,0:T(8,128)S(1)} %pad_add_fusion), channel_id=1, source_target_pairs={{0,20},{1,21},{2,22},{3,23},{4,24},{5,25},{6,26},{7,27},{8,28},{9,... | collective-permute-start | bytes 442376 | tf_op jit(solution)/shard_map/ppermute | solution.py:284
  17.5 6.1 %collective-permute-start.4 = (s32[4,72,128]{2,1,0:T(8,128)S(1)}, s32[4,72,128]{2,1,0:T(8,128)S(1)}, u32[]{:S(2)}, u32[]{:S(2)}) collective-permute-start(s32[4,72,128]{2,1,0:T(8,128)S(1)} %pad_add_fusion), channel_id=1, source_target_pairs={{0,16},{1,17},{2,18},{3,19},{4,20},{5,21},{6,22},{7,23},{8,24},{9,... | collective-permute-start | bytes 442376 | tf_op jit(solution)/shard_map/ppermute | solution.py:284
  24.9 4.9 %collective-permute-start.10 = (s32[72,128]{1,0:T(8,128)S(1)}, s32[72,128]{1,0:T(8,128)S(1)}, u32[]{:S(2)}, u32[]{:S(2)}) collective-permute-start(s32[72,128]{1,0:T(8,128)S(1)} %shard_map.104), channel_id=1, source_target_pairs={{0,80},{1,81},{2,82},{3,83},{4,84},{5,85},{6,86},{7,87},{8,88},{9,... | collective-permute-start | bytes 110600 | tf_op jit(solution)/shard_map/ppermute | solution.py:284
  28.0 3.4 %collective-permute-start.9 = (s32[72,128]{1,0:T(8,128)S(1)}, s32[72,128]{1,0:T(8,128)S(1)}, u32[]{:S(2)}, u32[]{:S(2)}) collective-permute-start(s32[72,128]{1,0:T(8,128)S(1)} %shard_map.104), channel_id=1, source_target_pairs={{0,112},{1,113},{2,114},{3,115},{4,116},{5,117},{6,118},{7,119},{8... | collective-permute-start | bytes 110600 | tf_op jit(solution)/shard_map/ppermute | solution.py:284
  28.9 4.6 %collective-permute-start.8 = (s32[72,128]{1,0:T(8,128)S(1)}, s32[72,128]{1,0:T(8,128)S(1)}, u32[]{:S(2)}, u32[]{:S(2)}) collective-permute-start(s32[72,128]{1,0:T(8,128)S(1)} %shard_map.104), channel_id=1, source_target_pairs={{0,48},{1,49},{2,50},{3,51},{4,52},{5,53},{6,54},{7,55},{8,56},{9,... | collective-permute-start | bytes 110600 | tf_op jit(solution)/shard_map/ppermute | solution.py:284
  33.5 1.5 %collective-permute-start.11 = (s32[4,72,128]{2,1,0:T(8,128)S(1)}, s32[4,72,128]{2,1,0:T(8,128)S(1)}, u32[]{:S(2)}, u32[]{:S(2)}) collective-permute-start(s32[4,72,128]{2,1,0:T(8,128)S(1)} %pad_add_fusion.1.rest_0_), channel_id=1, source_target_pairs={{0,16},{1,17},{2,18},{3,19},{4,20},{5,21},{6,22},{7,23},{8,24},{9,... | collective-permute-start | bytes 442376 | tf_op jit(solution)/shard_map/ppermute | solution.py:284
  36.1 4.9 %collective-permute-start.15 = (s32[72,128]{1,0:T(8,128)S(1)}, s32[72,128]{1,0:T(8,128)S(1)}, u32[]{:S(2)}, u32[]{:S(2)}) collective-permute-start(s32[72,128]{1,0:T(8,128)S(1)} %shard_map.105), channel_id=1, source_target_pairs={{0,24},{1,25},{2,26},{3,27},{4,28},{5,29},{6,30},{7,31},{8,16},{9,... | collective-permute-start | bytes 110600 | tf_op jit(solution)/shard_map/ppermute | solution.py:284
  37.6 3.4 %collective-permute-start.14 = (s32[72,128]{1,0:T(8,128)S(1)}, s32[72,128]{1,0:T(8,128)S(1)}, u32[]{:S(2)}, u32[]{:S(2)}) collective-permute-start(s32[72,128]{1,0:T(8,128)S(1)} %shard_map.105), channel_id=1, source_target_pairs={{0,28},{1,29},{2,30},{3,31},{4,16},{5,17},{6,18},{7,19},{8,20},{9,... | collective-permute-start | bytes 110600 | tf_op jit(solution)/shard_map/ppermute | solution.py:284
  38.6 4.6 %collective-permute-start.13 = (s32[72,128]{1,0:T(8,128)S(1)}, s32[72,128]{1,0:T(8,128)S(1)}, u32[]{:S(2)}, u32[]{:S(2)}) collective-permute-start(s32[72,128]{1,0:T(8,128)S(1)} %shard_map.105), channel_id=1, source_target_pairs={{0,20},{1,21},{2,22},{3,23},{4,24},{5,25},{6,26},{7,27},{8,28},{9,... | collective-permute-start | bytes 110600 | tf_op jit(solution)/shard_map/ppermute | solution.py:284
  38.6 4.6 %collective-permute-start.12 = (s32[72,128]{1,0:T(8,128)S(1)}, s32[72,128]{1,0:T(8,128)S(1)}, u32[]{:S(2)}, u32[]{:S(2)}) collective-permute-start(s32[72,128]{1,0:T(8,128)S(1)} %shard_map.105), channel_id=1, source_target_pairs={{0,16},{1,17},{2,18},{3,19},{4,20},{5,21},{6,22},{7,23},{8,24},{9,... | collective-permute-start | bytes 110600 | tf_op jit(solution)/shard_map/ppermute | solution.py:284
  43.2 6.2 %collective-permute-start.19 = (s32[4,72,128]{2,1,0:T(8,128)S(1)}, s32[4,72,128]{2,1,0:T(8,128)S(1)}, u32[]{:S(2)}, u32[]{:S(2)}) collective-permute-start(s32[4,72,128]{2,1,0:T(8,128)S(1)} %pad_add_fusion.2), channel_id=1, source_target_pairs={{0,24},{1,25},{2,26},{3,27},{4,28},{5,29},{6,30},{7,31},{8,16},{9,... | collective-permute-start | bytes 442376 | tf_op jit(solution)/shard_map/ppermute | solution.py:284
  43.3 6.1 %collective-permute-start.18 = (s32[4,72,128]{2,1,0:T(8,128)S(1)}, s32[4,72,128]{2,1,0:T(8,128)S(1)}, u32[]{:S(2)}, u32[]{:S(2)}) collective-permute-start(s32[4,72,128]{2,1,0:T(8,128)S(1)} %pad_add_fusion.2), channel_id=1, source_target_pairs={{0,28},{1,29},{2,30},{3,31},{4,16},{5,17},{6,18},{7,19},{8,20},{9,... | collective-permute-start | bytes 442376 | tf_op jit(solution)/shard_map/ppermute | solution.py:284
  44.8 6.1 %collective-permute-start.17 = (s32[4,72,128]{2,1,0:T(8,128)S(1)}, s32[4,72,128]{2,1,0:T(8,128)S(1)}, u32[]{:S(2)}, u32[]{:S(2)}) collective-permute-start(s32[4,72,128]{2,1,0:T(8,128)S(1)} %pad_add_fusion.2), channel_id=1, source_target_pairs={{0,20},{1,21},{2,22},{3,23},{4,24},{5,25},{6,26},{7,27},{8,28},{9,... | collective-permute-start | bytes 442376 | tf_op jit(solution)/shard_map/ppermute | solution.py:284
  45.4 5.6 %collective-permute-start.16 = (s32[4,72,128]{2,1,0:T(8,128)S(1)}, s32[4,72,128]{2,1,0:T(8,128)S(1)}, u32[]{:S(2)}, u32[]{:S(2)}) collective-permute-start(s32[4,72,128]{2,1,0:T(8,128)S(1)} %pad_add_fusion.2), channel_id=1, source_target_pairs={{0,16},{1,17},{2,18},{3,19},{4,20},{5,21},{6,22},{7,23},{8,24},{9,... | collective-permute-start | bytes 442376 | tf_op jit(solution)/shard_map/ppermute | solution.py:284
  52.2 4.9 %collective-permute-start.22 = (s32[72,128]{1,0:T(8,128)S(1)}, s32[72,128]{1,0:T(8,128)S(1)}, u32[]{:S(2)}, u32[]{:S(2)}) collective-permute-start(s32[72,128]{1,0:T(8,128)S(1)} %shard_map.108), channel_id=1, source_target_pairs={{0,80},{1,81},{2,82},{3,83},{4,84},{5,85},{6,86},{7,87},{8,88},{9,... | collective-permute-start | bytes 110600 | tf_op jit(solution)/shard_map/ppermute | solution.py:284
  52.9 4.3 %collective-permute-start.21 = (s32[72,128]{1,0:T(8,128)S(1)}, s32[72,128]{1,0:T(8,128)S(1)}, u32[]{:S(2)}, u32[]{:S(2)}) collective-permute-start(s32[72,128]{1,0:T(8,128)S(1)} %shard_map.108), channel_id=1, source_target_pairs={{0,112},{1,113},{2,114},{3,115},{4,116},{5,117},{6,118},{7,119},{8... | collective-permute-start | bytes 110600 | tf_op jit(solution)/shard_map/ppermute | solution.py:284
  54.5 4.6 %collective-permute-start.20 = (s32[72,128]{1,0:T(8,128)S(1)}, s32[72,128]{1,0:T(8,128)S(1)}, u32[]{:S(2)}, u32[]{:S(2)}) collective-permute-start(s32[72,128]{1,0:T(8,128)S(1)} %shard_map.108), channel_id=1, source_target_pairs={{0,48},{1,49},{2,50},{3,51},{4,52},{5,53},{6,54},{7,55},{8,56},{9,... | collective-permute-start | bytes 110600 | tf_op jit(solution)/shard_map/ppermute | solution.py:284
  59.1 3.4 %collective-permute-start.23 = (s32[4,72,128]{2,1,0:T(8,128)S(1)}, s32[4,72,128]{2,1,0:T(8,128)S(1)}, u32[]{:S(2)}, u32[]{:S(2)}) collective-permute-start(s32[4,72,128]{2,1,0:T(8,128)S(1)} %pad_add_fusion.3.rest_0_), channel_id=1, source_target_pairs={{0,16},{1,17},{2,18},{3,19},{4,20},{5,21},{6,22},{7,23},{8,24},{9,... | collective-permute-start | bytes 442376 | tf_op jit(solution)/shard_map/ppermute | solution.py:284

commit v2 on v1

--- a/solution.py
+++ b/solution.py
@@ -20,7 +20,7 @@
 EXPONENT = HALF + 1
 GROUP = 16
 CHUNKS = S // GROUP
-FETCH = 32
+FETCH = 64
 
 SM = pl.BlockSpec(memory_space=pltpu.SMEM)
 HB = pl.BlockSpec(memory_space=pltpu.HBM)
@@ -99,9 +99,15 @@
         out[rows, :] = dot(spread(picked[rows, :], own), tiles[rows].reshape(GROUP * T, T))
 
 
-def turn_kernel(tiles, out):
+def turn_kernel(tiles, *rest):
+    sources, (out, *kept), sems = rest[:7], rest[7:15], rest[15]
+    copies = [pltpu.make_async_copy(a, b, sems.at[i]) for i, (a, b) in enumerate(zip(sources, kept))]
+    for c in copies:
+        c.start()
     for s in range(S):
         out[s] = tiles[s].T
+    for c in copies:
+        c.wait()
 
 
 def first_route_kernel(
@@ -119,7 +125,7 @@
     for c in small:
         c.start()
     for g in range(S // FETCH):
-        copy(g).start()
+        copy(g).start(priority=min(g, 1))
     for c in small:
         c.wait()
     used = count[0, 0]
@@ -141,9 +147,23 @@
     put_payload(out, terms[...], flow_used)
 
 
-def load_kernel(index, own, tiles, *rest):
+def early_kernel(index, *rest):
+    blocks, out = rest[:-1], rest[-1]
+    out[...] = matched_sum(index[:S, :], blocks, decode(blocks))
+
+
+def early_price_kernel(*rest):
+    blocks, (out, code, hits) = rest[:-3], rest[-3:]
+
+    def emit(rows, total):
+        out[rows, :] = total
+
+    every_sum(blocks, code, hits, out.shape[0] // T, emit)
+
+
+def load_kernel(index, own, tiles, early, *rest):
     blocks, (out, sent, terms) = rest[:-3], rest[-3:]
-    route_sum = matched_sum(index[:S, :], blocks, decode(blocks))
+    route_sum = early[...] + matched_sum(index[:S, :], blocks, decode(blocks))
     sent[...] = (own[0] / (own[1] + route_sum)).astype(bf16)
     tile_terms(tiles, lambda g: None, sent, terms)
     put_payload(out, terms[...], index[2 * S + 1 : 2 * S + 2, :])
@@ -178,11 +198,30 @@
 
 
 def rate_kernel(weight, access, *rest):
-    blocks, (out, code, hits, buf, sems) = rest[:-5], rest[-5:]
-    copies = []
+    blocks, (out, code, hits) = rest[:-3], rest[-3:]
 
     def emit(rows, total):
-        buf[rows, :] = weight[rows, :] / (access[rows, :] + total)
+        out[rows, :] = weight[rows, :] / (access[rows, :] + total)
+
+    every_sum(blocks, code, hits, out.shape[0] // T, emit)
+
+
+def first_price_kernel(price, capacity, *rest):
+    blocks, (out, code, hits) = rest[:-3], rest[-3:]
+
+    def emit(rows, total):
+        out[rows, :] = price[rows, :] * jnp.exp(step_size * (total / capacity[rows, :] - 1.0))
+
+    every_sum(blocks, code, hits, out.shape[0] // T, emit)
+
+
+def last_price_kernel(price, capacity, early, rate, *rest):
+    blocks, (out, rate_out, code, hits, buf, sems) = rest[:-6], rest[-6:]
+    copies = [pltpu.make_async_copy(rate, rate_out, sems.at[0])]
+    copies[0].start()
+
+    def emit(rows, total):
+        buf[rows, :] = price[rows, :] * jnp.exp(step_size * ((early[rows, :] + total) / capacity[rows, :] - 1.0))
         copies.append(pltpu.make_async_copy(buf.at[rows], out.at[rows], sems.at[len(copies)]))
         copies[-1].start()
 
@@ -191,47 +230,7 @@
         c.wait()
 
 
-def first_price_kernel(price, capacity, *rest):
-    blocks, (out, code, hits) = rest[:-3], rest[-3:]
-
-    def emit(rows, total):
-        out[rows, :] = price[rows, :] * jnp.exp(step_size * (total / capacity[rows, :] - 1.0))
-
-    every_sum(blocks, code, hits, out.shape[0] // T, emit)
-
-
-def last_price_kernel(price, capacity, *rest):
-    blocks, (out, code, hits, buf, sems) = rest[:-5], rest[-5:]
-    copies = []
-
-    def emit(rows, total):
-        buf[rows, :] = price[rows, :] * jnp.exp(step_size * (total / capacity[rows, :] - 1.0))
-        copies.append(pltpu.make_async_copy(buf.at[rows], out.at[rows], sems.at[len(copies)]))
-        copies[-1].start()
-
-    every_sum(blocks, code, hits, out.shape[0] // T, emit)
-    for c in copies:
-        c.wait()
-
-
-def prepare_kernel(
-    flow_in, link_in, class_in, table_in, access_in, price_in, capacity_in,
-    weight, own, access, price, capacity, sems, flow_at, link_at, flow_class, table,
-):
-    ends = (
-        (class_in, flow_class),
-        (table_in, table),
-        (flow_in, flow_at),
-        (link_in, link_at),
-        (access_in, access),
-        (price_in, price),
-        (capacity_in, capacity),
-    )
-    copies = [pltpu.make_async_copy(a, b, sems.at[i]) for i, (a, b) in enumerate(ends)]
-    for c in copies:
-        c.start()
-    for c in copies[:2]:
-        c.wait()
+def prepare_kernel(flow_at, link_at, flow_class, table, access, price, capacity, weight, own):
     low = jnp.broadcast_to(table[0:1, :], (8, T))
     high = jnp.broadcast_to(table[1:2, :], (8, T))
 
@@ -245,8 +244,6 @@
         return carry
 
     lax.fori_loop(0, flow_class.shape[0] // 8, look, 0, unroll=16)
-    for c in copies[2:]:
-        c.wait()
 
     def pick(s, carry):
         f = flow_at[0, s]
@@ -320,29 +317,53 @@
     access = access_price.reshape(flow_blocks, T)
     payload = pltpu.VMEM((PAYLOAD, T), jnp.int32)
 
-    def tile_call(body, own, tiles, blocks):
+    def early_call(blocks):
+        return pl.pallas_call(
+            early_kernel,
+            out_shape=pltpu.VMEM((S, T), f32),
+            in_specs=[VM] * (1 + len(blocks)),
+            out_specs=VM,
+            compiler_params=PARAMS,
+        )(in_vmem(index), *[in_vmem(x) for x in blocks])
+
+    def load_call(routes):
+        early = early_call([routes[0]] + routes[2:])
+        return tile_call(load_kernel, own, turned, [early], [routes[1]])
+
+    def tile_call(body, own, tiles, early, blocks):
         return pl.pallas_call(
             body,
             out_shape=payload,
-            in_specs=[VM] * (3 + len(blocks)),
+            in_specs=[VM] * (3 + len(early) + len(blocks)),
             out_specs=VM,
             scratch_shapes=[pltpu.VMEM((S, T), bf16), pltpu.VMEM((S, T), f32)],
             compiler_params=PARAMS,
-        )(in_vmem(index), in_vmem(own), in_vmem(tiles), *[in_vmem(x) for x in blocks])
-
-    def full_call(body, a, b, blocks, last):
+        )(in_vmem(index), in_vmem(own), in_vmem(tiles), *[in_vmem(x) for x in early + blocks])
+
+    def early_price_call(blocks):
+        pieces = sum(x.shape[0] for x in blocks)
+        return pl.pallas_call(
+            early_price_kernel,
+            out_shape=pltpu.VMEM(price.shape, f32),
+            in_specs=[VM] * len(blocks),
+            out_specs=VM,
+            scratch_shapes=[pltpu.VMEM((pieces * S, 2 * T), bf16), pltpu.VMEM((S, pieces * S), bf16)],
+            compiler_params=PARAMS,
+        )(*[in_vmem(x) for x in blocks])
+
+    def full_call(body, a, b, early, blocks, last):
         pieces = sum(x.shape[0] for x in blocks)
         scratch = [pltpu.VMEM((pieces * S, 2 * T), bf16), pltpu.VMEM((S, pieces * S), bf16)]
         if last:
-            scratch += [pltpu.VMEM(a.shape, f32), pltpu.SemaphoreType.DMA((a.shape[0] // T,))]
+            scratch += [pltpu.VMEM(a.shape, f32), pltpu.SemaphoreType.DMA((1 + a.shape[0] // T,))]
         return pl.pallas_call(
             body,
-            out_shape=pltpu.HBM(a.shape, f32) if last else pltpu.VMEM(a.shape, f32),
-            in_specs=[VM] * (2 + len(blocks)),
-            out_specs=HB if last else VM,
+            out_shape=tuple(pltpu.HBM(x.shape, f32) for x in (a, early[1])) if last else pltpu.VMEM(a.shape, f32),
+            in_specs=[VM] * (2 + len(early) + len(blocks)),
+            out_specs=(HB, HB) if last else VM,
             scratch_shapes=scratch,
             compiler_params=PARAMS,
-        )(in_vmem(a), in_vmem(b), *[in_vmem(x) for x in blocks])
+        )(in_vmem(a), in_vmem(b), *[in_vmem(x) for x in early + blocks])
 
     route_one, tiles, index = pl.pallas_call(
         first_route_kernel,
@@ -361,55 +382,43 @@
         compiler_params=PARAMS,
         name="first_route",
     )(tile_count, *[in_hbm(x) for x in (tile_flow, tile_link, price, route_tiles)])
-    turned = pl.pallas_call(
+    fetched = (
+        pltpu.SMEM((1, S), jnp.int32),
+        pltpu.SMEM((1, S), jnp.int32),
+        pltpu.VMEM((flow_blocks, T), jnp.int32),
+        pltpu.VMEM((2, T), f32),
+        pltpu.VMEM(access.shape, f32),
+        pltpu.VMEM(price.shape, f32),
+        pltpu.VMEM(cap.shape, f32),
+    )
+    sources = (tile_flow, tile_link, flow_class.reshape(flow_blocks, T), class_weight.reshape(2, T), access, price, cap)
+    turned, flow_at, link_at, *sources = pl.pallas_call(
         turn_kernel,
-        out_shape=pltpu.VMEM((S, T, T), bf16),
-        in_specs=[VM],
-        out_specs=VM,
+        out_shape=(pltpu.VMEM((S, T, T), bf16), *fetched),
+        in_specs=[VM] + [HB] * 7,
+        out_specs=(VM, SM, SM) + (VM,) * 5,
+        scratch_shapes=[pltpu.SemaphoreType.DMA((7,))],
         compiler_params=PARAMS,
         name="turn",
-    )(in_vmem(tiles))
-    full = (access.shape, price.shape, cap.shape)
-    weight, own, access, price, cap = pl.pallas_call(
+    )(in_vmem(tiles), *[in_hbm(x) for x in sources])
+    access, price, cap = sources[2:]
+    weight, own = pl.pallas_call(
         prepare_kernel,
-        out_shape=(
-            pltpu.VMEM((flow_blocks, T), f32),
-            pltpu.VMEM((4, S, T), f32),
-            *[pltpu.VMEM(shape, f32) for shape in full],
-        ),
-        in_specs=[HB] * 7,
-        out_specs=(VM,) * 5,
-        scratch_shapes=[
-            pltpu.SemaphoreType.DMA((7,)),
-            pltpu.SMEM((1, S), jnp.int32),
-            pltpu.SMEM((1, S), jnp.int32),
-            pltpu.VMEM((flow_blocks, T), jnp.int32),
-            pltpu.VMEM((2, T), f32),
-        ],
+        out_shape=(pltpu.VMEM((flow_blocks, T), f32), pltpu.VMEM((4, S, T), f32)),
+        in_specs=[SM, SM] + [VM] * 5,
+        out_specs=(VM, VM),
         compiler_params=PARAMS,
         name="prepare",
-    )(
-        *[
-            in_hbm(x)
-            for x in (
-                tile_flow,
-                tile_link,
-                flow_class.reshape(flow_blocks, T),
-                class_weight.reshape(2, T),
-                access,
-                price,
-                cap,
-            )
-        ]
-    )
+    )(flow_at, link_at, *[in_vmem(x) for x in sources])
 
     routes = gather_link(route_one)
-    loads = gather_flow(tile_call(load_kernel, own, turned, routes))
-    price_one = full_call(first_price_kernel, price, cap, loads, False)
-    routes = gather_link(tile_call(route_kernel, own, tiles, loads))
-    rate = full_call(rate_kernel, weight, access, routes, True)
-    loads = gather_flow(tile_call(load_kernel, own, turned, routes))
-    price_two = full_call(last_price_kernel, price_one, cap, loads, True)
+    loads = gather_flow(load_call(routes))
+    price_one = full_call(first_price_kernel, price, cap, [], loads, False)
+    routes = gather_link(tile_call(route_kernel, own, tiles, [], loads))
+    rate = full_call(rate_kernel, weight, access, [], routes, False)
+    loads = gather_flow(load_call(routes))
+    early = early_price_call(loads[:1])
+    price_two, rate = full_call(last_price_kernel, price_one, cap, [early, rate], loads[1:], True)
     return (rate.reshape(-1), price_two.reshape(-1))
 
 

time: 65 us -> 65.3 us (level)
  waiting for transfers between devices: 24.2 us -> 26.7 us
  Pallas kernels: 15 us -> 13.2 us
  starting transfers between devices: 23.2 us -> 22.5 us
    ppermute x24, waiting for transfers between devices: 24.2 us -> 26.7 us  [send(): return lax.ppermute(x, ('flow', 'link'), perm)]
    pallas_call x1, Pallas kernels: 2.58 us -> 1.45 us  [on_device(): pl.pallas_call(prepare_kernel, out_shape=(pltpu.VMEM((flow_blocks, T), f3...]
    ppermute x24, starting transfers between devices: 23.2 us -> 22.5 us  [send(): return lax.ppermute(x, ('flow', 'link'), perm)]
    pallas_call x7 -> x10, Pallas kernels: 9.01 us -> 8.83 us  [the longest x3 3.21 us: full_call(): pl.pallas_call(body, out_shape=tuple((pltpu.HBM(x.shape, f32) for x in (a...]
  transfers between devices with their start and end apart: 24 -> 24, of which waited for: 14 -> 16; matrix products, arithmetic and copies ran while one was open for 0% -> 0% of each run, Pallas kernels for 10% -> 10%
where the time goes in v2:
time: 65.3 us; the launch traced here: 64 us
  waiting for transfers between devices  26.7 us (41%)
  starting transfers between devices  22.5 us (34%)
  Pallas kernels  13.2 us (20%)
  between operations  1.56 us (2%)
    ppermute x24, waiting for transfers between devices, send(): return lax.ppermute(x, ('flow', 'link'), perm)  26.7 us
    ppermute x24, starting transfers between devices, send(): return lax.ppermute(x, ('flow', 'link'), perm)  22.5 us
    pallas_call x3, Pallas kernels, full_call(): pl.pallas_call(body, out_shape=tuple((pltpu.HBM(x.shape, f32) for x in (a...  3.21 us
    pallas_call x3, Pallas kernels, tile_call(): pl.pallas_call(body, out_shape=payload, in_specs=[VM] * (3 + len(early) +...  3.13 us
    pallas_call x1, Pallas kernels, on_device(): pl.pallas_call(first_route_kernel, out_shape=(payload, pltpu.VMEM((S, T,...  2.9 us
    pallas_call x1, Pallas kernels, on_device(): pl.pallas_call(prepare_kernel, out_shape=(pltpu.VMEM((flow_blocks, T), f3...  1.45 us
    pallas_call x1, Pallas kernels, on_device(): pl.pallas_call(turn_kernel, out_shape=(pltpu.VMEM((S, T, T), bf16), *fetc...  1.42 us
  transfers between devices with their start and end apart: 24, of which 16 were waited for; matrix products, arithmetic and copies ran while one was open for 0% of the time, Pallas kernels for 10%

profile of v2, /device:TPU:0, one launch (start us, length us, event | category | flops | bytes accessed | tf_op | source)
XLA Modules:
  0.0 64.0 jit_solution(6685637045651984128)
XLA Ops:
  1.3 2.9 %first_route.1 = (s32[72,128]{1,0:T(8,128)S(1)}, bf16[128,128,128]{2,1,0:T(8,128)(2,1)S(1)}, s32[264,128]{1,0:T(8,128)S(1)}) custom-call(s32[1,1]{1,0:T(1,128)S(6)} %copy.11.count, s32[1,128]{1,0:T(1,128)} %rest_0_.1, s32[1,128]{1,0:T(1,128)} %rest_1_.1, f32[512,128]{1,0:T(8,128)} %bitcast.25, bf16[128,128,128]{2,1,0:T(8,128)(2,1)} %tiles.1), custom_call_target="tpu_custom_call" | custom-call | tf_op jit(solution)/shard_map/first_route/pallas_call | solution.py:368
  4.2 2.6 %collective-permute-start.3 = (s32[72,128]{1,0:T(8,128)S(1)}, s32[72,128]{1,0:T(8,128)S(1)}, u32[]{:S(2)}, u32[]{:S(2)}) collective-permute-start(s32[72,128]{1,0:T(8,128)S(1)} %get-tuple-element.28), channel_id=1, source_target_pairs={{0,24},{1,25},{2,26},{3,27},{4,28},{5,29},{6,30},{7,31},{8,16},{9,... | collective-permute-start | bytes 110600 | tf_op jit(solution)/shard_map/ppermute | solution.py:281
  6.8 3.9 %collective-permute-start.2 = (s32[72,128]{1,0:T(8,128)S(1)}, s32[72,128]{1,0:T(8,128)S(1)}, u32[]{:S(2)}, u32[]{:S(2)}) collective-permute-start(s32[72,128]{1,0:T(8,128)S(1)} %get-tuple-element.28), channel_id=1, source_target_pairs={{0,28},{1,29},{2,30},{3,31},{4,16},{5,17},{6,18},{7,19},{8,20},{9,... | collective-permute-start | bytes 110600 | tf_op jit(solution)/shard_map/ppermute | solution.py:281
  12.4 3.0 %collective-permute-done.1 = s32[72,128]{1,0:T(8,128)S(1)} collective-permute-done((s32[72,128]{1,0:T(8,128)S(1)}, s32[72,128]{1,0:T(8,128)S(1)}, u32[]{:S(2)}, u32[]{:S(2)}) %collective-permute-start.1) | collective-permute-done | bytes 36896 | tf_op jit(solution)/shard_map/ppermute | solution.py:281
  17.1 1.4 %turn.1 = (bf16[128,128,128]{2,1,0:T(8,128)(2,1)S(1)}, s32[1,128]{1,0:T(1,128)S(4)}, s32[1,128]{1,0:T(1,128)S(4)}, s32[1024,128]{1,0:T(8,128)S(1)}, f32[2,128]{1...) custom-call(bf16[128,128,128]{2,1,0:T(8,128)(2,1)S(1)} %get-tuple-element.17.tiles, ...), custom_call_target="tpu_custom_call" | custom-call | tf_op jit(solution)/shard_map/turn/pallas_call | solution.py:395
  18.5 1.4 %prepare.1 = (f32[1024,128]{1,0:T(8,128)S(1)}, f32[4,128,128]{2,1,0:T(8,128)S(1)}) custom-call(s32[1,128]{1,0:T(1,128)S(4)} %get-tuple-element.21.flow_at, s32[1,128]{1,0:T(1,128)S(4)} %get-tuple-element.22.link_at, s32[1024,128]{1,0:T(8,128)S(1)} %get-tuple-element.23.flow_class, f32[2,128]{1,0:T(2,128)S(1)} %get-tuple-element.24.table, ...), custom_call_target="tpu_custom_call" | custom-call | tf_op jit(solution)/shard_map/prepare/pallas_call | solution.py:405
  20.2 2.3 %collective-permute-done.6.rest_2_ = s32[4,72,128]{2,1,0:T(8,128)S(1)} collective-permute-done((s32[4,72,128]{2,1,0:T(8,128)S(1)}, s32[4,72,128]{2,1,0:T(8,128)S(1)}, u32[]{:S(2)}, u32[]{:S(2)}) %collective-permute-start.6) | collective-permute-done | bytes 147488 | tf_op jit(solution)/shard_map/ppermute | solution.py:281
  24.8 3.0 %collective-permute-start.10 = (s32[72,128]{1,0:T(8,128)S(1)}, s32[72,128]{1,0:T(8,128)S(1)}, u32[]{:S(2)}, u32[]{:S(2)}) collective-permute-start(s32[72,128]{1,0:T(8,128)S(1)} %shard_map.105), channel_id=1, source_target_pairs={{0,80},{1,81},{2,82},{3,83},{4,84},{5,85},{6,86},{7,87},{8,88},{9,... | collective-permute-start | bytes 110600 | tf_op jit(solution)/shard_map/ppermute | solution.py:281
  29.8 1.3 %collective-permute-done.9 = s32[72,128]{1,0:T(8,128)S(1)} collective-permute-done((s32[72,128]{1,0:T(8,128)S(1)}, s32[72,128]{1,0:T(8,128)S(1)}, u32[]{:S(2)}, u32[]{:S(2)}) %collective-permute-start.9) | collective-permute-done | bytes 36896 | tf_op jit(solution)/shard_map/ppermute | solution.py:281
  31.1 2.4 %collective-permute-done.8 = s32[72,128]{1,0:T(8,128)S(1)} collective-permute-done((s32[72,128]{1,0:T(8,128)S(1)}, s32[72,128]{1,0:T(8,128)S(1)}, u32[]{:S(2)}, u32[]{:S(2)}) %collective-permute-start.8) | collective-permute-done | bytes 36896 | tf_op jit(solution)/shard_map/ppermute | solution.py:281
  33.7 1.3 %collective-permute-done.11.rest_1_ = s32[4,72,128]{2,1,0:T(8,128)S(1)} collective-permute-done((s32[4,72,128]{2,1,0:T(8,128)S(1)}, s32[4,72,128]{2,1,0:T(8,128)S(1)}, u32[]{:S(2)}, u32[]{:S(2)}) %collective-permute-start.11) | collective-permute-done | bytes 147488 | tf_op jit(solution)/shard_map/ppermute | solution.py:281
  35.0 1.1 %shard_map.107 = s32[72,128]{1,0:T(8,128)S(1)} custom-call(s32[264,128]{1,0:T(8,128)S(1)} %get-tuple-element.20.index, f32[4,128,128]{2,1,0:T(8,128)S(1)} %get-tuple-element.26.own, bf16[128,128,128]{2,1,0:T(8,128)(2,1)S(1)} %get-tuple-element.17.tiles, s32[4,72,128]{2,1,0:T(8,128)S(1)} %pad_add_fusion.1.rest_0_, ...), custom_call_target="tpu_custom_call" | custom-call | tf_op jit(solution)/shard_map/pallas_call | solution.py:334
  37.1 1.1 %collective-permute-start.14 = (s32[72,128]{1,0:T(8,128)S(1)}, s32[72,128]{1,0:T(8,128)S(1)}, u32[]{:S(2)}, u32[]{:S(2)}) collective-permute-start(s32[72,128]{1,0:T(8,128)S(1)} %shard_map.107), channel_id=1, source_target_pairs={{0,28},{1,29},{2,30},{3,31},{4,16},{5,17},{6,18},{7,19},{8,20},{9,... | collective-permute-start | bytes 110600 | tf_op jit(solution)/shard_map/ppermute | solution.py:281
  38.6 2.4 %collective-permute-done.15 = s32[72,128]{1,0:T(8,128)S(1)} collective-permute-done((s32[72,128]{1,0:T(8,128)S(1)}, s32[72,128]{1,0:T(8,128)S(1)}, u32[]{:S(2)}, u32[]{:S(2)}) %collective-permute-start.15) | collective-permute-done | bytes 36896 | tf_op jit(solution)/shard_map/ppermute | solution.py:281
  41.0 1.8 %collective-permute-done.13 = s32[72,128]{1,0:T(8,128)S(1)} collective-permute-done((s32[72,128]{1,0:T(8,128)S(1)}, s32[72,128]{1,0:T(8,128)S(1)}, u32[]{:S(2)}, u32[]{:S(2)}) %collective-permute-start.13) | collective-permute-done | bytes 36896 | tf_op jit(solution)/shard_map/ppermute | solution.py:281
  43.0 1.4 %collective-permute-start.17 = (s32[4,72,128]{2,1,0:T(8,128)S(1)}, s32[4,72,128]{2,1,0:T(8,128)S(1)}, u32[]{:S(2)}, u32[]{:S(2)}) collective-permute-start(s32[4,72,128]{2,1,0:T(8,128)S(1)} %pad_add_fusion.2), channel_id=1, source_target_pairs={{0,28},{1,29},{2,30},{3,31},{4,16},{5,17},{6,18},{7,19},{8,20},{9,... | collective-permute-start | bytes 442376 | tf_op jit(solution)/shard_map/ppermute | solution.py:281
  46.0 1.7 %collective-permute-done.17.rest_1_.rest_2_ = s32[4,72,128]{2,1,0:T(8,128)S(1)} collective-permute-done((s32[4,72,128]{2,1,0:T(8,128)S(1)}, s32[4,72,128]{2,1,0:T(8,128)S(1)}, u32[]{:S(2)}, u32[]{:S(2)}) %collective-permute-start.17) | collective-permute-done | bytes 147488 | tf_op jit(solution)/shard_map/ppermute | solution.py:281
  47.6 3.0 %collective-permute-done.18.rest_2_.rest_3_ = s32[4,72,128]{2,1,0:T(8,128)S(1)} collective-permute-done((s32[4,72,128]{2,1,0:T(8,128)S(1)}, s32[4,72,128]{2,1,0:T(8,128)S(1)}, u32[]{:S(2)}, u32[]{:S(2)}) %collective-permute-start.18) | collective-permute-done | bytes 147488 | tf_op jit(solution)/shard_map/ppermute | solution.py:281
  51.0 1.1 %collective-permute-done.19.rest_0_.rest_1_ = s32[4,72,128]{2,1,0:T(8,128)S(1)} collective-permute-done((s32[4,72,128]{2,1,0:T(8,128)S(1)}, s32[4,72,128]{2,1,0:T(8,128)S(1)}, u32[]{:S(2)}, u32[]{:S(2)}) %collective-permute-start.19) | collective-permute-done | bytes 147488 | tf_op jit(solution)/shard_map/ppermute | solution.py:281
  53.6 1.7 %collective-permute-start.21 = (s32[72,128]{1,0:T(8,128)S(1)}, s32[72,128]{1,0:T(8,128)S(1)}, u32[]{:S(2)}, u32[]{:S(2)}) collective-permute-start(s32[72,128]{1,0:T(8,128)S(1)} %shard_map.109), channel_id=1, source_target_pairs={{0,112},{1,113},{2,114},{3,115},{4,116},{5,117},{6,118},{7,119},{8... | collective-permute-start | bytes 110600 | tf_op jit(solution)/shard_map/ppermute | solution.py:281
  55.4 2.6 %collective-permute-done.22 = s32[72,128]{1,0:T(8,128)S(1)} collective-permute-done((s32[72,128]{1,0:T(8,128)S(1)}, s32[72,128]{1,0:T(8,128)S(1)}, u32[]{:S(2)}, u32[]{:S(2)}) %collective-permute-start.22) | collective-permute-done | bytes 36896 | tf_op jit(solution)/shard_map/ppermute | solution.py:281
  58.0 1.9 %collective-permute-done.20 = s32[72,128]{1,0:T(8,128)S(1)} collective-permute-done((s32[72,128]{1,0:T(8,128)S(1)}, s32[72,128]{1,0:T(8,128)S(1)}, u32[]{:S(2)}, u32[]{:S(2)}) %collective-permute-start.20) | collective-permute-done | bytes 36896 | tf_op jit(solution)/shard_map/ppermute | solution.py:281
  60.8 1.6 %shard_map.111.rate = f32[1024,128]{1,0:T(8,128)S(1)} custom-call(f32[1024,128]{1,0:T(8,128)S(1)} %get-tuple-element.29.weight, f32[1024,128]{1,0:T(8,128)S(1)} %get-tuple-element.25.access, s32[4,72,128]{2,1,0:T(8,128)S(1)} %collective-permute-done.16.rest_0_, s32[4,72,128]{2,1,0:T(8,128)S(1)} %collective-permute-done.19.rest_0_.rest_1_, ...), custom_call_target="tpu_custom_call" | custom-call | tf_op jit(solution)/shard_map/pallas_call | solution.py:359
  62.8 1.1 %shard_map.112 = (f32[512,128]{1,0:T(8,128)}, f32[1024,128]{1,0:T(8,128)}) custom-call(f32[512,128]{1,0:T(8,128)S(1)} %shard_map.106.price, f32[512,128]{1,0:T(8,128)S(1)} %get-tuple-element.19.capacity, f32[512,128]{1,0:T(8,128)S(1)} %shard_map.110.early, f32[1024,128]{1,0:T(8,128)S(1)} %shard_map.111.rate, s32[4,72,128]{2,1,0:T(8,128)S(1)} %collective-permute-done.23.rest_0_), custom_call_target="tpu_custom_call" | custom-call | tf_op jit(solution)/shard_map/pallas_call | solution.py:359
  (40 shorter events, 14.5 us)
Async XLA Ops:
  4.2 7.7 %collective-permute-start.3 = (s32[72,128]{1,0:T(8,128)S(1)}, s32[72,128]{1,0:T(8,128)S(1)}, u32[]{:S(2)}, u32[]{:S(2)}) collective-permute-start(s32[72,128]{1,0:T(8,128)S(1)} %get-tuple-element.28), channel_id=1, source_target_pairs={{0,24},{1,25},{2,26},{3,27},{4,28},{5,29},{6,30},{7,31},{8,16},{9,... | collective-permute-start | bytes 110600 | tf_op jit(solution)/shard_map/ppermute | solution.py:281
  6.8 5.5 %collective-permute-start.2 = (s32[72,128]{1,0:T(8,128)S(1)}, s32[72,128]{1,0:T(8,128)S(1)}, u32[]{:S(2)}, u32[]{:S(2)}) collective-permute-start(s32[72,128]{1,0:T(8,128)S(1)} %get-tuple-element.28), channel_id=1, source_target_pairs={{0,28},{1,29},{2,30},{3,31},{4,16},{5,17},{6,18},{7,19},{8,20},{9,... | collective-permute-start | bytes 110600 | tf_op jit(solution)/shard_map/ppermute | solution.py:281
  10.7 4.6 %collective-permute-start.1 = (s32[72,128]{1,0:T(8,128)S(1)}, s32[72,128]{1,0:T(8,128)S(1)}, u32[]{:S(2)}, u32[]{:S(2)}) collective-permute-start(s32[72,128]{1,0:T(8,128)S(1)} %get-tuple-element.28), channel_id=1, source_target_pairs={{0,20},{1,21},{2,22},{3,23},{4,24},{5,25},{6,26},{7,27},{8,28},{9,... | collective-permute-start | bytes 110600 | tf_op jit(solution)/shard_map/ppermute | solution.py:281
  11.2 4.1 %collective-permute-start = (s32[72,128]{1,0:T(8,128)S(1)}, s32[72,128]{1,0:T(8,128)S(1)}, u32[]{:S(2)}, u32[]{:S(2)}) collective-permute-start(s32[72,128]{1,0:T(8,128)S(1)} %get-tuple-element.28), channel_id=1, source_target_pairs={{0,16},{1,17},{2,18},{3,19},{4,20},{5,21},{6,22},{7,23},{8,24},{9,... | collective-permute-start | bytes 110600 | tf_op jit(solution)/shard_map/ppermute | solution.py:281
  15.3 4.6 %collective-permute-start.4 = (s32[4,72,128]{2,1,0:T(8,128)S(1)}, s32[4,72,128]{2,1,0:T(8,128)S(1)}, u32[]{:S(2)}, u32[]{:S(2)}) collective-permute-start(s32[4,72,128]{2,1,0:T(8,128)S(1)} %pad_add_fusion), channel_id=1, source_target_pairs={{0,16},{1,17},{2,18},{3,19},{4,20},{5,21},{6,22},{7,23},{8,24},{9,... | collective-permute-start | bytes 442376 | tf_op jit(solution)/shard_map/ppermute | solution.py:281
  15.7 4.6 %collective-permute-start.5 = (s32[4,72,128]{2,1,0:T(8,128)S(1)}, s32[4,72,128]{2,1,0:T(8,128)S(1)}, u32[]{:S(2)}, u32[]{:S(2)}) collective-permute-start(s32[4,72,128]{2,1,0:T(8,128)S(1)} %pad_add_fusion), channel_id=1, source_target_pairs={{0,28},{1,29},{2,30},{3,31},{4,16},{5,17},{6,18},{7,19},{8,20},{9,... | collective-permute-start | bytes 442376 | tf_op jit(solution)/shard_map/ppermute | solution.py:281
  16.4 6.2 %collective-permute-start.6 = (s32[4,72,128]{2,1,0:T(8,128)S(1)}, s32[4,72,128]{2,1,0:T(8,128)S(1)}, u32[]{:S(2)}, u32[]{:S(2)}) collective-permute-start(s32[4,72,128]{2,1,0:T(8,128)S(1)} %pad_add_fusion), channel_id=1, source_target_pairs={{0,24},{1,25},{2,26},{3,27},{4,28},{5,29},{6,30},{7,31},{8,16},{9,... | collective-permute-start | bytes 442376 | tf_op jit(solution)/shard_map/ppermute | solution.py:281
  16.4 7.4 %collective-permute-start.7 = (s32[4,72,128]{2,1,0:T(8,128)S(1)}, s32[4,72,128]{2,1,0:T(8,128)S(1)}, u32[]{:S(2)}, u32[]{:S(2)}) collective-permute-start(s32[4,72,128]{2,1,0:T(8,128)S(1)} %pad_add_fusion), channel_id=1, source_target_pairs={{0,20},{1,21},{2,22},{3,23},{4,24},{5,25},{6,26},{7,27},{8,28},{9,... | collective-permute-start | bytes 442376 | tf_op jit(solution)/shard_map/ppermute | solution.py:281
  24.8 5.0 %collective-permute-start.10 = (s32[72,128]{1,0:T(8,128)S(1)}, s32[72,128]{1,0:T(8,128)S(1)}, u32[]{:S(2)}, u32[]{:S(2)}) collective-permute-start(s32[72,128]{1,0:T(8,128)S(1)} %shard_map.105), channel_id=1, source_target_pairs={{0,80},{1,81},{2,82},{3,83},{4,84},{5,85},{6,86},{7,87},{8,88},{9,... | collective-permute-start | bytes 110600 | tf_op jit(solution)/shard_map/ppermute | solution.py:281
  27.7 3.4 %collective-permute-start.9 = (s32[72,128]{1,0:T(8,128)S(1)}, s32[72,128]{1,0:T(8,128)S(1)}, u32[]{:S(2)}, u32[]{:S(2)}) collective-permute-start(s32[72,128]{1,0:T(8,128)S(1)} %shard_map.105), channel_id=1, source_target_pairs={{0,112},{1,113},{2,114},{3,115},{4,116},{5,117},{6,118},{7,119},{8... | collective-permute-start | bytes 110600 | tf_op jit(solution)/shard_map/ppermute | solution.py:281
  28.8 4.7 %collective-permute-start.8 = (s32[72,128]{1,0:T(8,128)S(1)}, s32[72,128]{1,0:T(8,128)S(1)}, u32[]{:S(2)}, u32[]{:S(2)}) collective-permute-start(s32[72,128]{1,0:T(8,128)S(1)} %shard_map.105), channel_id=1, source_target_pairs={{0,48},{1,49},{2,50},{3,51},{4,52},{5,53},{6,54},{7,55},{8,56},{9,... | collective-permute-start | bytes 110600 | tf_op jit(solution)/shard_map/ppermute | solution.py:281
  33.5 1.4 %collective-permute-start.11 = (s32[4,72,128]{2,1,0:T(8,128)S(1)}, s32[4,72,128]{2,1,0:T(8,128)S(1)}, u32[]{:S(2)}, u32[]{:S(2)}) collective-permute-start(s32[4,72,128]{2,1,0:T(8,128)S(1)} %pad_add_fusion.1.rest_0_), channel_id=1, source_target_pairs={{0,16},{1,17},{2,18},{3,19},{4,20},{5,21},{6,22},{7,23},{8,24},{9,... | collective-permute-start | bytes 442376 | tf_op jit(solution)/shard_map/ppermute | solution.py:281
  36.1 4.9 %collective-permute-start.15 = (s32[72,128]{1,0:T(8,128)S(1)}, s32[72,128]{1,0:T(8,128)S(1)}, u32[]{:S(2)}, u32[]{:S(2)}) collective-permute-start(s32[72,128]{1,0:T(8,128)S(1)} %shard_map.107), channel_id=1, source_target_pairs={{0,24},{1,25},{2,26},{3,27},{4,28},{5,29},{6,30},{7,31},{8,16},{9,... | collective-permute-start | bytes 110600 | tf_op jit(solution)/shard_map/ppermute | solution.py:281
  37.1 3.9 %collective-permute-start.14 = (s32[72,128]{1,0:T(8,128)S(1)}, s32[72,128]{1,0:T(8,128)S(1)}, u32[]{:S(2)}, u32[]{:S(2)}) collective-permute-start(s32[72,128]{1,0:T(8,128)S(1)} %shard_map.107), channel_id=1, source_target_pairs={{0,28},{1,29},{2,30},{3,31},{4,16},{5,17},{6,18},{7,19},{8,20},{9,... | collective-permute-start | bytes 110600 | tf_op jit(solution)/shard_map/ppermute | solution.py:281
  38.3 4.6 %collective-permute-start.13 = (s32[72,128]{1,0:T(8,128)S(1)}, s32[72,128]{1,0:T(8,128)S(1)}, u32[]{:S(2)}, u32[]{:S(2)}) collective-permute-start(s32[72,128]{1,0:T(8,128)S(1)} %shard_map.107), channel_id=1, source_target_pairs={{0,20},{1,21},{2,22},{3,23},{4,24},{5,25},{6,26},{7,27},{8,28},{9,... | collective-permute-start | bytes 110600 | tf_op jit(solution)/shard_map/ppermute | solution.py:281
  38.3 4.6 %collective-permute-start.12 = (s32[72,128]{1,0:T(8,128)S(1)}, s32[72,128]{1,0:T(8,128)S(1)}, u32[]{:S(2)}, u32[]{:S(2)}) collective-permute-start(s32[72,128]{1,0:T(8,128)S(1)} %shard_map.107), channel_id=1, source_target_pairs={{0,16},{1,17},{2,18},{3,19},{4,20},{5,21},{6,22},{7,23},{8,24},{9,... | collective-permute-start | bytes 110600 | tf_op jit(solution)/shard_map/ppermute | solution.py:281
  42.9 3.1 %collective-permute-start.16 = (s32[4,72,128]{2,1,0:T(8,128)S(1)}, s32[4,72,128]{2,1,0:T(8,128)S(1)}, u32[]{:S(2)}, u32[]{:S(2)}) collective-permute-start(s32[4,72,128]{2,1,0:T(8,128)S(1)} %pad_add_fusion.2), channel_id=1, source_target_pairs={{0,16},{1,17},{2,18},{3,19},{4,20},{5,21},{6,22},{7,23},{8,24},{9,... | collective-permute-start | bytes 442376 | tf_op jit(solution)/shard_map/ppermute | solution.py:281
  43.0 4.6 %collective-permute-start.17 = (s32[4,72,128]{2,1,0:T(8,128)S(1)}, s32[4,72,128]{2,1,0:T(8,128)S(1)}, u32[]{:S(2)}, u32[]{:S(2)}) collective-permute-start(s32[4,72,128]{2,1,0:T(8,128)S(1)} %pad_add_fusion.2), channel_id=1, source_target_pairs={{0,28},{1,29},{2,30},{3,31},{4,16},{5,17},{6,18},{7,19},{8,20},{9,... | collective-permute-start | bytes 442376 | tf_op jit(solution)/shard_map/ppermute | solution.py:281
  44.4 6.2 %collective-permute-start.18 = (s32[4,72,128]{2,1,0:T(8,128)S(1)}, s32[4,72,128]{2,1,0:T(8,128)S(1)}, u32[]{:S(2)}, u32[]{:S(2)}) collective-permute-start(s32[4,72,128]{2,1,0:T(8,128)S(1)} %pad_add_fusion.2), channel_id=1, source_target_pairs={{0,24},{1,25},{2,26},{3,27},{4,28},{5,29},{6,30},{7,31},{8,16},{9,... | collective-permute-start | bytes 442376 | tf_op jit(solution)/shard_map/ppermute | solution.py:281
  45.1 6.9 %collective-permute-start.19 = (s32[4,72,128]{2,1,0:T(8,128)S(1)}, s32[4,72,128]{2,1,0:T(8,128)S(1)}, u32[]{:S(2)}, u32[]{:S(2)}) collective-permute-start(s32[4,72,128]{2,1,0:T(8,128)S(1)} %pad_add_fusion.2), channel_id=1, source_target_pairs={{0,20},{1,21},{2,22},{3,23},{4,24},{5,25},{6,26},{7,27},{8,28},{9,... | collective-permute-start | bytes 442376 | tf_op jit(solution)/shard_map/ppermute | solution.py:281
  53.1 4.9 %collective-permute-start.22 = (s32[72,128]{1,0:T(8,128)S(1)}, s32[72,128]{1,0:T(8,128)S(1)}, u32[]{:S(2)}, u32[]{:S(2)}) collective-permute-start(s32[72,128]{1,0:T(8,128)S(1)} %shard_map.109), channel_id=1, source_target_pairs={{0,80},{1,81},{2,82},{3,83},{4,84},{5,85},{6,86},{7,87},{8,88},{9,... | collective-permute-start | bytes 110600 | tf_op jit(solution)/shard_map/ppermute | solution.py:281
  53.6 4.4 %collective-permute-start.21 = (s32[72,128]{1,0:T(8,128)S(1)}, s32[72,128]{1,0:T(8,128)S(1)}, u32[]{:S(2)}, u32[]{:S(2)}) collective-permute-start(s32[72,128]{1,0:T(8,128)S(1)} %shard_map.109), channel_id=1, source_target_pairs={{0,112},{1,113},{2,114},{3,115},{4,116},{5,117},{6,118},{7,119},{8... | collective-permute-start | bytes 110600 | tf_op jit(solution)/shard_map/ppermute | solution.py:281
  55.3 4.6 %collective-permute-start.20 = (s32[72,128]{1,0:T(8,128)S(1)}, s32[72,128]{1,0:T(8,128)S(1)}, u32[]{:S(2)}, u32[]{:S(2)}) collective-permute-start(s32[72,128]{1,0:T(8,128)S(1)} %shard_map.109), channel_id=1, source_target_pairs={{0,48},{1,49},{2,50},{3,51},{4,52},{5,53},{6,54},{7,55},{8,56},{9,... | collective-permute-start | bytes 110600 | tf_op jit(solution)/shard_map/ppermute | solution.py:281
  59.9 2.9 %collective-permute-start.23 = (s32[4,72,128]{2,1,0:T(8,128)S(1)}, s32[4,72,128]{2,1,0:T(8,128)S(1)}, u32[]{:S(2)}, u32[]{:S(2)}) collective-permute-start(s32[4,72,128]{2,1,0:T(8,128)S(1)} %pad_add_fusion.3.rest_0_), channel_id=1, source_target_pairs={{0,16},{1,17},{2,18},{3,19},{4,20},{5,21},{6,22},{7,23},{8,24},{9,... | collective-permute-start | bytes 442376 | tf_op jit(solution)/shard_map/ppermute | solution.py:281

commit v3 on v2

--- a/solution.py
+++ b/solution.py
@@ -18,6 +18,7 @@
 PAYLOAD = HALF + 8
 INDEX = HALF
 EXPONENT = HALF + 1
+PIECES = 4
 GROUP = 16
 CHUNKS = S // GROUP
 FETCH = 64
@@ -71,15 +72,40 @@
 def matched_sum(column, blocks, codes):
     hits = []
     for ref in blocks:
-        for k in range(ref.shape[0]):
-            scale = jnp.exp2((ref[k, EXPONENT : EXPONENT + 1, :] - 16).astype(f32))
-            hits.append(jnp.where(column == ref[k, INDEX:EXPONENT, :], scale, 0.0).astype(bf16))
+        for k in range(PIECES):
+            index, scale = index_and_scale(ref, k)
+            hits.append(jnp.where(column == index, scale, 0.0).astype(bf16))
     both = dot(jnp.concatenate(hits, axis=1), codes)
     return both[:, :T] + both[:, T:]
 
 
 def decode(blocks):
-    return jnp.concatenate([decoded(ref[k, :HALF, :]) for ref in blocks for k in range(ref.shape[0])], axis=0)
+    words = [ref[k * HALF : (k + 1) * HALF, :] for ref in blocks for k in range(PIECES)]
+    return jnp.concatenate([decoded(w) for w in words], axis=0)
+
+
+def index_and_scale(ref, k):
+    at = PIECES * HALF + 2 * k
+    return ref[at : at + 1, :], jnp.exp2((ref[at + 1 : at + 2, :] - 16).astype(f32))
+
+
+def join_kernel(*refs):
+    payloads, out = refs[:-1], refs[-1]
+    for k, p in enumerate(payloads):
+        out[k * HALF : (k + 1) * HALF, :] = p[:HALF, :]
+        at = PIECES * HALF + 2 * k
+        out[at : at + 2, :] = p[INDEX : EXPONENT + 1, :]
+
+
+def gathered(payloads):
+    return pl.pallas_call(
+        join_kernel,
+        out_shape=pltpu.VMEM((PIECES * HALF + 2 * PIECES, T), jnp.int32),
+        in_specs=[VM] * PIECES,
+        out_specs=VM,
+        compiler_params=PARAMS,
+        name="join",
+    )(*[in_vmem(p) for p in payloads])
 
 
 def own_slots():
@@ -182,12 +208,12 @@
     rows = lax.broadcasted_iota(jnp.int32, (S, T), 0)
     chunk, scale = [], []
     for ref in blocks:
-        for k in range(ref.shape[0]):
-            index = ref[k, INDEX:EXPONENT, :]
+        for k in range(PIECES):
+            index, factor = index_and_scale(ref, k)
             at = slice(len(chunk) * T, (len(chunk) + 1) * T)
             hits[:, at] = jnp.where(rows == (index & (T - 1)), 1.0, 0.0).astype(bf16)
             chunk.append(index >> 7)
-            scale.append(jnp.exp2((ref[k, EXPONENT : EXPONENT + 1, :] - 16).astype(f32)))
+            scale.append(factor)
     chunk = jnp.concatenate(chunk, axis=1)
     scale = jnp.concatenate(scale, axis=1)
     for c in range(n):
@@ -285,7 +311,7 @@
     near, far = [send(x, PARTNER)], []
     for p in FIRST:
         near.append(send(x, p))
-    near = jnp.stack(near)
+    near = gathered(near)
     for p in SECOND:
         far.append(send(near, p))
     return [send(near, PARTNER)] + far
@@ -295,7 +321,7 @@
     near = [x]
     for p in ALONG_Y:
         near.append(send(x, p))
-    near = jnp.stack(near)
+    near = gathered(near)
     return [near, send(near, PARTNER)]
 
 
@@ -341,7 +367,7 @@
         )(in_vmem(index), in_vmem(own), in_vmem(tiles), *[in_vmem(x) for x in early + blocks])
 
     def early_price_call(blocks):
-        pieces = sum(x.shape[0] for x in blocks)
+        pieces = PIECES * len(blocks)
         return pl.pallas_call(
             early_price_kernel,
             out_shape=pltpu.VMEM(price.shape, f32),
@@ -352,7 +378,7 @@
         )(*[in_vmem(x) for x in blocks])
 
     def full_call(body, a, b, early, blocks, last):
-        pieces = sum(x.shape[0] for x in blocks)
+        pieces = PIECES * len(blocks)
         scratch = [pltpu.VMEM((pieces * S, 2 * T), bf16), pltpu.VMEM((S, pieces * S), bf16)]
         if last:
             scratch += [pltpu.VMEM(a.shape, f32), pltpu.SemaphoreType.DMA((1 + a.shape[0] // T,))]

time: 65.3 us -> 66.6 us (1.020)
  starting transfers between devices: 22.5 us -> 30.3 us
  waiting for transfers between devices: 26.7 us -> 20.5 us
    ppermute x24, starting transfers between devices: 22.5 us -> 30.3 us  [send(): return lax.ppermute(x, ('flow', 'link'), perm)]
    ppermute x24, waiting for transfers between devices: 26.7 us -> 20.5 us  [send(): return lax.ppermute(x, ('flow', 'link'), perm)]
  transfers between devices with their start and end apart: 24 -> 24, of which waited for: 16 -> 13; matrix products, arithmetic and copies ran while one was open for 0% -> 0% of each run, Pallas kernels for 10% -> 9%
where the time goes in v3:
time: 66.6 us; the launch traced here: 65.5 us
  starting transfers between devices  30.3 us (45%)
  waiting for transfers between devices  20.5 us (31%)
  Pallas kernels  13.2 us (20%)
  between operations  1.57 us (2%)
    ppermute x24, starting transfers between devices, send(): return lax.ppermute(x, ('flow', 'link'), perm)  30.3 us
    ppermute x24, waiting for transfers between devices, send(): return lax.ppermute(x, ('flow', 'link'), perm)  20.5 us
    pallas_call x3, Pallas kernels, full_call(): pl.pallas_call(body, out_shape=tuple((pltpu.HBM(x.shape, f32) for x in (a...  3.15 us
    pallas_call x3, Pallas kernels, tile_call(): pl.pallas_call(body, out_shape=payload, in_specs=[VM] * (3 + len(early) +...  3.13 us
    pallas_call x1, Pallas kernels, on_device(): pl.pallas_call(first_route_kernel, out_shape=(payload, pltpu.VMEM((S, T,...  2.9 us
    pallas_call x1, Pallas kernels, on_device(): pl.pallas_call(prepare_kernel, out_shape=(pltpu.VMEM((flow_blocks, T), f3...  1.45 us
    pallas_call x1, Pallas kernels, on_device(): pl.pallas_call(turn_kernel, out_shape=(pltpu.VMEM((S, T, T), bf16), *fetc...  1.42 us
  transfers between devices with their start and end apart: 24, of which 13 were waited for; matrix products, arithmetic and copies ran while one was open for 0% of the time, Pallas kernels for 9%

profile of v3, /device:TPU:0, one launch (start us, length us, event | category | flops | bytes accessed | tf_op | source)
XLA Modules:
  0.0 65.5 jit_solution(16542494312796690934)
XLA Ops:
  1.3 2.9 %first_route.1 = (s32[72,128]{1,0:T(8,128)S(1)}, bf16[128,128,128]{2,1,0:T(8,128)(2,1)S(1)}, s32[264,128]{1,0:T(8,128)S(1)}) custom-call(s32[1,1]{1,0:T(1,128)S(6)} %copy.11.count, s32[1,128]{1,0:T(1,128)} %rest_0_.1, s32[1,128]{1,0:T(1,128)} %rest_1_.1, f32[512,128]{1,0:T(8,128)} %bitcast.7, bf16[128,128,128]{2,1,0:T(8,128)(2,1)} %tiles.1), custom_call_target="tpu_custom_call" | custom-call | tf_op jit(solution)/shard_map/first_route/pallas_call | solution.py:394
  4.3 1.7 %collective-permute-start.1 = (s32[72,128]{1,0:T(8,128)S(1)}, s32[72,128]{1,0:T(8,128)S(1)}, u32[]{:S(2)}, u32[]{:S(2)}) collective-permute-start(s32[72,128]{1,0:T(8,128)S(1)} %get-tuple-element.28), channel_id=1, source_target_pairs={{0,20},{1,21},{2,22},{3,23},{4,24},{5,25},{6,26},{7,27},{8,28},{9,... | collective-permute-start | bytes 110600 | tf_op jit(solution)/shard_map/ppermute | solution.py:307
  6.0 2.9 %collective-permute-start.2 = (s32[72,128]{1,0:T(8,128)S(1)}, s32[72,128]{1,0:T(8,128)S(1)}, u32[]{:S(2)}, u32[]{:S(2)}) collective-permute-start(s32[72,128]{1,0:T(8,128)S(1)} %get-tuple-element.28), channel_id=1, source_target_pairs={{0,28},{1,29},{2,30},{3,31},{4,16},{5,17},{6,18},{7,19},{8,20},{9,... | collective-permute-start | bytes 110600 | tf_op jit(solution)/shard_map/ppermute | solution.py:307
  8.8 3.6 %collective-permute-start.3 = (s32[72,128]{1,0:T(8,128)S(1)}, s32[72,128]{1,0:T(8,128)S(1)}, u32[]{:S(2)}, u32[]{:S(2)}) collective-permute-start(s32[72,128]{1,0:T(8,128)S(1)} %get-tuple-element.28), channel_id=1, source_target_pairs={{0,24},{1,25},{2,26},{3,27},{4,28},{5,29},{6,30},{7,31},{8,16},{9,... | collective-permute-start | bytes 110600 | tf_op jit(solution)/shard_map/ppermute | solution.py:307
  12.5 1.6 %collective-permute-done.3.refs_3_ = s32[72,128]{1,0:T(8,128)S(1)} collective-permute-done((s32[72,128]{1,0:T(8,128)S(1)}, s32[72,128]{1,0:T(8,128)S(1)}, u32[]{:S(2)}, u32[]{:S(2)}) %collective-permute-start.3) | collective-permute-done | bytes 36896 | tf_op jit(solution)/shard_map/ppermute | solution.py:307
  15.1 1.4 %collective-permute-start.5 = (s32[264,128]{1,0:T(8,128)S(1)}, s32[264,128]{1,0:T(8,128)S(1)}, u32[]{:S(2)}, u32[]{:S(2)}) collective-permute-start(s32[264,128]{1,0:T(8,128)S(1)} %join.4), channel_id=1, source_target_pairs={{0,28},{1,29},{2,30},{3,31},{4,16},{5,17},{6,18},{7,19},{8,20},{9,... | collective-permute-start | bytes 405512 | tf_op jit(solution)/shard_map/ppermute | solution.py:307
  16.5 1.4 %collective-permute-start.6 = (s32[264,128]{1,0:T(8,128)S(1)}, s32[264,128]{1,0:T(8,128)S(1)}, u32[]{:S(2)}, u32[]{:S(2)}) collective-permute-start(s32[264,128]{1,0:T(8,128)S(1)} %join.4), channel_id=1, source_target_pairs={{0,24},{1,25},{2,26},{3,27},{4,28},{5,29},{6,30},{7,31},{8,16},{9,... | collective-permute-start | bytes 405512 | tf_op jit(solution)/shard_map/ppermute | solution.py:307
  18.0 1.3 %collective-permute-start.7 = (s32[264,128]{1,0:T(8,128)S(1)}, s32[264,128]{1,0:T(8,128)S(1)}, u32[]{:S(2)}, u32[]{:S(2)}) collective-permute-start(s32[264,128]{1,0:T(8,128)S(1)} %join.4), channel_id=1, source_target_pairs={{0,20},{1,21},{2,22},{3,23},{4,24},{5,25},{6,26},{7,27},{8,28},{9,... | collective-permute-start | bytes 405512 | tf_op jit(solution)/shard_map/ppermute | solution.py:307
  19.3 1.4 %turn.1 = (bf16[128,128,128]{2,1,0:T(8,128)(2,1)S(1)}, s32[1,128]{1,0:T(1,128)S(4)}, s32[1,128]{1,0:T(1,128)S(4)}, s32[1024,128]{1,0:T(8,128)S(1)}, f32[2,128]{1...) custom-call(bf16[128,128,128]{2,1,0:T(8,128)(2,1)S(1)} %get-tuple-element.17.tiles, ...), custom_call_target="tpu_custom_call" | custom-call | tf_op jit(solution)/shard_map/turn/pallas_call | solution.py:421
  20.7 1.4 %prepare.1 = (f32[1024,128]{1,0:T(8,128)S(1)}, f32[4,128,128]{2,1,0:T(8,128)S(1)}) custom-call(s32[1,128]{1,0:T(1,128)S(4)} %get-tuple-element.21.flow_at, s32[1,128]{1,0:T(1,128)S(4)} %get-tuple-element.22.link_at, s32[1024,128]{1,0:T(8,128)S(1)} %get-tuple-element.23.flow_class, f32[2,128]{1,0:T(2,128)S(1)} %get-tuple-element.24.table, ...), custom_call_target="tpu_custom_call" | custom-call | tf_op jit(solution)/shard_map/prepare/pallas_call | solution.py:431
  24.9 1.4 %collective-permute-start.8 = (s32[72,128]{1,0:T(8,128)S(1)}, s32[72,128]{1,0:T(8,128)S(1)}, u32[]{:S(2)}, u32[]{:S(2)}) collective-permute-start(s32[72,128]{1,0:T(8,128)S(1)} %shard_map.105.refs_0_), channel_id=1, source_target_pairs={{0,48},{1,49},{2,50},{3,51},{4,52},{5,53},{6,54},{7,55},{8,56},{9,... | collective-permute-start | bytes 110600 | tf_op jit(solution)/shard_map/ppermute | solution.py:307
  26.4 1.6 %collective-permute-start.9 = (s32[72,128]{1,0:T(8,128)S(1)}, s32[72,128]{1,0:T(8,128)S(1)}, u32[]{:S(2)}, u32[]{:S(2)}) collective-permute-start(s32[72,128]{1,0:T(8,128)S(1)} %shard_map.105.refs_0_), channel_id=1, source_target_pairs={{0,112},{1,113},{2,114},{3,115},{4,116},{5,117},{6,118},{7,119},{8... | collective-permute-start | bytes 110600 | tf_op jit(solution)/shard_map/ppermute | solution.py:307
  28.0 1.8 %collective-permute-start.10 = (s32[72,128]{1,0:T(8,128)S(1)}, s32[72,128]{1,0:T(8,128)S(1)}, u32[]{:S(2)}, u32[]{:S(2)}) collective-permute-start(s32[72,128]{1,0:T(8,128)S(1)} %shard_map.105.refs_0_), channel_id=1, source_target_pairs={{0,80},{1,81},{2,82},{3,83},{4,84},{5,85},{6,86},{7,87},{8,88},{9,... | collective-permute-start | bytes 110600 | tf_op jit(solution)/shard_map/ppermute | solution.py:307
  29.8 3.1 %collective-permute-done.10.refs_3_ = s32[72,128]{1,0:T(8,128)S(1)} collective-permute-done((s32[72,128]{1,0:T(8,128)S(1)}, s32[72,128]{1,0:T(8,128)S(1)}, u32[]{:S(2)}, u32[]{:S(2)}) %collective-permute-start.10) | collective-permute-done | bytes 36896 | tf_op jit(solution)/shard_map/ppermute | solution.py:307
  35.9 1.3 %collective-permute-start.14 = (s32[72,128]{1,0:T(8,128)S(1)}, s32[72,128]{1,0:T(8,128)S(1)}, u32[]{:S(2)}, u32[]{:S(2)}) collective-permute-start(s32[72,128]{1,0:T(8,128)S(1)} %shard_map.107), channel_id=1, source_target_pairs={{0,28},{1,29},{2,30},{3,31},{4,16},{5,17},{6,18},{7,19},{8,20},{9,... | collective-permute-start | bytes 110600 | tf_op jit(solution)/shard_map/ppermute | solution.py:307
  37.1 1.7 %collective-permute-start.15 = (s32[72,128]{1,0:T(8,128)S(1)}, s32[72,128]{1,0:T(8,128)S(1)}, u32[]{:S(2)}, u32[]{:S(2)}) collective-permute-start(s32[72,128]{1,0:T(8,128)S(1)} %shard_map.107), channel_id=1, source_target_pairs={{0,24},{1,25},{2,26},{3,27},{4,28},{5,29},{6,30},{7,31},{8,16},{9,... | collective-permute-start | bytes 110600 | tf_op jit(solution)/shard_map/ppermute | solution.py:307
  38.9 1.4 %collective-permute-done.13.refs_1_ = s32[72,128]{1,0:T(8,128)S(1)} collective-permute-done((s32[72,128]{1,0:T(8,128)S(1)}, s32[72,128]{1,0:T(8,128)S(1)}, u32[]{:S(2)}, u32[]{:S(2)}) %collective-permute-start.13) | collective-permute-done | bytes 36896 | tf_op jit(solution)/shard_map/ppermute | solution.py:307
  40.3 1.7 %collective-permute-done.15.refs_3_ = s32[72,128]{1,0:T(8,128)S(1)} collective-permute-done((s32[72,128]{1,0:T(8,128)S(1)}, s32[72,128]{1,0:T(8,128)S(1)}, u32[]{:S(2)}, u32[]{:S(2)}) %collective-permute-start.15) | collective-permute-done | bytes 36896 | tf_op jit(solution)/shard_map/ppermute | solution.py:307
  42.3 2.7 %collective-permute-start.17 = (s32[264,128]{1,0:T(8,128)S(1)}, s32[264,128]{1,0:T(8,128)S(1)}, u32[]{:S(2)}, u32[]{:S(2)}) collective-permute-start(s32[264,128]{1,0:T(8,128)S(1)} %join.6), channel_id=1, source_target_pairs={{0,28},{1,29},{2,30},{3,31},{4,16},{5,17},{6,18},{7,19},{8,20},{9,... | collective-permute-start | bytes 405512 | tf_op jit(solution)/shard_map/ppermute | solution.py:307
  45.9 1.7 %collective-permute-done.17.rest_1_.rest_2_ = s32[264,128]{1,0:T(8,128)S(1)} collective-permute-done((s32[264,128]{1,0:T(8,128)S(1)}, s32[264,128]{1,0:T(8,128)S(1)}, u32[]{:S(2)}, u32[]{:S(2)}) %collective-permute-start.17) | collective-permute-done | bytes 135200 | tf_op jit(solution)/shard_map/ppermute | solution.py:307
  47.6 3.5 %collective-permute-done.18.rest_2_.rest_3_ = s32[264,128]{1,0:T(8,128)S(1)} collective-permute-done((s32[264,128]{1,0:T(8,128)S(1)}, s32[264,128]{1,0:T(8,128)S(1)}, u32[]{:S(2)}, u32[]{:S(2)}) %collective-permute-start.18) | collective-permute-done | bytes 135200 | tf_op jit(solution)/shard_map/ppermute | solution.py:307
  54.0 2.4 %collective-permute-start.21 = (s32[72,128]{1,0:T(8,128)S(1)}, s32[72,128]{1,0:T(8,128)S(1)}, u32[]{:S(2)}, u32[]{:S(2)}) collective-permute-start(s32[72,128]{1,0:T(8,128)S(1)} %shard_map.109.refs_0_), channel_id=1, source_target_pairs={{0,112},{1,113},{2,114},{3,115},{4,116},{5,117},{6,118},{7,119},{8... | collective-permute-start | bytes 110600 | tf_op jit(solution)/shard_map/ppermute | solution.py:307
  58.4 2.8 %collective-permute-done.22.refs_3_ = s32[72,128]{1,0:T(8,128)S(1)} collective-permute-done((s32[72,128]{1,0:T(8,128)S(1)}, s32[72,128]{1,0:T(8,128)S(1)}, u32[]{:S(2)}, u32[]{:S(2)}) %collective-permute-start.22) | collective-permute-done | bytes 36896 | tf_op jit(solution)/shard_map/ppermute | solution.py:307
  62.4 1.5 %shard_map.111.rate = f32[1024,128]{1,0:T(8,128)S(1)} custom-call(f32[1024,128]{1,0:T(8,128)S(1)} %get-tuple-element.29.weight, f32[1024,128]{1,0:T(8,128)S(1)} %get-tuple-element.25.access, s32[264,128]{1,0:T(8,128)S(1)} %collective-permute-done.16.rest_0_, s32[264,128]{1,0:T(8,128)S(1)} %collective-permute-done.19.rest_0_.rest_1_, ...), custom_call_target="tpu_custom_call" | custom-call | tf_op jit(solution)/shard_map/pallas_call | solution.py:385
  (40 shorter events, 15.5 us)
Async XLA Ops:
  4.2 8.3 %collective-permute-start = (s32[72,128]{1,0:T(8,128)S(1)}, s32[72,128]{1,0:T(8,128)S(1)}, u32[]{:S(2)}, u32[]{:S(2)}) collective-permute-start(s32[72,128]{1,0:T(8,128)S(1)} %get-tuple-element.28), channel_id=1, source_target_pairs={{0,16},{1,17},{2,18},{3,19},{4,20},{5,21},{6,22},{7,23},{8,24},{9,... | collective-permute-start | bytes 110600 | tf_op jit(solution)/shard_map/ppermute | solution.py:307
  4.3 8.2 %collective-permute-start.1 = (s32[72,128]{1,0:T(8,128)S(1)}, s32[72,128]{1,0:T(8,128)S(1)}, u32[]{:S(2)}, u32[]{:S(2)}) collective-permute-start(s32[72,128]{1,0:T(8,128)S(1)} %get-tuple-element.28), channel_id=1, source_target_pairs={{0,20},{1,21},{2,22},{3,23},{4,24},{5,25},{6,26},{7,27},{8,28},{9,... | collective-permute-start | bytes 110600 | tf_op jit(solution)/shard_map/ppermute | solution.py:307
  6.0 6.5 %collective-permute-start.2 = (s32[72,128]{1,0:T(8,128)S(1)}, s32[72,128]{1,0:T(8,128)S(1)}, u32[]{:S(2)}, u32[]{:S(2)}) collective-permute-start(s32[72,128]{1,0:T(8,128)S(1)} %get-tuple-element.28), channel_id=1, source_target_pairs={{0,28},{1,29},{2,30},{3,31},{4,16},{5,17},{6,18},{7,19},{8,20},{9,... | collective-permute-start | bytes 110600 | tf_op jit(solution)/shard_map/ppermute | solution.py:307
  8.8 5.3 %collective-permute-start.3 = (s32[72,128]{1,0:T(8,128)S(1)}, s32[72,128]{1,0:T(8,128)S(1)}, u32[]{:S(2)}, u32[]{:S(2)}) collective-permute-start(s32[72,128]{1,0:T(8,128)S(1)} %get-tuple-element.28), channel_id=1, source_target_pairs={{0,24},{1,25},{2,26},{3,27},{4,28},{5,29},{6,30},{7,31},{8,16},{9,... | collective-permute-start | bytes 110600 | tf_op jit(solution)/shard_map/ppermute | solution.py:307
  14.1 8.0 %collective-permute-start.4 = (s32[264,128]{1,0:T(8,128)S(1)}, s32[264,128]{1,0:T(8,128)S(1)}, u32[]{:S(2)}, u32[]{:S(2)}) collective-permute-start(s32[264,128]{1,0:T(8,128)S(1)} %join.4), channel_id=1, source_target_pairs={{0,16},{1,17},{2,18},{3,19},{4,20},{5,21},{6,22},{7,23},{8,24},{9,... | collective-permute-start | bytes 405512 | tf_op jit(solution)/shard_map/ppermute | solution.py:307
  15.1 7.1 %collective-permute-start.5 = (s32[264,128]{1,0:T(8,128)S(1)}, s32[264,128]{1,0:T(8,128)S(1)}, u32[]{:S(2)}, u32[]{:S(2)}) collective-permute-start(s32[264,128]{1,0:T(8,128)S(1)} %join.4), channel_id=1, source_target_pairs={{0,28},{1,29},{2,30},{3,31},{4,16},{5,17},{6,18},{7,19},{8,20},{9,... | collective-permute-start | bytes 405512 | tf_op jit(solution)/shard_map/ppermute | solution.py:307
  16.5 6.0 %collective-permute-start.6 = (s32[264,128]{1,0:T(8,128)S(1)}, s32[264,128]{1,0:T(8,128)S(1)}, u32[]{:S(2)}, u32[]{:S(2)}) collective-permute-start(s32[264,128]{1,0:T(8,128)S(1)} %join.4), channel_id=1, source_target_pairs={{0,24},{1,25},{2,26},{3,27},{4,28},{5,29},{6,30},{7,31},{8,16},{9,... | collective-permute-start | bytes 405512 | tf_op jit(solution)/shard_map/ppermute | solution.py:307
  18.0 6.0 %collective-permute-start.7 = (s32[264,128]{1,0:T(8,128)S(1)}, s32[264,128]{1,0:T(8,128)S(1)}, u32[]{:S(2)}, u32[]{:S(2)}) collective-permute-start(s32[264,128]{1,0:T(8,128)S(1)} %join.4), channel_id=1, source_target_pairs={{0,20},{1,21},{2,22},{3,23},{4,24},{5,25},{6,26},{7,27},{8,28},{9,... | collective-permute-start | bytes 405512 | tf_op jit(solution)/shard_map/ppermute | solution.py:307
  24.9 4.8 %collective-permute-start.8 = (s32[72,128]{1,0:T(8,128)S(1)}, s32[72,128]{1,0:T(8,128)S(1)}, u32[]{:S(2)}, u32[]{:S(2)}) collective-permute-start(s32[72,128]{1,0:T(8,128)S(1)} %shard_map.105.refs_0_), channel_id=1, source_target_pairs={{0,48},{1,49},{2,50},{3,51},{4,52},{5,53},{6,54},{7,55},{8,56},{9,... | collective-permute-start | bytes 110600 | tf_op jit(solution)/shard_map/ppermute | solution.py:307
  26.4 3.4 %collective-permute-start.9 = (s32[72,128]{1,0:T(8,128)S(1)}, s32[72,128]{1,0:T(8,128)S(1)}, u32[]{:S(2)}, u32[]{:S(2)}) collective-permute-start(s32[72,128]{1,0:T(8,128)S(1)} %shard_map.105.refs_0_), channel_id=1, source_target_pairs={{0,112},{1,113},{2,114},{3,115},{4,116},{5,117},{6,118},{7,119},{8... | collective-permute-start | bytes 110600 | tf_op jit(solution)/shard_map/ppermute | solution.py:307
  28.0 4.9 %collective-permute-start.10 = (s32[72,128]{1,0:T(8,128)S(1)}, s32[72,128]{1,0:T(8,128)S(1)}, u32[]{:S(2)}, u32[]{:S(2)}) collective-permute-start(s32[72,128]{1,0:T(8,128)S(1)} %shard_map.105.refs_0_), channel_id=1, source_target_pairs={{0,80},{1,81},{2,82},{3,83},{4,84},{5,85},{6,86},{7,87},{8,88},{9,... | collective-permute-start | bytes 110600 | tf_op jit(solution)/shard_map/ppermute | solution.py:307
  32.9 1.4 %collective-permute-start.11 = (s32[264,128]{1,0:T(8,128)S(1)}, s32[264,128]{1,0:T(8,128)S(1)}, u32[]{:S(2)}, u32[]{:S(2)}) collective-permute-start(s32[264,128]{1,0:T(8,128)S(1)} %join.5.rest_0_), channel_id=1, source_target_pairs={{0,16},{1,17},{2,18},{3,19},{4,20},{5,21},{6,22},{7,23},{8,24},{9,... | collective-permute-start | bytes 405512 | tf_op jit(solution)/shard_map/ppermute | solution.py:307
  35.4 3.5 %collective-permute-start.12 = (s32[72,128]{1,0:T(8,128)S(1)}, s32[72,128]{1,0:T(8,128)S(1)}, u32[]{:S(2)}, u32[]{:S(2)}) collective-permute-start(s32[72,128]{1,0:T(8,128)S(1)} %shard_map.107), channel_id=1, source_target_pairs={{0,16},{1,17},{2,18},{3,19},{4,20},{5,21},{6,22},{7,23},{8,24},{9,... | collective-permute-start | bytes 110600 | tf_op jit(solution)/shard_map/ppermute | solution.py:307
  35.7 4.6 %collective-permute-start.13 = (s32[72,128]{1,0:T(8,128)S(1)}, s32[72,128]{1,0:T(8,128)S(1)}, u32[]{:S(2)}, u32[]{:S(2)}) collective-permute-start(s32[72,128]{1,0:T(8,128)S(1)} %shard_map.107), channel_id=1, source_target_pairs={{0,20},{1,21},{2,22},{3,23},{4,24},{5,25},{6,26},{7,27},{8,28},{9,... | collective-permute-start | bytes 110600 | tf_op jit(solution)/shard_map/ppermute | solution.py:307
  35.9 4.5 %collective-permute-start.14 = (s32[72,128]{1,0:T(8,128)S(1)}, s32[72,128]{1,0:T(8,128)S(1)}, u32[]{:S(2)}, u32[]{:S(2)}) collective-permute-start(s32[72,128]{1,0:T(8,128)S(1)} %shard_map.107), channel_id=1, source_target_pairs={{0,28},{1,29},{2,30},{3,31},{4,16},{5,17},{6,18},{7,19},{8,20},{9,... | collective-permute-start | bytes 110600 | tf_op jit(solution)/shard_map/ppermute | solution.py:307
  37.1 4.9 %collective-permute-start.15 = (s32[72,128]{1,0:T(8,128)S(1)}, s32[72,128]{1,0:T(8,128)S(1)}, u32[]{:S(2)}, u32[]{:S(2)}) collective-permute-start(s32[72,128]{1,0:T(8,128)S(1)} %shard_map.107), channel_id=1, source_target_pairs={{0,24},{1,25},{2,26},{3,27},{4,28},{5,29},{6,30},{7,31},{8,16},{9,... | collective-permute-start | bytes 110600 | tf_op jit(solution)/shard_map/ppermute | solution.py:307
  42.0 3.8 %collective-permute-start.16 = (s32[264,128]{1,0:T(8,128)S(1)}, s32[264,128]{1,0:T(8,128)S(1)}, u32[]{:S(2)}, u32[]{:S(2)}) collective-permute-start(s32[264,128]{1,0:T(8,128)S(1)} %join.6), channel_id=1, source_target_pairs={{0,16},{1,17},{2,18},{3,19},{4,20},{5,21},{6,22},{7,23},{8,24},{9,... | collective-permute-start | bytes 405512 | tf_op jit(solution)/shard_map/ppermute | solution.py:307
  42.3 5.3 %collective-permute-start.17 = (s32[264,128]{1,0:T(8,128)S(1)}, s32[264,128]{1,0:T(8,128)S(1)}, u32[]{:S(2)}, u32[]{:S(2)}) collective-permute-start(s32[264,128]{1,0:T(8,128)S(1)} %join.6), channel_id=1, source_target_pairs={{0,28},{1,29},{2,30},{3,31},{4,16},{5,17},{6,18},{7,19},{8,20},{9,... | collective-permute-start | bytes 405512 | tf_op jit(solution)/shard_map/ppermute | solution.py:307
  45.0 6.0 %collective-permute-start.18 = (s32[264,128]{1,0:T(8,128)S(1)}, s32[264,128]{1,0:T(8,128)S(1)}, u32[]{:S(2)}, u32[]{:S(2)}) collective-permute-start(s32[264,128]{1,0:T(8,128)S(1)} %join.6), channel_id=1, source_target_pairs={{0,24},{1,25},{2,26},{3,27},{4,28},{5,29},{6,30},{7,31},{8,16},{9,... | collective-permute-start | bytes 405512 | tf_op jit(solution)/shard_map/ppermute | solution.py:307
  45.8 6.5 %collective-permute-start.19 = (s32[264,128]{1,0:T(8,128)S(1)}, s32[264,128]{1,0:T(8,128)S(1)}, u32[]{:S(2)}, u32[]{:S(2)}) collective-permute-start(s32[264,128]{1,0:T(8,128)S(1)} %join.6), channel_id=1, source_target_pairs={{0,20},{1,21},{2,22},{3,23},{4,24},{5,25},{6,26},{7,27},{8,28},{9,... | collective-permute-start | bytes 405512 | tf_op jit(solution)/shard_map/ppermute | solution.py:307
  53.4 4.6 %collective-permute-start.20 = (s32[72,128]{1,0:T(8,128)S(1)}, s32[72,128]{1,0:T(8,128)S(1)}, u32[]{:S(2)}, u32[]{:S(2)}) collective-permute-start(s32[72,128]{1,0:T(8,128)S(1)} %shard_map.109.refs_0_), channel_id=1, source_target_pairs={{0,48},{1,49},{2,50},{3,51},{4,52},{5,53},{6,54},{7,55},{8,56},{9,... | collective-permute-start | bytes 110600 | tf_op jit(solution)/shard_map/ppermute | solution.py:307
  54.0 4.4 %collective-permute-start.21 = (s32[72,128]{1,0:T(8,128)S(1)}, s32[72,128]{1,0:T(8,128)S(1)}, u32[]{:S(2)}, u32[]{:S(2)}) collective-permute-start(s32[72,128]{1,0:T(8,128)S(1)} %shard_map.109.refs_0_), channel_id=1, source_target_pairs={{0,112},{1,113},{2,114},{3,115},{4,116},{5,117},{6,118},{7,119},{8... | collective-permute-start | bytes 110600 | tf_op jit(solution)/shard_map/ppermute | solution.py:307
  56.4 4.9 %collective-permute-start.22 = (s32[72,128]{1,0:T(8,128)S(1)}, s32[72,128]{1,0:T(8,128)S(1)}, u32[]{:S(2)}, u32[]{:S(2)}) collective-permute-start(s32[72,128]{1,0:T(8,128)S(1)} %shard_map.109.refs_0_), channel_id=1, source_target_pairs={{0,80},{1,81},{2,82},{3,83},{4,84},{5,85},{6,86},{7,87},{8,88},{9,... | collective-permute-start | bytes 110600 | tf_op jit(solution)/shard_map/ppermute | solution.py:307
  61.3 3.0 %collective-permute-start.23 = (s32[264,128]{1,0:T(8,128)S(1)}, s32[264,128]{1,0:T(8,128)S(1)}, u32[]{:S(2)}, u32[]{:S(2)}) collective-permute-start(s32[264,128]{1,0:T(8,128)S(1)} %join.7.rest_0_), channel_id=1, source_target_pairs={{0,16},{1,17},{2,18},{3,19},{4,20},{5,21},{6,22},{7,23},{8,24},{9,... | collective-permute-start | bytes 405512 | tf_op jit(solution)/shard_map/ppermute | solution.py:307

commit v4 on v3

--- a/solution.py
+++ b/solution.py
@@ -256,31 +256,38 @@
         c.wait()
 
 
-def prepare_kernel(flow_at, link_at, flow_class, table, access, price, capacity, weight, own):
+def look_up(classes, table, weight):
     low = jnp.broadcast_to(table[0:1, :], (8, T))
     high = jnp.broadcast_to(table[1:2, :], (8, T))
 
     def look(r, carry):
         rows = pl.ds(pl.multiple_of(r * 8, 8), 8)
-        which = flow_class[rows, :]
+        which = classes[rows, :]
         lane = which & (T - 1)
         from_low = jnp.take_along_axis(low, lane, axis=1)
         from_high = jnp.take_along_axis(high, lane, axis=1)
         weight[rows, :] = jnp.where(which < T, from_low, from_high)
         return carry
 
-    lax.fori_loop(0, flow_class.shape[0] // 8, look, 0, unroll=16)
-
+    lax.fori_loop(0, classes.shape[0] // 8, look, 0, unroll=16)
+
+
+def weigh_kernel(flow_class, table, weight):
+    look_up(flow_class, table, weight)
+
+
+def prepare_kernel(flow_at, link_at, flow_class, table, access, price, capacity, own, own_class):
     def pick(s, carry):
         f = flow_at[0, s]
         l = link_at[0, s]
-        own[0, pl.ds(s, 1), :] = weight[pl.ds(f, 1), :]
+        own_class[pl.ds(s, 1), :] = flow_class[pl.ds(f, 1), :]
         own[1, pl.ds(s, 1), :] = access[pl.ds(f, 1), :]
         own[2, pl.ds(s, 1), :] = price[pl.ds(l, 1), :]
         own[3, pl.ds(s, 1), :] = capacity[pl.ds(l, 1), :]
         return carry
 
     lax.fori_loop(0, S, pick, 0, unroll=16)
+    look_up(own_class, table, own.at[0])
 
 
 def shifts():
@@ -428,11 +435,20 @@
         name="turn",
     )(in_vmem(tiles), *[in_hbm(x) for x in sources])
     access, price, cap = sources[2:]
-    weight, own = pl.pallas_call(
+    weight = pl.pallas_call(
+        weigh_kernel,
+        out_shape=pltpu.VMEM((flow_blocks, T), f32),
+        in_specs=[VM, VM],
+        out_specs=VM,
+        compiler_params=PARAMS,
+        name="weigh",
+    )(in_vmem(sources[0]), in_vmem(sources[1]))
+    own = pl.pallas_call(
         prepare_kernel,
-        out_shape=(pltpu.VMEM((flow_blocks, T), f32), pltpu.VMEM((4, S, T), f32)),
+        out_shape=pltpu.VMEM((4, S, T), f32),
         in_specs=[SM, SM] + [VM] * 5,
-        out_specs=(VM, VM),
+        out_specs=VM,
+        scratch_shapes=[pltpu.VMEM((S, T), jnp.int32)],
         compiler_params=PARAMS,
         name="prepare",
     )(flow_at, link_at, *[in_vmem(x) for x in sources])

time: 66.6 us -> 64.9 us (0.974)
  the two profiles are of different devices: /device:TPU:0 before, /device:TPU:1 now
where the time goes in v4:
time: 64.9 us; the launch traced here: 64.8 us
  waiting for transfers between devices  25.1 us (39%)
  starting transfers between devices  24.9 us (38%)
  Pallas kernels  13.3 us (20%)
  between operations  1.56 us (2%)
    ppermute x24, waiting for transfers between devices, send(): return lax.ppermute(x, ('flow', 'link'), perm)  25.1 us
    ppermute x24, starting transfers between devices, send(): return lax.ppermute(x, ('flow', 'link'), perm)  24.9 us
    pallas_call x3, Pallas kernels, full_call(): pl.pallas_call(body, out_shape=tuple((pltpu.HBM(x.shape, f32) for x in (a...  3.17 us
    pallas_call x3, Pallas kernels, tile_call(): pl.pallas_call(body, out_shape=payload, in_specs=[VM] * (3 + len(early) +...  3.13 us
    pallas_call x1, Pallas kernels, on_device(): pl.pallas_call(first_route_kernel, out_shape=(payload, pltpu.VMEM((S, T,...  2.9 us
    pallas_call x1, Pallas kernels, on_device(): pl.pallas_call(turn_kernel, out_shape=(pltpu.VMEM((S, T, T), bf16), *fetc...  1.42 us
  transfers between devices with their start and end apart: 24, of which 15 were waited for; matrix products, arithmetic and copies ran while one was open for 0% of the time, Pallas kernels for 9%

profile of v4, /device:TPU:1, one launch (start us, length us, event | category | flops | bytes accessed | tf_op | source)
XLA Modules:
  0.0 64.8 jit_solution(10757527480185615943)
XLA Ops:
  1.3 2.9 %first_route.1 = (s32[72,128]{1,0:T(8,128)S(1)}, bf16[128,128,128]{2,1,0:T(8,128)(2,1)S(1)}, s32[264,128]{1,0:T(8,128)S(1)}) custom-call(s32[1,1]{1,0:T(1,128)S(6)} %copy.11.count, s32[1,128]{1,0:T(1,128)} %rest_0_.1, s32[1,128]{1,0:T(1,128)} %rest_1_.1, f32[512,128]{1,0:T(8,128)} %bitcast.7, bf16[128,128,128]{2,1,0:T(8,128)(2,1)} %tiles.1), custom_call_target="tpu_custom_call" | custom-call | tf_op jit(solution)/shard_map/first_route/pallas_call | solution.py:401
  4.2 5.0 %collective-permute-start.3 = (s32[72,128]{1,0:T(8,128)S(1)}, s32[72,128]{1,0:T(8,128)S(1)}, u32[]{:S(2)}, u32[]{:S(2)}) collective-permute-start(s32[72,128]{1,0:T(8,128)S(1)} %get-tuple-element.25), channel_id=1, source_target_pairs={{0,24},{1,25},{2,26},{3,27},{4,28},{5,29},{6,30},{7,31},{8,16},{9,... | collective-permute-start | bytes 110600 | tf_op jit(solution)/shard_map/ppermute | solution.py:314
  9.2 2.6 %collective-permute-start.2 = (s32[72,128]{1,0:T(8,128)S(1)}, s32[72,128]{1,0:T(8,128)S(1)}, u32[]{:S(2)}, u32[]{:S(2)}) collective-permute-start(s32[72,128]{1,0:T(8,128)S(1)} %get-tuple-element.25), channel_id=1, source_target_pairs={{0,28},{1,29},{2,30},{3,31},{4,16},{5,17},{6,18},{7,19},{8,20},{9,... | collective-permute-start | bytes 110600 | tf_op jit(solution)/shard_map/ppermute | solution.py:314
  12.9 3.5 %collective-permute-done.1.refs_1_ = s32[72,128]{1,0:T(8,128)S(1)} collective-permute-done((s32[72,128]{1,0:T(8,128)S(1)}, s32[72,128]{1,0:T(8,128)S(1)}, u32[]{:S(2)}, u32[]{:S(2)}) %collective-permute-start.1) | collective-permute-done | bytes 36896 | tf_op jit(solution)/shard_map/ppermute | solution.py:314
  17.2 1.4 %collective-permute-start.7 = (s32[264,128]{1,0:T(8,128)S(1)}, s32[264,128]{1,0:T(8,128)S(1)}, u32[]{:S(2)}, u32[]{:S(2)}) collective-permute-start(s32[264,128]{1,0:T(8,128)S(1)} %join.4), channel_id=1, source_target_pairs={{0,20},{1,21},{2,22},{3,23},{4,24},{5,25},{6,26},{7,27},{8,28},{9,... | collective-permute-start | bytes 405512 | tf_op jit(solution)/shard_map/ppermute | solution.py:314
  18.6 1.4 %turn.1 = (bf16[128,128,128]{2,1,0:T(8,128)(2,1)S(1)}, s32[1,128]{1,0:T(1,128)S(4)}, s32[1,128]{1,0:T(1,128)S(4)}, s32[1024,128]{1,0:T(8,128)S(1)}, f32[2,128]{1...) custom-call(bf16[128,128,128]{2,1,0:T(8,128)(2,1)S(1)} %get-tuple-element.15.tiles, ...), custom_call_target="tpu_custom_call" | custom-call | tf_op jit(solution)/shard_map/turn/pallas_call | solution.py:428
  20.5 2.1 %collective-permute-done.6.rest_2_ = s32[264,128]{1,0:T(8,128)S(1)} collective-permute-done((s32[264,128]{1,0:T(8,128)S(1)}, s32[264,128]{1,0:T(8,128)S(1)}, u32[]{:S(2)}, u32[]{:S(2)}) %collective-permute-start.6) | collective-permute-done | bytes 135200 | tf_op jit(solution)/shard_map/ppermute | solution.py:314
  24.9 3.1 %collective-permute-start.10 = (s32[72,128]{1,0:T(8,128)S(1)}, s32[72,128]{1,0:T(8,128)S(1)}, u32[]{:S(2)}, u32[]{:S(2)}) collective-permute-start(s32[72,128]{1,0:T(8,128)S(1)} %shard_map.105.refs_0_), channel_id=1, source_target_pairs={{0,80},{1,81},{2,82},{3,83},{4,84},{5,85},{6,86},{7,87},{8,88},{9,... | collective-permute-start | bytes 110600 | tf_op jit(solution)/shard_map/ppermute | solution.py:314
  29.9 1.5 %collective-permute-done.9.refs_2_ = s32[72,128]{1,0:T(8,128)S(1)} collective-permute-done((s32[72,128]{1,0:T(8,128)S(1)}, s32[72,128]{1,0:T(8,128)S(1)}, u32[]{:S(2)}, u32[]{:S(2)}) %collective-permute-start.9) | collective-permute-done | bytes 36896 | tf_op jit(solution)/shard_map/ppermute | solution.py:314
  31.4 2.1 %collective-permute-done.8.refs_1_ = s32[72,128]{1,0:T(8,128)S(1)} collective-permute-done((s32[72,128]{1,0:T(8,128)S(1)}, s32[72,128]{1,0:T(8,128)S(1)}, u32[]{:S(2)}, u32[]{:S(2)}) %collective-permute-start.8) | collective-permute-done | bytes 36896 | tf_op jit(solution)/shard_map/ppermute | solution.py:314
  33.9 1.1 %collective-permute-done.11.rest_1_ = s32[264,128]{1,0:T(8,128)S(1)} collective-permute-done((s32[264,128]{1,0:T(8,128)S(1)}, s32[264,128]{1,0:T(8,128)S(1)}, u32[]{:S(2)}, u32[]{:S(2)}) %collective-permute-start.11) | collective-permute-done | bytes 135200 | tf_op jit(solution)/shard_map/ppermute | solution.py:314
  35.0 1.1 %shard_map.107 = s32[72,128]{1,0:T(8,128)S(1)} custom-call(s32[264,128]{1,0:T(8,128)S(1)} %get-tuple-element.18.index, f32[4,128,128]{2,1,0:T(8,128)S(1)} %prepare.1.own, bf16[128,128,128]{2,1,0:T(8,128)(2,1)S(1)} %get-tuple-element.15.tiles, s32[264,128]{1,0:T(8,128)S(1)} %join.5.rest_0_, s32[264,128]{1,0:T(8,128)S(1)} %collective-permute-done.11.rest_1_), custom_call_target="tpu_custom_call" | custom-call | tf_op jit(solution)/shard_map/pallas_call | solution.py:367
  36.1 2.4 %collective-permute-start.15 = (s32[72,128]{1,0:T(8,128)S(1)}, s32[72,128]{1,0:T(8,128)S(1)}, u32[]{:S(2)}, u32[]{:S(2)}) collective-permute-start(s32[72,128]{1,0:T(8,128)S(1)} %shard_map.107), channel_id=1, source_target_pairs={{0,24},{1,25},{2,26},{3,27},{4,28},{5,29},{6,30},{7,31},{8,16},{9,... | collective-permute-start | bytes 110600 | tf_op jit(solution)/shard_map/ppermute | solution.py:314
  38.9 2.2 %collective-permute-done.15.refs_3_ = s32[72,128]{1,0:T(8,128)S(1)} collective-permute-done((s32[72,128]{1,0:T(8,128)S(1)}, s32[72,128]{1,0:T(8,128)S(1)}, u32[]{:S(2)}, u32[]{:S(2)}) %collective-permute-start.15) | collective-permute-done | bytes 36896 | tf_op jit(solution)/shard_map/ppermute | solution.py:314
  41.9 1.2 %collective-permute-done.13.refs_1_ = s32[72,128]{1,0:T(8,128)S(1)} collective-permute-done((s32[72,128]{1,0:T(8,128)S(1)}, s32[72,128]{1,0:T(8,128)S(1)}, u32[]{:S(2)}, u32[]{:S(2)}) %collective-permute-start.13) | collective-permute-done | bytes 36896 | tf_op jit(solution)/shard_map/ppermute | solution.py:314
  43.9 1.9 %collective-permute-start.17 = (s32[264,128]{1,0:T(8,128)S(1)}, s32[264,128]{1,0:T(8,128)S(1)}, u32[]{:S(2)}, u32[]{:S(2)}) collective-permute-start(s32[264,128]{1,0:T(8,128)S(1)} %join.6), channel_id=1, source_target_pairs={{0,28},{1,29},{2,30},{3,31},{4,16},{5,17},{6,18},{7,19},{8,20},{9,... | collective-permute-start | bytes 405512 | tf_op jit(solution)/shard_map/ppermute | solution.py:314
  46.6 2.5 %collective-permute-done.18.rest_2_.rest_3_ = s32[264,128]{1,0:T(8,128)S(1)} collective-permute-done((s32[264,128]{1,0:T(8,128)S(1)}, s32[264,128]{1,0:T(8,128)S(1)}, u32[]{:S(2)}, u32[]{:S(2)}) %collective-permute-start.18) | collective-permute-done | bytes 135200 | tf_op jit(solution)/shard_map/ppermute | solution.py:314
  49.5 2.0 %collective-permute-done.19.rest_0_.rest_1_ = s32[264,128]{1,0:T(8,128)S(1)} collective-permute-done((s32[264,128]{1,0:T(8,128)S(1)}, s32[264,128]{1,0:T(8,128)S(1)}, u32[]{:S(2)}, u32[]{:S(2)}) %collective-permute-start.19) | collective-permute-done | bytes 135200 | tf_op jit(solution)/shard_map/ppermute | solution.py:314
  53.1 1.7 %collective-permute-start.21 = (s32[72,128]{1,0:T(8,128)S(1)}, s32[72,128]{1,0:T(8,128)S(1)}, u32[]{:S(2)}, u32[]{:S(2)}) collective-permute-start(s32[72,128]{1,0:T(8,128)S(1)} %shard_map.109.refs_0_), channel_id=1, source_target_pairs={{0,112},{1,113},{2,114},{3,115},{4,116},{5,117},{6,118},{7,119},{8... | collective-permute-start | bytes 110600 | tf_op jit(solution)/shard_map/ppermute | solution.py:314
  54.8 2.8 %collective-permute-done.22.refs_3_ = s32[72,128]{1,0:T(8,128)S(1)} collective-permute-done((s32[72,128]{1,0:T(8,128)S(1)}, s32[72,128]{1,0:T(8,128)S(1)}, u32[]{:S(2)}, u32[]{:S(2)}) %collective-permute-start.22) | collective-permute-done | bytes 36896 | tf_op jit(solution)/shard_map/ppermute | solution.py:314
  57.6 1.9 %collective-permute-done.20.refs_1_ = s32[72,128]{1,0:T(8,128)S(1)} collective-permute-done((s32[72,128]{1,0:T(8,128)S(1)}, s32[72,128]{1,0:T(8,128)S(1)}, u32[]{:S(2)}, u32[]{:S(2)}) %collective-permute-start.20) | collective-permute-done | bytes 36896 | tf_op jit(solution)/shard_map/ppermute | solution.py:314
  59.9 1.1 %weigh.1.weight = f32[1024,128]{1,0:T(8,128)S(1)} custom-call(s32[1024,128]{1,0:T(8,128)S(1)} %get-tuple-element.21.flow_class, f32[2,128]{1,0:T(2,128)S(1)} %get-tuple-element.22.table), custom_call_target="tpu_custom_call" | custom-call | tf_op jit(solution)/shard_map/weigh/pallas_call | solution.py:438
  61.7 1.5 %shard_map.111.rate = f32[1024,128]{1,0:T(8,128)S(1)} custom-call(f32[1024,128]{1,0:T(8,128)S(1)} %weigh.1.weight, f32[1024,128]{1,0:T(8,128)S(1)} %get-tuple-element.23.access, s32[264,128]{1,0:T(8,128)S(1)} %collective-permute-done.16.rest_0_, s32[264,128]{1,0:T(8,128)S(1)} %collective-permute-done.19.rest_0_.rest_1_, ...), custom_call_target="tpu_custom_call" | custom-call | tf_op jit(solution)/shard_map/pallas_call | solution.py:392
  63.6 1.1 %shard_map.112 = (f32[512,128]{1,0:T(8,128)}, f32[1024,128]{1,0:T(8,128)}) custom-call(f32[512,128]{1,0:T(8,128)S(1)} %shard_map.106.price, f32[512,128]{1,0:T(8,128)S(1)} %get-tuple-element.17.capacity, f32[512,128]{1,0:T(8,128)S(1)} %shard_map.110.early, f32[1024,128]{1,0:T(8,128)S(1)} %shard_map.111.rate, s32[264,128]{1,0:T(8,128)S(1)} %collective-permute-done.23.rest_0_), custom_call_target="tpu_custom_call" | custom-call | tf_op jit(solution)/shard_map/pallas_call | solution.py:392
  (41 shorter events, 12.9 us)
Async XLA Ops:
  4.2 8.5 %collective-permute-start.3 = (s32[72,128]{1,0:T(8,128)S(1)}, s32[72,128]{1,0:T(8,128)S(1)}, u32[]{:S(2)}, u32[]{:S(2)}) collective-permute-start(s32[72,128]{1,0:T(8,128)S(1)} %get-tuple-element.25), channel_id=1, source_target_pairs={{0,24},{1,25},{2,26},{3,27},{4,28},{5,29},{6,30},{7,31},{8,16},{9,... | collective-permute-start | bytes 110600 | tf_op jit(solution)/shard_map/ppermute | solution.py:314
  9.2 3.7 %collective-permute-start.2 = (s32[72,128]{1,0:T(8,128)S(1)}, s32[72,128]{1,0:T(8,128)S(1)}, u32[]{:S(2)}, u32[]{:S(2)}) collective-permute-start(s32[72,128]{1,0:T(8,128)S(1)} %get-tuple-element.25), channel_id=1, source_target_pairs={{0,28},{1,29},{2,30},{3,31},{4,16},{5,17},{6,18},{7,19},{8,20},{9,... | collective-permute-start | bytes 110600 | tf_op jit(solution)/shard_map/ppermute | solution.py:314
  11.8 4.6 %collective-permute-start.1 = (s32[72,128]{1,0:T(8,128)S(1)}, s32[72,128]{1,0:T(8,128)S(1)}, u32[]{:S(2)}, u32[]{:S(2)}) collective-permute-start(s32[72,128]{1,0:T(8,128)S(1)} %get-tuple-element.25), channel_id=1, source_target_pairs={{0,20},{1,21},{2,22},{3,23},{4,24},{5,25},{6,26},{7,27},{8,28},{9,... | collective-permute-start | bytes 110600 | tf_op jit(solution)/shard_map/ppermute | solution.py:314
  12.7 3.7 %collective-permute-start = (s32[72,128]{1,0:T(8,128)S(1)}, s32[72,128]{1,0:T(8,128)S(1)}, u32[]{:S(2)}, u32[]{:S(2)}) collective-permute-start(s32[72,128]{1,0:T(8,128)S(1)} %get-tuple-element.25), channel_id=1, source_target_pairs={{0,16},{1,17},{2,18},{3,19},{4,20},{5,21},{6,22},{7,23},{8,24},{9,... | collective-permute-start | bytes 110600 | tf_op jit(solution)/shard_map/ppermute | solution.py:314
  16.5 6.1 %collective-permute-start.6 = (s32[264,128]{1,0:T(8,128)S(1)}, s32[264,128]{1,0:T(8,128)S(1)}, u32[]{:S(2)}, u32[]{:S(2)}) collective-permute-start(s32[264,128]{1,0:T(8,128)S(1)} %join.4), channel_id=1, source_target_pairs={{0,24},{1,25},{2,26},{3,27},{4,28},{5,29},{6,30},{7,31},{8,16},{9,... | collective-permute-start | bytes 405512 | tf_op jit(solution)/shard_map/ppermute | solution.py:314
  16.5 6.0 %collective-permute-start.5 = (s32[264,128]{1,0:T(8,128)S(1)}, s32[264,128]{1,0:T(8,128)S(1)}, u32[]{:S(2)}, u32[]{:S(2)}) collective-permute-start(s32[264,128]{1,0:T(8,128)S(1)} %join.4), channel_id=1, source_target_pairs={{0,28},{1,29},{2,30},{3,31},{4,16},{5,17},{6,18},{7,19},{8,20},{9,... | collective-permute-start | bytes 405512 | tf_op jit(solution)/shard_map/ppermute | solution.py:314
  17.1 5.4 %collective-permute-start.4 = (s32[264,128]{1,0:T(8,128)S(1)}, s32[264,128]{1,0:T(8,128)S(1)}, u32[]{:S(2)}, u32[]{:S(2)}) collective-permute-start(s32[264,128]{1,0:T(8,128)S(1)} %join.4), channel_id=1, source_target_pairs={{0,16},{1,17},{2,18},{3,19},{4,20},{5,21},{6,22},{7,23},{8,24},{9,... | collective-permute-start | bytes 405512 | tf_op jit(solution)/shard_map/ppermute | solution.py:314
  17.2 6.8 %collective-permute-start.7 = (s32[264,128]{1,0:T(8,128)S(1)}, s32[264,128]{1,0:T(8,128)S(1)}, u32[]{:S(2)}, u32[]{:S(2)}) collective-permute-start(s32[264,128]{1,0:T(8,128)S(1)} %join.4), channel_id=1, source_target_pairs={{0,20},{1,21},{2,22},{3,23},{4,24},{5,25},{6,26},{7,27},{8,28},{9,... | collective-permute-start | bytes 405512 | tf_op jit(solution)/shard_map/ppermute | solution.py:314
  24.9 4.9 %collective-permute-start.10 = (s32[72,128]{1,0:T(8,128)S(1)}, s32[72,128]{1,0:T(8,128)S(1)}, u32[]{:S(2)}, u32[]{:S(2)}) collective-permute-start(s32[72,128]{1,0:T(8,128)S(1)} %shard_map.105.refs_0_), channel_id=1, source_target_pairs={{0,80},{1,81},{2,82},{3,83},{4,84},{5,85},{6,86},{7,87},{8,88},{9,... | collective-permute-start | bytes 110600 | tf_op jit(solution)/shard_map/ppermute | solution.py:314
  28.0 3.4 %collective-permute-start.9 = (s32[72,128]{1,0:T(8,128)S(1)}, s32[72,128]{1,0:T(8,128)S(1)}, u32[]{:S(2)}, u32[]{:S(2)}) collective-permute-start(s32[72,128]{1,0:T(8,128)S(1)} %shard_map.105.refs_0_), channel_id=1, source_target_pairs={{0,112},{1,113},{2,114},{3,115},{4,116},{5,117},{6,118},{7,119},{8... | collective-permute-start | bytes 110600 | tf_op jit(solution)/shard_map/ppermute | solution.py:314
  29.0 4.6 %collective-permute-start.8 = (s32[72,128]{1,0:T(8,128)S(1)}, s32[72,128]{1,0:T(8,128)S(1)}, u32[]{:S(2)}, u32[]{:S(2)}) collective-permute-start(s32[72,128]{1,0:T(8,128)S(1)} %shard_map.105.refs_0_), channel_id=1, source_target_pairs={{0,48},{1,49},{2,50},{3,51},{4,52},{5,53},{6,54},{7,55},{8,56},{9,... | collective-permute-start | bytes 110600 | tf_op jit(solution)/shard_map/ppermute | solution.py:314
  33.6 1.4 %collective-permute-start.11 = (s32[264,128]{1,0:T(8,128)S(1)}, s32[264,128]{1,0:T(8,128)S(1)}, u32[]{:S(2)}, u32[]{:S(2)}) collective-permute-start(s32[264,128]{1,0:T(8,128)S(1)} %join.5.rest_0_), channel_id=1, source_target_pairs={{0,16},{1,17},{2,18},{3,19},{4,20},{5,21},{6,22},{7,23},{8,24},{9,... | collective-permute-start | bytes 405512 | tf_op jit(solution)/shard_map/ppermute | solution.py:314
  36.1 4.9 %collective-permute-start.15 = (s32[72,128]{1,0:T(8,128)S(1)}, s32[72,128]{1,0:T(8,128)S(1)}, u32[]{:S(2)}, u32[]{:S(2)}) collective-permute-start(s32[72,128]{1,0:T(8,128)S(1)} %shard_map.107), channel_id=1, source_target_pairs={{0,24},{1,25},{2,26},{3,27},{4,28},{5,29},{6,30},{7,31},{8,16},{9,... | collective-permute-start | bytes 110600 | tf_op jit(solution)/shard_map/ppermute | solution.py:314
  38.5 3.4 %collective-permute-start.14 = (s32[72,128]{1,0:T(8,128)S(1)}, s32[72,128]{1,0:T(8,128)S(1)}, u32[]{:S(2)}, u32[]{:S(2)}) collective-permute-start(s32[72,128]{1,0:T(8,128)S(1)} %shard_map.107), channel_id=1, source_target_pairs={{0,28},{1,29},{2,30},{3,31},{4,16},{5,17},{6,18},{7,19},{8,20},{9,... | collective-permute-start | bytes 110600 | tf_op jit(solution)/shard_map/ppermute | solution.py:314
  38.5 4.6 %collective-permute-start.13 = (s32[72,128]{1,0:T(8,128)S(1)}, s32[72,128]{1,0:T(8,128)S(1)}, u32[]{:S(2)}, u32[]{:S(2)}) collective-permute-start(s32[72,128]{1,0:T(8,128)S(1)} %shard_map.107), channel_id=1, source_target_pairs={{0,20},{1,21},{2,22},{3,23},{4,24},{5,25},{6,26},{7,27},{8,28},{9,... | collective-permute-start | bytes 110600 | tf_op jit(solution)/shard_map/ppermute | solution.py:314
  38.5 4.6 %collective-permute-start.12 = (s32[72,128]{1,0:T(8,128)S(1)}, s32[72,128]{1,0:T(8,128)S(1)}, u32[]{:S(2)}, u32[]{:S(2)}) collective-permute-start(s32[72,128]{1,0:T(8,128)S(1)} %shard_map.107), channel_id=1, source_target_pairs={{0,16},{1,17},{2,18},{3,19},{4,20},{5,21},{6,22},{7,23},{8,24},{9,... | collective-permute-start | bytes 110600 | tf_op jit(solution)/shard_map/ppermute | solution.py:314
  43.1 6.0 %collective-permute-start.18 = (s32[264,128]{1,0:T(8,128)S(1)}, s32[264,128]{1,0:T(8,128)S(1)}, u32[]{:S(2)}, u32[]{:S(2)}) collective-permute-start(s32[264,128]{1,0:T(8,128)S(1)} %join.6), channel_id=1, source_target_pairs={{0,24},{1,25},{2,26},{3,27},{4,28},{5,29},{6,30},{7,31},{8,16},{9,... | collective-permute-start | bytes 405512 | tf_op jit(solution)/shard_map/ppermute | solution.py:314
  43.9 5.3 %collective-permute-start.17 = (s32[264,128]{1,0:T(8,128)S(1)}, s32[264,128]{1,0:T(8,128)S(1)}, u32[]{:S(2)}, u32[]{:S(2)}) collective-permute-start(s32[264,128]{1,0:T(8,128)S(1)} %join.6), channel_id=1, source_target_pairs={{0,28},{1,29},{2,30},{3,31},{4,16},{5,17},{6,18},{7,19},{8,20},{9,... | collective-permute-start | bytes 405512 | tf_op jit(solution)/shard_map/ppermute | solution.py:314
  45.8 3.4 %collective-permute-start.16 = (s32[264,128]{1,0:T(8,128)S(1)}, s32[264,128]{1,0:T(8,128)S(1)}, u32[]{:S(2)}, u32[]{:S(2)}) collective-permute-start(s32[264,128]{1,0:T(8,128)S(1)} %join.6), channel_id=1, source_target_pairs={{0,16},{1,17},{2,18},{3,19},{4,20},{5,21},{6,22},{7,23},{8,24},{9,... | collective-permute-start | bytes 405512 | tf_op jit(solution)/shard_map/ppermute | solution.py:314
  45.8 5.8 %collective-permute-start.19 = (s32[264,128]{1,0:T(8,128)S(1)}, s32[264,128]{1,0:T(8,128)S(1)}, u32[]{:S(2)}, u32[]{:S(2)}) collective-permute-start(s32[264,128]{1,0:T(8,128)S(1)} %join.6), channel_id=1, source_target_pairs={{0,20},{1,21},{2,22},{3,23},{4,24},{5,25},{6,26},{7,27},{8,28},{9,... | collective-permute-start | bytes 405512 | tf_op jit(solution)/shard_map/ppermute | solution.py:314
  52.5 5.0 %collective-permute-start.22 = (s32[72,128]{1,0:T(8,128)S(1)}, s32[72,128]{1,0:T(8,128)S(1)}, u32[]{:S(2)}, u32[]{:S(2)}) collective-permute-start(s32[72,128]{1,0:T(8,128)S(1)} %shard_map.109.refs_0_), channel_id=1, source_target_pairs={{0,80},{1,81},{2,82},{3,83},{4,84},{5,85},{6,86},{7,87},{8,88},{9,... | collective-permute-start | bytes 110600 | tf_op jit(solution)/shard_map/ppermute | solution.py:314
  53.1 4.5 %collective-permute-start.21 = (s32[72,128]{1,0:T(8,128)S(1)}, s32[72,128]{1,0:T(8,128)S(1)}, u32[]{:S(2)}, u32[]{:S(2)}) collective-permute-start(s32[72,128]{1,0:T(8,128)S(1)} %shard_map.109.refs_0_), channel_id=1, source_target_pairs={{0,112},{1,113},{2,114},{3,115},{4,116},{5,117},{6,118},{7,119},{8... | collective-permute-start | bytes 110600 | tf_op jit(solution)/shard_map/ppermute | solution.py:314
  54.8 4.7 %collective-permute-start.20 = (s32[72,128]{1,0:T(8,128)S(1)}, s32[72,128]{1,0:T(8,128)S(1)}, u32[]{:S(2)}, u32[]{:S(2)}) collective-permute-start(s32[72,128]{1,0:T(8,128)S(1)} %shard_map.109.refs_0_), channel_id=1, source_target_pairs={{0,48},{1,49},{2,50},{3,51},{4,52},{5,53},{6,54},{7,55},{8,56},{9,... | collective-permute-start | bytes 110600 | tf_op jit(solution)/shard_map/ppermute | solution.py:314
  59.5 4.1 %collective-permute-start.23 = (s32[264,128]{1,0:T(8,128)S(1)}, s32[264,128]{1,0:T(8,128)S(1)}, u32[]{:S(2)}, u32[]{:S(2)}) collective-permute-start(s32[264,128]{1,0:T(8,128)S(1)} %join.7.rest_0_), channel_id=1, source_target_pairs={{0,16},{1,17},{2,18},{3,19},{4,20},{5,21},{6,22},{7,23},{8,24},{9,... | collective-permute-start | bytes 405512 | tf_op jit(solution)/shard_map/ppermute | solution.py:314

commit v5 on v4

--- a/solution.py
+++ b/solution.py
@@ -178,6 +178,11 @@
     out[...] = matched_sum(index[:S, :], blocks, decode(blocks))
 
 
+def early_load_kernel(index, *rest):
+    blocks, out = rest[:-1], rest[-1]
+    out[...] = matched_sum(index[S : 2 * S, :], blocks, decode(blocks))
+
+
 def early_price_kernel(*rest):
     blocks, (out, code, hits) = rest[:-3], rest[-3:]
 
@@ -195,9 +200,9 @@
     put_payload(out, terms[...], index[2 * S + 1 : 2 * S + 2, :])
 
 
-def route_kernel(index, own, tiles, *rest):
+def route_kernel(index, own, tiles, early, *rest):
     blocks, (out, picked, terms) = rest[:-3], rest[-3:]
-    load = matched_sum(index[S : 2 * S, :], blocks, decode(blocks))
+    load = early[...] + matched_sum(index[S : 2 * S, :], blocks, decode(blocks))
     picked[...] = (own[2] * jnp.exp(step_size * (load / own[3] - 1.0))).astype(bf16)
     tile_terms(tiles, lambda g: None, picked, terms)
     put_payload(out, terms[...], index[2 * S : 2 * S + 1, :])
@@ -350,9 +355,9 @@
     access = access_price.reshape(flow_blocks, T)
     payload = pltpu.VMEM((PAYLOAD, T), jnp.int32)
 
-    def early_call(blocks):
+    def early_call(blocks, body=early_kernel):
         return pl.pallas_call(
-            early_kernel,
+            body,
             out_shape=pltpu.VMEM((S, T), f32),
             in_specs=[VM] * (1 + len(blocks)),
             out_specs=VM,
@@ -362,6 +367,10 @@
     def load_call(routes):
         early = early_call([routes[0]] + routes[2:])
         return tile_call(load_kernel, own, turned, [early], [routes[1]])
+
+    def route_call(loads):
+        early = early_call(loads[:1], early_load_kernel)
+        return tile_call(route_kernel, own, tiles, [early], loads[1:])
 
     def tile_call(body, own, tiles, early, blocks):
         return pl.pallas_call(
@@ -456,7 +465,7 @@
     routes = gather_link(route_one)
     loads = gather_flow(load_call(routes))
     price_one = full_call(first_price_kernel, price, cap, [], loads, False)
-    routes = gather_link(tile_call(route_kernel, own, tiles, [], loads))
+    routes = gather_link(route_call(loads))
     rate = full_call(rate_kernel, weight, access, [], routes, False)
     loads = gather_flow(load_call(routes))
     early = early_price_call(loads[:1])

time: 64.9 us -> 64.8 us (level)
  transfers between devices with their start and end apart: 24 -> 24, of which waited for: 15 -> 15; matrix products, arithmetic and copies ran while one was open for 0% -> 0% of each run, Pallas kernels for 9% -> 10%
where the time goes in v5:
time: 64.8 us; the launch traced here: 64.7 us
  starting transfers between devices  24.9 us (38%)
  waiting for transfers between devices  24.9 us (38%)
  Pallas kernels  13.4 us (21%)
  between operations  1.57 us (2%)
    ppermute x24, starting transfers between devices, send(): return lax.ppermute(x, ('flow', 'link'), perm)  24.9 us
    ppermute x24, waiting for transfers between devices, send(): return lax.ppermute(x, ('flow', 'link'), perm)  24.9 us
    pallas_call x3, Pallas kernels, full_call(): pl.pallas_call(body, out_shape=tuple((pltpu.HBM(x.shape, f32) for x in (a...  3.17 us
    pallas_call x3, Pallas kernels, tile_call(): pl.pallas_call(body, out_shape=payload, in_specs=[VM] * (3 + len(early) +...  3.03 us
    pallas_call x1, Pallas kernels, on_device(): pl.pallas_call(first_route_kernel, out_shape=(payload, pltpu.VMEM((S, T,...  2.9 us
    pallas_call x1, Pallas kernels, on_device(): pl.pallas_call(turn_kernel, out_shape=(pltpu.VMEM((S, T, T), bf16), *fetc...  1.42 us
  transfers between devices with their start and end apart: 24, of which 15 were waited for; matrix products, arithmetic and copies ran while one was open for 0% of the time, Pallas kernels for 10%

profile of v5, /device:TPU:1, one launch (start us, length us, event | category | flops | bytes accessed | tf_op | source)
XLA Modules:
  0.0 64.7 jit_solution(16339495627408307213)
XLA Ops:
  1.3 2.9 %first_route.1 = (s32[72,128]{1,0:T(8,128)S(1)}, bf16[128,128,128]{2,1,0:T(8,128)(2,1)S(1)}, s32[264,128]{1,0:T(8,128)S(1)}) custom-call(s32[1,1]{1,0:T(1,128)S(6)} %copy.11.count, s32[1,128]{1,0:T(1,128)} %rest_0_.1, s32[1,128]{1,0:T(1,128)} %rest_1_.1, f32[512,128]{1,0:T(8,128)} %bitcast.7, bf16[128,128,128]{2,1,0:T(8,128)(2,1)} %tiles.1), custom_call_target="tpu_custom_call" | custom-call | tf_op jit(solution)/shard_map/first_route/pallas_call | solution.py:410
  4.2 5.0 %collective-permute-start.3 = (s32[72,128]{1,0:T(8,128)S(1)}, s32[72,128]{1,0:T(8,128)S(1)}, u32[]{:S(2)}, u32[]{:S(2)}) collective-permute-start(s32[72,128]{1,0:T(8,128)S(1)} %get-tuple-element.25), channel_id=1, source_target_pairs={{0,24},{1,25},{2,26},{3,27},{4,28},{5,29},{6,30},{7,31},{8,16},{9,... | collective-permute-start | bytes 110600 | tf_op jit(solution)/shard_map/ppermute | solution.py:319
  9.2 2.6 %collective-permute-start.2 = (s32[72,128]{1,0:T(8,128)S(1)}, s32[72,128]{1,0:T(8,128)S(1)}, u32[]{:S(2)}, u32[]{:S(2)}) collective-permute-start(s32[72,128]{1,0:T(8,128)S(1)} %get-tuple-element.25), channel_id=1, source_target_pairs={{0,28},{1,29},{2,30},{3,31},{4,16},{5,17},{6,18},{7,19},{8,20},{9,... | collective-permute-start | bytes 110600 | tf_op jit(solution)/shard_map/ppermute | solution.py:319
  12.9 3.5 %collective-permute-done.1.refs_1_ = s32[72,128]{1,0:T(8,128)S(1)} collective-permute-done((s32[72,128]{1,0:T(8,128)S(1)}, s32[72,128]{1,0:T(8,128)S(1)}, u32[]{:S(2)}, u32[]{:S(2)}) %collective-permute-start.1) | collective-permute-done | bytes 36896 | tf_op jit(solution)/shard_map/ppermute | solution.py:319
  17.2 1.4 %collective-permute-start.7 = (s32[264,128]{1,0:T(8,128)S(1)}, s32[264,128]{1,0:T(8,128)S(1)}, u32[]{:S(2)}, u32[]{:S(2)}) collective-permute-start(s32[264,128]{1,0:T(8,128)S(1)} %join.4), channel_id=1, source_target_pairs={{0,20},{1,21},{2,22},{3,23},{4,24},{5,25},{6,26},{7,27},{8,28},{9,... | collective-permute-start | bytes 405512 | tf_op jit(solution)/shard_map/ppermute | solution.py:319
  18.6 1.4 %turn.1 = (bf16[128,128,128]{2,1,0:T(8,128)(2,1)S(1)}, s32[1,128]{1,0:T(1,128)S(4)}, s32[1,128]{1,0:T(1,128)S(4)}, s32[1024,128]{1,0:T(8,128)S(1)}, f32[2,128]{1...) custom-call(bf16[128,128,128]{2,1,0:T(8,128)(2,1)S(1)} %get-tuple-element.15.tiles, ...), custom_call_target="tpu_custom_call" | custom-call | tf_op jit(solution)/shard_map/turn/pallas_call | solution.py:437
  20.5 2.1 %collective-permute-done.6.rest_2_ = s32[264,128]{1,0:T(8,128)S(1)} collective-permute-done((s32[264,128]{1,0:T(8,128)S(1)}, s32[264,128]{1,0:T(8,128)S(1)}, u32[]{:S(2)}, u32[]{:S(2)}) %collective-permute-start.6) | collective-permute-done | bytes 135200 | tf_op jit(solution)/shard_map/ppermute | solution.py:319
  23.9 1.0 %shard_map.105.refs_0_ = s32[72,128]{1,0:T(8,128)S(1)} custom-call(s32[264,128]{1,0:T(8,128)S(1)} %get-tuple-element.18.index, f32[4,128,128]{2,1,0:T(8,128)S(1)} %prepare.1.own, bf16[128,128,128]{2,1,0:T(8,128)(2,1)S(1)} %get-tuple-element.24.tiles, f32[128,128]{1,0:T(8,128)S(1)} %shard_map.104.early, s32[264,128]{1,0:T(8,128)S(1)} %collective-permute-done.7.rest_0_), custom_call_target="tpu_custom_call" | custom-call | tf_op jit(solution)/shard_map/pallas_call | solution.py:376
  24.9 3.1 %collective-permute-start.10 = (s32[72,128]{1,0:T(8,128)S(1)}, s32[72,128]{1,0:T(8,128)S(1)}, u32[]{:S(2)}, u32[]{:S(2)}) collective-permute-start(s32[72,128]{1,0:T(8,128)S(1)} %shard_map.105.refs_0_), channel_id=1, source_target_pairs={{0,80},{1,81},{2,82},{3,83},{4,84},{5,85},{6,86},{7,87},{8,88},{9,... | collective-permute-start | bytes 110600 | tf_op jit(solution)/shard_map/ppermute | solution.py:319
  29.9 1.5 %collective-permute-done.9.refs_2_ = s32[72,128]{1,0:T(8,128)S(1)} collective-permute-done((s32[72,128]{1,0:T(8,128)S(1)}, s32[72,128]{1,0:T(8,128)S(1)}, u32[]{:S(2)}, u32[]{:S(2)}) %collective-permute-start.9) | collective-permute-done | bytes 36896 | tf_op jit(solution)/shard_map/ppermute | solution.py:319
  31.4 2.1 %collective-permute-done.8.refs_1_ = s32[72,128]{1,0:T(8,128)S(1)} collective-permute-done((s32[72,128]{1,0:T(8,128)S(1)}, s32[72,128]{1,0:T(8,128)S(1)}, u32[]{:S(2)}, u32[]{:S(2)}) %collective-permute-start.8) | collective-permute-done | bytes 36896 | tf_op jit(solution)/shard_map/ppermute | solution.py:319
  35.0 1.0 %shard_map.108 = s32[72,128]{1,0:T(8,128)S(1)} custom-call(s32[264,128]{1,0:T(8,128)S(1)} %get-tuple-element.18.index, f32[4,128,128]{2,1,0:T(8,128)S(1)} %prepare.1.own, bf16[128,128,128]{2,1,0:T(8,128)(2,1)S(1)} %get-tuple-element.15.tiles, f32[128,128]{1,0:T(8,128)S(1)} %shard_map.107.early, s32[264,128]{1,0:T(8,128)S(1)} %collective-permute-done.11.rest_1_.rest_0_), custom_call_target="tpu_custom_call" | custom-call | tf_op jit(solution)/shard_map/pallas_call | solution.py:376
  36.0 2.4 %collective-permute-start.15 = (s32[72,128]{1,0:T(8,128)S(1)}, s32[72,128]{1,0:T(8,128)S(1)}, u32[]{:S(2)}, u32[]{:S(2)}) collective-permute-start(s32[72,128]{1,0:T(8,128)S(1)} %shard_map.108), channel_id=1, source_target_pairs={{0,24},{1,25},{2,26},{3,27},{4,28},{5,29},{6,30},{7,31},{8,16},{9,... | collective-permute-start | bytes 110600 | tf_op jit(solution)/shard_map/ppermute | solution.py:319
  38.8 2.2 %collective-permute-done.15.refs_3_ = s32[72,128]{1,0:T(8,128)S(1)} collective-permute-done((s32[72,128]{1,0:T(8,128)S(1)}, s32[72,128]{1,0:T(8,128)S(1)}, u32[]{:S(2)}, u32[]{:S(2)}) %collective-permute-start.15) | collective-permute-done | bytes 36896 | tf_op jit(solution)/shard_map/ppermute | solution.py:319
  41.8 1.2 %collective-permute-done.13.refs_1_ = s32[72,128]{1,0:T(8,128)S(1)} collective-permute-done((s32[72,128]{1,0:T(8,128)S(1)}, s32[72,128]{1,0:T(8,128)S(1)}, u32[]{:S(2)}, u32[]{:S(2)}) %collective-permute-start.13) | collective-permute-done | bytes 36896 | tf_op jit(solution)/shard_map/ppermute | solution.py:319
  43.8 1.9 %collective-permute-start.17 = (s32[264,128]{1,0:T(8,128)S(1)}, s32[264,128]{1,0:T(8,128)S(1)}, u32[]{:S(2)}, u32[]{:S(2)}) collective-permute-start(s32[264,128]{1,0:T(8,128)S(1)} %join.6), channel_id=1, source_target_pairs={{0,28},{1,29},{2,30},{3,31},{4,16},{5,17},{6,18},{7,19},{8,20},{9,... | collective-permute-start | bytes 405512 | tf_op jit(solution)/shard_map/ppermute | solution.py:319
  46.5 2.5 %collective-permute-done.18.rest_2_.rest_3_ = s32[264,128]{1,0:T(8,128)S(1)} collective-permute-done((s32[264,128]{1,0:T(8,128)S(1)}, s32[264,128]{1,0:T(8,128)S(1)}, u32[]{:S(2)}, u32[]{:S(2)}) %collective-permute-start.18) | collective-permute-done | bytes 135200 | tf_op jit(solution)/shard_map/ppermute | solution.py:319
  49.4 2.0 %collective-permute-done.19.rest_0_.rest_1_ = s32[264,128]{1,0:T(8,128)S(1)} collective-permute-done((s32[264,128]{1,0:T(8,128)S(1)}, s32[264,128]{1,0:T(8,128)S(1)}, u32[]{:S(2)}, u32[]{:S(2)}) %collective-permute-start.19) | collective-permute-done | bytes 135200 | tf_op jit(solution)/shard_map/ppermute | solution.py:319
  53.0 1.7 %collective-permute-start.21 = (s32[72,128]{1,0:T(8,128)S(1)}, s32[72,128]{1,0:T(8,128)S(1)}, u32[]{:S(2)}, u32[]{:S(2)}) collective-permute-start(s32[72,128]{1,0:T(8,128)S(1)} %shard_map.110.refs_0_), channel_id=1, source_target_pairs={{0,112},{1,113},{2,114},{3,115},{4,116},{5,117},{6,118},{7,119},{8... | collective-permute-start | bytes 110600 | tf_op jit(solution)/shard_map/ppermute | solution.py:319
  54.7 2.8 %collective-permute-done.22.refs_3_ = s32[72,128]{1,0:T(8,128)S(1)} collective-permute-done((s32[72,128]{1,0:T(8,128)S(1)}, s32[72,128]{1,0:T(8,128)S(1)}, u32[]{:S(2)}, u32[]{:S(2)}) %collective-permute-start.22) | collective-permute-done | bytes 36896 | tf_op jit(solution)/shard_map/ppermute | solution.py:319
  57.5 1.9 %collective-permute-done.20.refs_1_ = s32[72,128]{1,0:T(8,128)S(1)} collective-permute-done((s32[72,128]{1,0:T(8,128)S(1)}, s32[72,128]{1,0:T(8,128)S(1)}, u32[]{:S(2)}, u32[]{:S(2)}) %collective-permute-start.20) | collective-permute-done | bytes 36896 | tf_op jit(solution)/shard_map/ppermute | solution.py:319
  59.8 1.1 %weigh.1.weight = f32[1024,128]{1,0:T(8,128)S(1)} custom-call(s32[1024,128]{1,0:T(8,128)S(1)} %get-tuple-element.21.flow_class, f32[2,128]{1,0:T(2,128)S(1)} %get-tuple-element.22.table), custom_call_target="tpu_custom_call" | custom-call | tf_op jit(solution)/shard_map/weigh/pallas_call | solution.py:447
  61.6 1.5 %shard_map.112.rate = f32[1024,128]{1,0:T(8,128)S(1)} custom-call(f32[1024,128]{1,0:T(8,128)S(1)} %weigh.1.weight, f32[1024,128]{1,0:T(8,128)S(1)} %get-tuple-element.23.access, s32[264,128]{1,0:T(8,128)S(1)} %collective-permute-done.16.rest_0_, s32[264,128]{1,0:T(8,128)S(1)} %collective-permute-done.19.rest_0_.rest_1_, ...), custom_call_target="tpu_custom_call" | custom-call | tf_op jit(solution)/shard_map/pallas_call | solution.py:401
  63.5 1.1 %shard_map.113 = (f32[512,128]{1,0:T(8,128)}, f32[1024,128]{1,0:T(8,128)}) custom-call(f32[512,128]{1,0:T(8,128)S(1)} %shard_map.106.price, f32[512,128]{1,0:T(8,128)S(1)} %get-tuple-element.17.capacity, f32[512,128]{1,0:T(8,128)S(1)} %shard_map.111.early, f32[1024,128]{1,0:T(8,128)S(1)} %shard_map.112.rate, s32[264,128]{1,0:T(8,128)S(1)} %collective-permute-done.23.rest_0_), custom_call_target="tpu_custom_call" | custom-call | tf_op jit(solution)/shard_map/pallas_call | solution.py:401
  (42 shorter events, 13.0 us)
Async XLA Ops:
  4.2 8.5 %collective-permute-start.3 = (s32[72,128]{1,0:T(8,128)S(1)}, s32[72,128]{1,0:T(8,128)S(1)}, u32[]{:S(2)}, u32[]{:S(2)}) collective-permute-start(s32[72,128]{1,0:T(8,128)S(1)} %get-tuple-element.25), channel_id=1, source_target_pairs={{0,24},{1,25},{2,26},{3,27},{4,28},{5,29},{6,30},{7,31},{8,16},{9,... | collective-permute-start | bytes 110600 | tf_op jit(solution)/shard_map/ppermute | solution.py:319
  9.2 3.7 %collective-permute-start.2 = (s32[72,128]{1,0:T(8,128)S(1)}, s32[72,128]{1,0:T(8,128)S(1)}, u32[]{:S(2)}, u32[]{:S(2)}) collective-permute-start(s32[72,128]{1,0:T(8,128)S(1)} %get-tuple-element.25), channel_id=1, source_target_pairs={{0,28},{1,29},{2,30},{3,31},{4,16},{5,17},{6,18},{7,19},{8,20},{9,... | collective-permute-start | bytes 110600 | tf_op jit(solution)/shard_map/ppermute | solution.py:319
  11.8 4.6 %collective-permute-start.1 = (s32[72,128]{1,0:T(8,128)S(1)}, s32[72,128]{1,0:T(8,128)S(1)}, u32[]{:S(2)}, u32[]{:S(2)}) collective-permute-start(s32[72,128]{1,0:T(8,128)S(1)} %get-tuple-element.25), channel_id=1, source_target_pairs={{0,20},{1,21},{2,22},{3,23},{4,24},{5,25},{6,26},{7,27},{8,28},{9,... | collective-permute-start | bytes 110600 | tf_op jit(solution)/shard_map/ppermute | solution.py:319
  12.7 3.7 %collective-permute-start = (s32[72,128]{1,0:T(8,128)S(1)}, s32[72,128]{1,0:T(8,128)S(1)}, u32[]{:S(2)}, u32[]{:S(2)}) collective-permute-start(s32[72,128]{1,0:T(8,128)S(1)} %get-tuple-element.25), channel_id=1, source_target_pairs={{0,16},{1,17},{2,18},{3,19},{4,20},{5,21},{6,22},{7,23},{8,24},{9,... | collective-permute-start | bytes 110600 | tf_op jit(solution)/shard_map/ppermute | solution.py:319
  16.5 6.1 %collective-permute-start.6 = (s32[264,128]{1,0:T(8,128)S(1)}, s32[264,128]{1,0:T(8,128)S(1)}, u32[]{:S(2)}, u32[]{:S(2)}) collective-permute-start(s32[264,128]{1,0:T(8,128)S(1)} %join.4), channel_id=1, source_target_pairs={{0,24},{1,25},{2,26},{3,27},{4,28},{5,29},{6,30},{7,31},{8,16},{9,... | collective-permute-start | bytes 405512 | tf_op jit(solution)/shard_map/ppermute | solution.py:319
  16.5 6.0 %collective-permute-start.5 = (s32[264,128]{1,0:T(8,128)S(1)}, s32[264,128]{1,0:T(8,128)S(1)}, u32[]{:S(2)}, u32[]{:S(2)}) collective-permute-start(s32[264,128]{1,0:T(8,128)S(1)} %join.4), channel_id=1, source_target_pairs={{0,28},{1,29},{2,30},{3,31},{4,16},{5,17},{6,18},{7,19},{8,20},{9,... | collective-permute-start | bytes 405512 | tf_op jit(solution)/shard_map/ppermute | solution.py:319
  17.1 5.4 %collective-permute-start.4 = (s32[264,128]{1,0:T(8,128)S(1)}, s32[264,128]{1,0:T(8,128)S(1)}, u32[]{:S(2)}, u32[]{:S(2)}) collective-permute-start(s32[264,128]{1,0:T(8,128)S(1)} %join.4), channel_id=1, source_target_pairs={{0,16},{1,17},{2,18},{3,19},{4,20},{5,21},{6,22},{7,23},{8,24},{9,... | collective-permute-start | bytes 405512 | tf_op jit(solution)/shard_map/ppermute | solution.py:319
  17.2 6.8 %collective-permute-start.7 = (s32[264,128]{1,0:T(8,128)S(1)}, s32[264,128]{1,0:T(8,128)S(1)}, u32[]{:S(2)}, u32[]{:S(2)}) collective-permute-start(s32[264,128]{1,0:T(8,128)S(1)} %join.4), channel_id=1, source_target_pairs={{0,20},{1,21},{2,22},{3,23},{4,24},{5,25},{6,26},{7,27},{8,28},{9,... | collective-permute-start | bytes 405512 | tf_op jit(solution)/shard_map/ppermute | solution.py:319
  24.9 4.9 %collective-permute-start.10 = (s32[72,128]{1,0:T(8,128)S(1)}, s32[72,128]{1,0:T(8,128)S(1)}, u32[]{:S(2)}, u32[]{:S(2)}) collective-permute-start(s32[72,128]{1,0:T(8,128)S(1)} %shard_map.105.refs_0_), channel_id=1, source_target_pairs={{0,80},{1,81},{2,82},{3,83},{4,84},{5,85},{6,86},{7,87},{8,88},{9,... | collective-permute-start | bytes 110600 | tf_op jit(solution)/shard_map/ppermute | solution.py:319
  28.0 3.4 %collective-permute-start.9 = (s32[72,128]{1,0:T(8,128)S(1)}, s32[72,128]{1,0:T(8,128)S(1)}, u32[]{:S(2)}, u32[]{:S(2)}) collective-permute-start(s32[72,128]{1,0:T(8,128)S(1)} %shard_map.105.refs_0_), channel_id=1, source_target_pairs={{0,112},{1,113},{2,114},{3,115},{4,116},{5,117},{6,118},{7,119},{8... | collective-permute-start | bytes 110600 | tf_op jit(solution)/shard_map/ppermute | solution.py:319
  29.0 4.6 %collective-permute-start.8 = (s32[72,128]{1,0:T(8,128)S(1)}, s32[72,128]{1,0:T(8,128)S(1)}, u32[]{:S(2)}, u32[]{:S(2)}) collective-permute-start(s32[72,128]{1,0:T(8,128)S(1)} %shard_map.105.refs_0_), channel_id=1, source_target_pairs={{0,48},{1,49},{2,50},{3,51},{4,52},{5,53},{6,54},{7,55},{8,56},{9,... | collective-permute-start | bytes 110600 | tf_op jit(solution)/shard_map/ppermute | solution.py:319
  33.6 1.4 %collective-permute-start.11 = (s32[264,128]{1,0:T(8,128)S(1)}, s32[264,128]{1,0:T(8,128)S(1)}, u32[]{:S(2)}, u32[]{:S(2)}) collective-permute-start(s32[264,128]{1,0:T(8,128)S(1)} %join.5.rest_0_), channel_id=1, source_target_pairs={{0,16},{1,17},{2,18},{3,19},{4,20},{5,21},{6,22},{7,23},{8,24},{9,... | collective-permute-start | bytes 405512 | tf_op jit(solution)/shard_map/ppermute | solution.py:319
  36.0 4.9 %collective-permute-start.15 = (s32[72,128]{1,0:T(8,128)S(1)}, s32[72,128]{1,0:T(8,128)S(1)}, u32[]{:S(2)}, u32[]{:S(2)}) collective-permute-start(s32[72,128]{1,0:T(8,128)S(1)} %shard_map.108), channel_id=1, source_target_pairs={{0,24},{1,25},{2,26},{3,27},{4,28},{5,29},{6,30},{7,31},{8,16},{9,... | collective-permute-start | bytes 110600 | tf_op jit(solution)/shard_map/ppermute | solution.py:319
  38.4 3.4 %collective-permute-start.14 = (s32[72,128]{1,0:T(8,128)S(1)}, s32[72,128]{1,0:T(8,128)S(1)}, u32[]{:S(2)}, u32[]{:S(2)}) collective-permute-start(s32[72,128]{1,0:T(8,128)S(1)} %shard_map.108), channel_id=1, source_target_pairs={{0,28},{1,29},{2,30},{3,31},{4,16},{5,17},{6,18},{7,19},{8,20},{9,... | collective-permute-start | bytes 110600 | tf_op jit(solution)/shard_map/ppermute | solution.py:319
  38.4 4.6 %collective-permute-start.13 = (s32[72,128]{1,0:T(8,128)S(1)}, s32[72,128]{1,0:T(8,128)S(1)}, u32[]{:S(2)}, u32[]{:S(2)}) collective-permute-start(s32[72,128]{1,0:T(8,128)S(1)} %shard_map.108), channel_id=1, source_target_pairs={{0,20},{1,21},{2,22},{3,23},{4,24},{5,25},{6,26},{7,27},{8,28},{9,... | collective-permute-start | bytes 110600 | tf_op jit(solution)/shard_map/ppermute | solution.py:319
  38.4 4.6 %collective-permute-start.12 = (s32[72,128]{1,0:T(8,128)S(1)}, s32[72,128]{1,0:T(8,128)S(1)}, u32[]{:S(2)}, u32[]{:S(2)}) collective-permute-start(s32[72,128]{1,0:T(8,128)S(1)} %shard_map.108), channel_id=1, source_target_pairs={{0,16},{1,17},{2,18},{3,19},{4,20},{5,21},{6,22},{7,23},{8,24},{9,... | collective-permute-start | bytes 110600 | tf_op jit(solution)/shard_map/ppermute | solution.py:319
  43.0 6.0 %collective-permute-start.18 = (s32[264,128]{1,0:T(8,128)S(1)}, s32[264,128]{1,0:T(8,128)S(1)}, u32[]{:S(2)}, u32[]{:S(2)}) collective-permute-start(s32[264,128]{1,0:T(8,128)S(1)} %join.6), channel_id=1, source_target_pairs={{0,24},{1,25},{2,26},{3,27},{4,28},{5,29},{6,30},{7,31},{8,16},{9,... | collective-permute-start | bytes 405512 | tf_op jit(solution)/shard_map/ppermute | solution.py:319
  43.8 5.3 %collective-permute-start.17 = (s32[264,128]{1,0:T(8,128)S(1)}, s32[264,128]{1,0:T(8,128)S(1)}, u32[]{:S(2)}, u32[]{:S(2)}) collective-permute-start(s32[264,128]{1,0:T(8,128)S(1)} %join.6), channel_id=1, source_target_pairs={{0,28},{1,29},{2,30},{3,31},{4,16},{5,17},{6,18},{7,19},{8,20},{9,... | collective-permute-start | bytes 405512 | tf_op jit(solution)/shard_map/ppermute | solution.py:319
  45.7 3.4 %collective-permute-start.16 = (s32[264,128]{1,0:T(8,128)S(1)}, s32[264,128]{1,0:T(8,128)S(1)}, u32[]{:S(2)}, u32[]{:S(2)}) collective-permute-start(s32[264,128]{1,0:T(8,128)S(1)} %join.6), channel_id=1, source_target_pairs={{0,16},{1,17},{2,18},{3,19},{4,20},{5,21},{6,22},{7,23},{8,24},{9,... | collective-permute-start | bytes 405512 | tf_op jit(solution)/shard_map/ppermute | solution.py:319
  45.7 5.8 %collective-permute-start.19 = (s32[264,128]{1,0:T(8,128)S(1)}, s32[264,128]{1,0:T(8,128)S(1)}, u32[]{:S(2)}, u32[]{:S(2)}) collective-permute-start(s32[264,128]{1,0:T(8,128)S(1)} %join.6), channel_id=1, source_target_pairs={{0,20},{1,21},{2,22},{3,23},{4,24},{5,25},{6,26},{7,27},{8,28},{9,... | collective-permute-start | bytes 405512 | tf_op jit(solution)/shard_map/ppermute | solution.py:319
  52.4 5.0 %collective-permute-start.22 = (s32[72,128]{1,0:T(8,128)S(1)}, s32[72,128]{1,0:T(8,128)S(1)}, u32[]{:S(2)}, u32[]{:S(2)}) collective-permute-start(s32[72,128]{1,0:T(8,128)S(1)} %shard_map.110.refs_0_), channel_id=1, source_target_pairs={{0,80},{1,81},{2,82},{3,83},{4,84},{5,85},{6,86},{7,87},{8,88},{9,... | collective-permute-start | bytes 110600 | tf_op jit(solution)/shard_map/ppermute | solution.py:319
  53.0 4.5 %collective-permute-start.21 = (s32[72,128]{1,0:T(8,128)S(1)}, s32[72,128]{1,0:T(8,128)S(1)}, u32[]{:S(2)}, u32[]{:S(2)}) collective-permute-start(s32[72,128]{1,0:T(8,128)S(1)} %shard_map.110.refs_0_), channel_id=1, source_target_pairs={{0,112},{1,113},{2,114},{3,115},{4,116},{5,117},{6,118},{7,119},{8... | collective-permute-start | bytes 110600 | tf_op jit(solution)/shard_map/ppermute | solution.py:319
  54.7 4.7 %collective-permute-start.20 = (s32[72,128]{1,0:T(8,128)S(1)}, s32[72,128]{1,0:T(8,128)S(1)}, u32[]{:S(2)}, u32[]{:S(2)}) collective-permute-start(s32[72,128]{1,0:T(8,128)S(1)} %shard_map.110.refs_0_), channel_id=1, source_target_pairs={{0,48},{1,49},{2,50},{3,51},{4,52},{5,53},{6,54},{7,55},{8,56},{9,... | collective-permute-start | bytes 110600 | tf_op jit(solution)/shard_map/ppermute | solution.py:319
  59.4 4.1 %collective-permute-start.23 = (s32[264,128]{1,0:T(8,128)S(1)}, s32[264,128]{1,0:T(8,128)S(1)}, u32[]{:S(2)}, u32[]{:S(2)}) collective-permute-start(s32[264,128]{1,0:T(8,128)S(1)} %join.7.rest_0_), channel_id=1, source_target_pairs={{0,16},{1,17},{2,18},{3,19},{4,20},{5,21},{6,22},{7,23},{8,24},{9,... | collective-permute-start | bytes 405512 | tf_op jit(solution)/shard_map/ppermute | solution.py:319
